TPU v7x, 32 devices: a whole 2x2x4 slice. The times are simulated.
32 devices in a mesh: energy: 8 (over y, x, core), space: 4 (over z).
Axes of the slice: x: 2, y: 2, z: 4, core: 2. Of those that a mesh axis runs over, the one named last changes fastest.
Arguments:
- green: bfloat16 [4, 8, 4, 384, 384], P(None, 'energy', 'space'), may hold values from -6 to 6
- v_diag: bfloat16 [4, 384, 384], P('space'), may hold values from -0.3125 to 0.3125
- v_low: bfloat16 [4, 384, 384], P('space'), may hold values from -0.3125 to 0.3125
- energy_slot: int32 [8], replicated, may hold values from 0 to 7, each once
Outputs:
- sigma: bfloat16 [2, 8, 4, 384, 384], P(None, None, 'space', 'energy')
Inputs may be any that keep to these rules, and one draw needn't show every extreme that they name: `energy_slot`: each grid energy appears in exactly one slot.
All inputs are finite; a program needn't handle non-finite values.
Results may differ from a plain program's by a relative error of at most 0.0066.
Values may be sent and summed in bfloat16 or wider, within the bound.
No kernel may reach another device: no remote copies, remote signals or barrier semaphores. Data moves between devices by JAX's collectives and lax.ppermute only.
A program may use at most 64 MiB of HBM per device.

v0:
```python
import functools
import math

import jax
import jax.numpy as jnp
from jax import lax
from jax.experimental import pallas as pl
from jax.experimental.pallas import tpu as pltpu
from jax.sharding import PartitionSpec as P


F32 = jnp.float32
BF16 = jnp.bfloat16
LANES = 128
SUBLANES = 16
PAIRED = 16
VMEM_LIMIT = 16 * 2**20


def vmem():
    return pl.BlockSpec(memory_space=pltpu.VMEM)


def smem():
    return pl.BlockSpec(memory_space=pltpu.SMEM)


def row_tile(rows):
    return 8 if rows % 8 == 0 else rows


def for_tiles(rows, cols, body):
    height = row_tile(rows)
    down = rows // height
    across = cols // LANES

    def step(index, carry):
        row = pl.multiple_of((index // across) * height, height)
        col = pl.multiple_of((index % across) * LANES, LANES)
        body((pl.ds(row, height), pl.ds(col, LANES)))
        return carry

    lax.fori_loop(0, down * across, step, 0)


def polar_kernel(order, scaling, *refs):
    count = (len(refs) - 4) // 2
    slot_ref = refs[0]
    pieces = refs[1 : 1 + count]
    outs = refs[1 + count : 1 + 2 * count]
    lesser, greater, polar = refs[1 + 2 * count :]
    energies, rows, cols = lesser.shape[1:]
    for j in range(count):
        grid = slot_ref[order(j)]
        for part in range(2):
            lesser[part, grid] = pieces[j][part].astype(F32)
            greater[part, grid] = pieces[j][part + 2].astype(F32)

    def body(tile):
        low_re = [lesser[(0, g) + tile] for g in range(energies)]
        low_im = [lesser[(1, g) + tile] for g in range(energies)]
        high_re = [greater[(0, g) + tile] for g in range(energies)]
        high_im = [greater[(1, g) + tile] for g in range(energies)]
        for w in range(energies):
            real = imag = None
            for g in range(energies - w):
                a, b, c, d = low_re[g + w], low_im[g + w], high_re[g], high_im[g]
                one = b * c - a * d
                two = a * c + b * d
                real = one if real is None else real + one
                imag = two if imag is None else imag + two
            polar[(w, 0) + tile] = real * scaling
            polar[(w, 1) + tile] = imag * -scaling

    for_tiles(rows, cols, body)
    for j in range(count):
        outs[j][...] = polar[order(j)].astype(BF16)


def sigma_kernel(order, scaling, *refs):
    count = len(refs) - 5
    slot_ref = refs[0]
    pieces = refs[1 : 1 + count]
    lesser, out, weight, total = refs[1 + count :]
    energies, rows, cols = lesser.shape[1:]
    for j in range(count):
        weight[order(j)] = pieces[j][...].astype(F32)

    def body(tile):
        low_re = [lesser[(0, g) + tile] for g in range(energies)]
        low_im = [lesser[(1, g) + tile] for g in range(energies)]
        w_re = [weight[(w, 0) + tile] for w in range(energies)]
        w_im = [weight[(w, 1) + tile] for w in range(energies)]
        for e in range(energies):
            real = imag = None
            for w in range(e + 1):
                a, b, c, d = low_re[e - w], low_im[e - w], w_re[w], w_im[w]
                one = a * d + b * c
                two = a * c - b * d
                real = one if real is None else real + one
                imag = two if imag is None else imag + two
            total[(0, e) + tile] = real * -scaling
            total[(1, e) + tile] = imag * scaling

    for_tiles(rows, cols, body)
    for s in range(energies):
        for part in range(2):
            out[part, s, 0] = total[part, slot_ref[s]].astype(BF16)


def dot(a, b, dims):
    return lax.dot_general(a, b, (dims, ((), ())), preferred_element_type=F32)


NN = ((1,), (0,))
NT = ((1,), (1,))
TN = ((0,), (0,))


def gather_kernel(order, *refs):
    pieces, out = refs[:-1], refs[-1]
    rows = pieces[0].shape[1]
    for j, piece in enumerate(pieces):
        at = pl.multiple_of((order(j) % len(pieces)) * rows, rows)
        for part in range(2):
            out[part, pl.ds(at, rows)] = piece[part]


def join(order, halves, whole):
    height = halves[0].shape[1]
    parts = whole.shape[1] // height
    mine = order(0) // (lax.axis_size("energy") // parts)
    for j, half in enumerate(halves):
        at = pl.multiple_of((mine ^ j) * height, height)
        whole[:, pl.ds(at, height)] = half[...]


def own_kernel(order, vd, *refs):
    halves, out, polar = refs[:-2], refs[-2], refs[-1]
    join(order, halves, polar)
    for part in range(2):
        left = dot(vd[...], polar[part], NN).astype(BF16)
        out[part] = dot(left, vd[...], NT)


def screen_kernel(order, count, vl, own, *refs):
    vu = refs[0:2]
    polar = refs[2 : 2 + count], refs[2 + count : 2 + 2 * count]
    outs, whole, total = refs[2 + 2 * count : -2], refs[-2], refs[-1]
    for pair in range(2):
        join(order, polar[pair], whole.at[pair])
    even = lax.axis_index("space") % 2 == 0

    def screen(upper, below, above):
        for part in range(2):
            left = dot(vl[...], below[part], NN).astype(BF16)
            lower = dot(left, vl[...], NT)
            left = dot(upper[...], above[part], TN).astype(BF16)
            raised = dot(left, upper[...], NN).astype(BF16).astype(F32)
            total[part] = (own[part] + lower + raised).astype(BF16)

    @pl.when(even)
    def _():
        screen(vu[0], whole.at[1], whole.at[0])

    @pl.when(jnp.logical_not(even))
    def _():
        screen(vu[1], whole.at[0], whole.at[1])

    rows = outs[0].shape[1]
    for j, out in enumerate(outs):
        at = pl.multiple_of(order(j) * rows, rows)
        for part in range(2):
            out[part] = total[part, pl.ds(at, rows)]


def call(kernel, outs, args, tables=0, scratch=(), flops=0):
    traffic = sum(x.size * x.dtype.itemsize for x in (*args, *outs))
    return pl.pallas_call(
        kernel,
        out_shape=outs,
        in_specs=[smem()] * tables + [vmem()] * (len(args) - tables),
        out_specs=[vmem()] * len(outs),
        scratch_shapes=scratch,
        compiler_params=pltpu.CompilerParams(vmem_limit_bytes=VMEM_LIMIT),
        cost_estimate=pl.CostEstimate(flops=flops, bytes_accessed=traffic, transcendentals=0),
    )(*args)


def struct(shape, kind=BF16):
    return jax.ShapeDtypeStruct(shape, kind)


def direct(energies, green, v_diag, v_low, energy_slot):
    parts = lax.axis_size("energy")
    layers = lax.axis_size("space")
    block, cols = green.shape[3:]
    rows = block // parts
    scaling = energies ** (-0.5)
    me = lax.axis_index("energy")

    def order(j):
        return lax.axis_index("energy") ^ j

    def swap(pieces, sequence):
        out = list(pieces)
        for j in sequence:
            out[j] = lax.ppermute(pieces[j], "energy", [(i, i ^ j) for i in range(parts)])
        return out

    def meet(value):
        out = []
        for first in range(2):
            lows = range(first, layers - 1, 2)
            out.append(lax.ppermute(value, "space", [p for i in lows for p in ((i, i + 1), (i + 1, i))]))
        return out

    cut = [lax.dynamic_slice_in_dim(green[:, 0, 0], (me ^ j) * rows, rows, 1) for j in range(parts)]
    arrived = swap(cut, range(1, parts))
    upper = meet(v_low[0])
    arrived[0], *upper = lax.optimization_barrier((arrived[0], *upper))
    piece = struct((2, rows, cols))
    *polar_out, lesser = call(
        functools.partial(polar_kernel, order, scaling),
        [piece] * parts + [struct((2, energies, rows, cols), F32)],
        [energy_slot] + arrived,
        tables=1,
        scratch=[pltpu.VMEM((2, energies, rows, cols), F32), pltpu.VMEM((energies, 2, rows, cols), F32)],
    )
    polar_in = swap(polar_out, range(1, parts))
    half = parts // 2
    part = struct((2, block // 2, cols))
    whole = struct((2, block, cols))
    own_halves, halves = [], ([], [])
    for h in range(2):
        pieces = polar_in[h * half : (h + 1) * half]
        own_halves.append(call(functools.partial(gather_kernel, order), [part], pieces)[0])
        for pair, value in enumerate(meet(own_halves[h])):
            halves[pair].append(value)
    work = 4 * block * block * cols
    own = call(
        functools.partial(own_kernel, order),
        [struct(whole.shape, F32)],
        [v_diag[0], *own_halves],
        scratch=[pltpu.VMEM(whole.shape, BF16)],
        flops=2 * work,
    )[0]
    screened_out = call(
        functools.partial(screen_kernel, order, 2),
        [piece] * parts,
        [v_low[0], own, *upper, *halves[0], *halves[1]],
        scratch=[pltpu.VMEM((2, *whole.shape), BF16), pltpu.VMEM(whole.shape, BF16)],
        flops=4 * work,
    )
    screened_in = swap(screened_out, range(1, parts))
    return call(
        functools.partial(sigma_kernel, order, scaling),
        [struct((2, energies, 1, rows, cols))],
        [energy_slot] + screened_in + [lesser],
        tables=1,
        scratch=[pltpu.VMEM((energies, 2, rows, cols), F32), pltpu.VMEM((2, energies, rows, cols), F32)],
    )[0]


def shifted(value, axis, steps):
    count = lax.axis_size(axis)
    leading, last = (max(0, -steps), min(count, count - steps))
    return lax.ppermute(value, axis, [(source, source + steps) for source in range(leading, last)])


def apply_table(table, values):
    return jnp.dot(
        table, values, precision=lax.Precision.HIGHEST, preferred_element_type=jnp.float32
    )


def spectra(cos_table, sin_table, real_part, imag_part):
    out_real = apply_table(cos_table, real_part) + apply_table(sin_table, imag_part)
    out_imag = apply_table(cos_table, imag_part) - apply_table(sin_table, real_part)
    return (out_real, out_imag)


def to_slots(cos_table, sin_table, real_part, imag_part):
    factor = 1.0 / cos_table.shape[0]
    cos_back = cos_table.T
    sin_back = sin_table.T
    out_real = (apply_table(cos_back, real_part) - apply_table(sin_back, imag_part)) * factor
    out_imag = (apply_table(cos_back, imag_part) + apply_table(sin_back, real_part)) * factor
    return (out_real, out_imag)


def sandwich(matrix, polar):
    left = jnp.einsum("ij,cejk->ceik", matrix, polar, preferred_element_type=jnp.float32).astype(
        jnp.bfloat16
    )
    return jnp.einsum("ceij,kj->ceik", left, matrix, preferred_element_type=jnp.float32)


def sandwich_t(matrix, polar):
    left = jnp.einsum("ji,cejk->ceik", matrix, polar, preferred_element_type=jnp.float32).astype(
        jnp.bfloat16
    )
    return jnp.einsum("ceij,jk->ceik", left, matrix, preferred_element_type=jnp.float32)


def general(green, v_diag, v_low, energy_slot):
    energies = energy_slot.shape[0]
    period = 2 * energies
    frequency = jnp.arange(period, dtype=jnp.int32)
    phases = frequency[:, None] * energy_slot[None, :] % period
    angles = phases.astype(jnp.float32) * (2.0 * math.pi / period)
    cos_table = jnp.cos(angles)
    sin_table = jnp.sin(angles)
    scaling = energies ** (-0.5)
    arrived = lax.all_to_all(green[:, :, 0], "energy", split_axis=2, concat_axis=1, tiled=True)
    row_count = arrived.shape[2]
    col_count = arrived.shape[3]
    flattened = arrived.reshape((4, energies, row_count * col_count)).astype(jnp.float32)
    lesser_re, lesser_im = spectra(cos_table, sin_table, flattened[0], flattened[1])
    greater_re, greater_im = spectra(cos_table, sin_table, flattened[2], flattened[3])
    cross_re = lesser_re * greater_re + lesser_im * greater_im
    cross_im = lesser_im * greater_re - lesser_re * greater_im
    corr_re, corr_im = to_slots(cos_table, sin_table, cross_re, cross_im)
    polar_slot = (
        jnp.stack([corr_im * scaling, -corr_re * scaling])
        .reshape((2, energies, row_count, col_count))
        .astype(jnp.bfloat16)
    )
    polar = lax.all_to_all(polar_slot, "energy", split_axis=1, concat_axis=2, tiled=True)
    diagonal = v_diag[0]
    lower = v_low[0]
    own_term = sandwich(diagonal, polar)
    below = shifted(polar, "space", 1)
    handed = sandwich_t(lower, polar).astype(jnp.bfloat16)
    received = shifted(handed, "space", -1)
    total = own_term + sandwich(lower, below) + received.astype(jnp.float32)
    screened = total.astype(jnp.bfloat16)
    screened_rows = lax.all_to_all(screened, "energy", split_axis=2, concat_axis=1, tiled=True)
    weights = screened_rows.reshape((2, energies, row_count * col_count)).astype(jnp.float32)
    weight_re, weight_im = spectra(cos_table, sin_table, weights[0], weights[1])
    joint_re = lesser_re * weight_re - lesser_im * weight_im
    joint_im = lesser_re * weight_im + lesser_im * weight_re
    conv_re, conv_im = to_slots(cos_table, sin_table, joint_re, joint_im)
    sigma = (
        jnp.stack([-conv_im * scaling, conv_re * scaling])
        .reshape((2, energies, row_count, col_count))
        .astype(jnp.bfloat16)
    )
    return sigma[:, :, None]


def solution(mesh):
    in_specs = (
        P(None, "energy", "space", None, None),
        P("space", None, None),
        P("space", None, None),
        P(),
    )
    out_specs = P(None, None, "space", "energy", None)
    parts = mesh.shape["energy"]
    paired = parts & (parts - 1) == 0 and 1 < parts <= PAIRED and mesh.shape["space"] > 2

    def whole(green, v_diag, v_low, energy_slot):
        rows = green.shape[3] // parts
        fast = paired and parts == energy_slot.shape[0] and rows % SUBLANES == 0
        body = functools.partial(direct, parts) if fast else general
        return jax.shard_map(body, mesh=mesh, in_specs=in_specs, out_specs=out_specs, check_vma=False)(
            green, v_diag, v_low, energy_slot
        )

    return whole
```

profile of v0, /device:TPU:0, one launch (start us, length us, event | category | flops | bytes accessed | tf_op | source)
XLA Modules:
  0.0 71.4 jit_solution(4761551772341244918)
XLA Ops:
  0.0 0.7 collective-permute-start.1
  0.7 5.9 %collective-permute-start = (bf16[384,384]{1,0:T(8,128)(2,1)}, bf16[384,384]{1,0:T(8,128)(2,1)S(1)}, u32[]{:S(2)}, u32[]{:S(2)}) collective-permute-start(bf16[384,384]{1,0:T(8,128)(2,1)} %bitcast.20), channel_id=1, source_target_pairs={{0,1},{1,0},{2,3},{3,2},{4,5},{5,4},{6,7},{7,6},{8,9},{9,8},{10,11... | collective-permute-start | bytes 884744 | tf_op jit(solution)/shard_map/ppermute | solution.py:215
  6.6 0.0 copy-start.1
  6.6 1.5 %dynamic-slice_bitcast_fusion = (bf16[4,48,384]{2,1,0:T(8,128)(2,1)S(1)}, bf16[4,48,384]{2,1,0:T(8,128)(2,1)S(1)}, bf16[4,48,384]{2,1,0:T(8,128)(2,1)S(1)}, bf16...) fusion(bf16[4,1,1,384,384]{4,3,2,1,0:T(8,128)(2,1)} %param.4, ...), kind=kLoop, calls=%fused_computation | loop fusion | bytes 2359328 | tf_op jit(solution)/shard_map/dynamic_slice | solution.py:218
  8.1 1.4 %collective-permute-start.8 = (bf16[4,48,384]{2,1,0:T(8,128)(2,1)S(1)}, bf16[4,48,384]{2,1,0:T(8,128)(2,1)S(1)}, u32[]{:S(2)}, u32[]{:S(2)}) collective-permute-start(bf16[4,48,384]{2,1,0:T(8,128)(2,1)S(1)} %get-tuple-element.45), channel_id=1, source_target_pairs={{0,28},{4,24},{8,20},{12,16},{16,12},{20,8},{24,4},{28,0},{1,29},{... | collective-permute-start | bytes 442376 | tf_op jit(solution)/shard_map/ppermute | solution.py:208
  9.5 1.3 %collective-permute-start.6 = (bf16[4,48,384]{2,1,0:T(8,128)(2,1)S(1)}, bf16[4,48,384]{2,1,0:T(8,128)(2,1)S(1)}, u32[]{:S(2)}, u32[]{:S(2)}) collective-permute-start(bf16[4,48,384]{2,1,0:T(8,128)(2,1)S(1)} %get-tuple-element.46), channel_id=1, source_target_pairs={{0,20},{4,16},{8,28},{12,24},{16,4},{20,0},{24,12},{28,8},{1,21},{... | collective-permute-start | bytes 442376 | tf_op jit(solution)/shard_map/ppermute | solution.py:208
  10.8 1.5 %collective-permute-start.5 = (bf16[4,48,384]{2,1,0:T(8,128)(2,1)S(1)}, bf16[4,48,384]{2,1,0:T(8,128)(2,1)S(1)}, u32[]{:S(2)}, u32[]{:S(2)}) collective-permute-start(bf16[4,48,384]{2,1,0:T(8,128)(2,1)S(1)} %get-tuple-element.47), channel_id=1, source_target_pairs={{0,16},{4,20},{8,24},{12,28},{16,0},{20,4},{24,8},{28,12},{1,17},{... | collective-permute-start | bytes 442376 | tf_op jit(solution)/shard_map/ppermute | solution.py:208
  12.3 2.8 %collective-permute-done.8.refs_8_ = bf16[4,48,384]{2,1,0:T(8,128)(2,1)S(1)} collective-permute-done((bf16[4,48,384]{2,1,0:T(8,128)(2,1)S(1)}, bf16[4,48,384]{2,1,0:T(8,128)(2,1)S(1)}, u32[]{:S(2)}, u32[]{:S(2)}) %collective-permute-start.8) | collective-permute-done | bytes 147488 | tf_op jit(solution)/shard_map/ppermute | solution.py:208
  15.2 0.2 collective-permute-start.4
  15.3 2.9 %collective-permute-done.6.refs_6_ = bf16[4,48,384]{2,1,0:T(8,128)(2,1)S(1)} collective-permute-done((bf16[4,48,384]{2,1,0:T(8,128)(2,1)S(1)}, bf16[4,48,384]{2,1,0:T(8,128)(2,1)S(1)}, u32[]{:S(2)}, u32[]{:S(2)}) %collective-permute-start.6) | collective-permute-done | bytes 147488 | tf_op jit(solution)/shard_map/ppermute | solution.py:208
  18.3 0.9 %collective-permute-start.3 = (bf16[4,48,384]{2,1,0:T(8,128)(2,1)S(1)}, bf16[4,48,384]{2,1,0:T(8,128)(2,1)S(1)}, u32[]{:S(2)}, u32[]{:S(2)}) collective-permute-start(bf16[4,48,384]{2,1,0:T(8,128)(2,1)S(1)} %get-tuple-element.49), channel_id=1, source_target_pairs={{0,8},{4,12},{8,0},{12,4},{16,24},{20,28},{24,16},{28,20},{1,9},{5... | collective-permute-start | bytes 442376 | tf_op jit(solution)/shard_map/ppermute | solution.py:208
  19.2 0.0 collective-permute-done.1.refs_1_
  19.2 0.0 collective-permute-start.2
  19.2 0.0 collective-permute-done.refs_0_
  19.2 1.6 %collective-permute-start.7 = (bf16[4,48,384]{2,1,0:T(8,128)(2,1)S(1)}, bf16[4,48,384]{2,1,0:T(8,128)(2,1)S(1)}, u32[]{:S(2)}, u32[]{:S(2)}) collective-permute-start(bf16[4,48,384]{2,1,0:T(8,128)(2,1)S(1)} %get-tuple-element.52), channel_id=1, source_target_pairs={{0,24},{4,28},{8,16},{12,20},{16,8},{20,12},{24,0},{28,4},{1,25},{... | collective-permute-start | bytes 442376 | tf_op jit(solution)/shard_map/ppermute | solution.py:208
  20.8 0.7 %collective-permute-done.5.refs_5_ = bf16[4,48,384]{2,1,0:T(8,128)(2,1)S(1)} collective-permute-done((bf16[4,48,384]{2,1,0:T(8,128)(2,1)S(1)}, bf16[4,48,384]{2,1,0:T(8,128)(2,1)S(1)}, u32[]{:S(2)}, u32[]{:S(2)}) %collective-permute-start.5) | collective-permute-done | bytes 147488 | tf_op jit(solution)/shard_map/ppermute | solution.py:208
  21.5 0.0 collective-permute-done.4.refs_4_
  21.5 3.5 %collective-permute-done.3.refs_3_ = bf16[4,48,384]{2,1,0:T(8,128)(2,1)S(1)} collective-permute-done((bf16[4,48,384]{2,1,0:T(8,128)(2,1)S(1)}, bf16[4,48,384]{2,1,0:T(8,128)(2,1)S(1)}, u32[]{:S(2)}, u32[]{:S(2)}) %collective-permute-start.3) | collective-permute-done | bytes 147488 | tf_op jit(solution)/shard_map/ppermute | solution.py:208
  25.0 0.0 collective-permute-done.2.refs_2_
  25.0 3.2 %collective-permute-done.7.refs_7_ = bf16[4,48,384]{2,1,0:T(8,128)(2,1)S(1)} collective-permute-done((bf16[4,48,384]{2,1,0:T(8,128)(2,1)S(1)}, bf16[4,48,384]{2,1,0:T(8,128)(2,1)S(1)}, u32[]{:S(2)}, u32[]{:S(2)}) %collective-permute-start.7) | collective-permute-done | bytes 147488 | tf_op jit(solution)/shard_map/ppermute | solution.py:208
  28.2 0.0 copy-done.1
  28.2 1.9 %shard_map.46 = (bf16[2,48,384]{2,1,0:T(8,128)(2,1)S(1)}, bf16[2,48,384]{2,1,0:T(8,128)(2,1)S(1)}, bf16[2,48,384]{2,1,0:T(8,128)(2,1)S(1)}, bf16[2,48,384]{2,1,0...) custom-call(s32[8]{0:T(128)S(1)} %copy-done.1, ...), custom_call_target="tpu_custom_call" | custom-call | bytes 2949152 | tf_op jit(solution)/shard_map/pallas_call | solution.py:179
  30.0 1.0 %collective-permute-start.12 = (bf16[2,48,384]{2,1,0:T(8,128)(2,1)S(1)}, bf16[2,48,384]{2,1,0:T(8,128)(2,1)S(1)}, u32[]{:S(2)}, u32[]{:S(2)}) collective-permute-start(bf16[2,48,384]{2,1,0:T(8,128)(2,1)S(1)} %get-tuple-element.30), channel_id=1, source_target_pairs={{0,16},{4,20},{8,24},{12,28},{16,0},{20,4},{24,8},{28,12},{1,17},{... | collective-permute-start | bytes 221192 | tf_op jit(solution)/shard_map/ppermute | solution.py:208
  31.0 0.1 collective-permute-start.13
  31.2 1.1 %collective-permute-start.9 = (bf16[2,48,384]{2,1,0:T(8,128)(2,1)S(1)}, bf16[2,48,384]{2,1,0:T(8,128)(2,1)S(1)}, u32[]{:S(2)}, u32[]{:S(2)}) collective-permute-start(bf16[2,48,384]{2,1,0:T(8,128)(2,1)S(1)} %get-tuple-element.27), channel_id=1, source_target_pairs={{0,4},{4,0},{8,12},{12,8},{16,20},{20,16},{24,28},{28,24},{1,5},{5... | collective-permute-start | bytes 221192 | tf_op jit(solution)/shard_map/ppermute | solution.py:208
  32.2 1.1 %collective-permute-start.14 = (bf16[2,48,384]{2,1,0:T(8,128)(2,1)S(1)}, bf16[2,48,384]{2,1,0:T(8,128)(2,1)S(1)}, u32[]{:S(2)}, u32[]{:S(2)}) collective-permute-start(bf16[2,48,384]{2,1,0:T(8,128)(2,1)S(1)} %get-tuple-element.32), channel_id=1, source_target_pairs={{0,24},{4,28},{8,16},{12,20},{16,8},{20,12},{24,0},{28,4},{1,25},{... | collective-permute-start | bytes 221192 | tf_op jit(solution)/shard_map/ppermute | solution.py:208
  33.4 1.1 %collective-permute-start.15 = (bf16[2,48,384]{2,1,0:T(8,128)(2,1)S(1)}, bf16[2,48,384]{2,1,0:T(8,128)(2,1)S(1)}, u32[]{:S(2)}, u32[]{:S(2)}) collective-permute-start(bf16[2,48,384]{2,1,0:T(8,128)(2,1)S(1)} %get-tuple-element.33), channel_id=1, source_target_pairs={{0,28},{4,24},{8,20},{12,16},{16,12},{20,8},{24,4},{28,0},{1,29},{... | collective-permute-start | bytes 221192 | tf_op jit(solution)/shard_map/ppermute | solution.py:208
  34.5 0.4 collective-permute-done.12.refs_0_
  34.9 1.5 %collective-permute-start.10 = (bf16[2,48,384]{2,1,0:T(8,128)(2,1)S(1)}, bf16[2,48,384]{2,1,0:T(8,128)(2,1)S(1)}, u32[]{:S(2)}, u32[]{:S(2)}) collective-permute-start(bf16[2,48,384]{2,1,0:T(8,128)(2,1)S(1)} %get-tuple-element.28), channel_id=1, source_target_pairs={{0,8},{4,12},{8,0},{12,4},{16,24},{20,28},{24,16},{28,20},{1,9},{5... | collective-permute-start | bytes 221192 | tf_op jit(solution)/shard_map/ppermute | solution.py:208
  36.4 0.0 collective-permute-done.13.refs_1_
  36.4 3.6 %collective-permute-start.11 = (bf16[2,48,384]{2,1,0:T(8,128)(2,1)S(1)}, bf16[2,48,384]{2,1,0:T(8,128)(2,1)S(1)}, u32[]{:S(2)}, u32[]{:S(2)}) collective-permute-start(bf16[2,48,384]{2,1,0:T(8,128)(2,1)S(1)} %get-tuple-element.29), channel_id=1, source_target_pairs={{0,12},{4,8},{8,4},{12,0},{16,28},{20,24},{24,20},{28,16},{1,13},{... | collective-permute-start | bytes 221192 | tf_op jit(solution)/shard_map/ppermute | solution.py:208
  39.9 0.0 collective-permute-done.14.refs_2_
  39.9 0.0 collective-permute-done.15.refs_3_
  40.0 0.7 collective-permute-start.19
  40.7 1.7 %collective-permute-start.17 = (bf16[2,192,384]{2,1,0:T(8,128)(2,1)S(1)}, bf16[2,192,384]{2,1,0:T(8,128)(2,1)S(1)}, u32[]{:S(2)}, u32[]{:S(2)}) collective-permute-start(bf16[2,192,384]{2,1,0:T(8,128)(2,1)S(1)} %shard_map.48.refs_1_), channel_id=1, source_target_pairs={{0,1},{1,0},{2,3},{3,2},{4,5},{5,4},{6,7},{7,6},{8,9},{9,8},{10,11... | collective-permute-start | bytes 884744 | tf_op jit(solution)/shard_map/ppermute | solution.py:215
  42.4 0.0 collective-permute-done.9.refs_1_
  42.4 0.0 collective-permute-done.10.refs_2_
  42.4 0.0 collective-permute-done.11.refs_3_
  42.5 0.0 copy-start.2
  42.5 0.8 %collective-permute-start.18 = (bf16[2,192,384]{2,1,0:T(8,128)(2,1)S(1)}, bf16[2,192,384]{2,1,0:T(8,128)(2,1)S(1)}, u32[]{:S(2)}, u32[]{:S(2)}) collective-permute-start(bf16[2,192,384]{2,1,0:T(8,128)(2,1)S(1)} %shard_map.47.refs_0_), channel_id=1, source_target_pairs={{1,2},{2,1},{5,6},{6,5},{9,10},{10,9},{13,14},{14,13},{17,18},{18,... | collective-permute-start | bytes 884744 | tf_op jit(solution)/shard_map/ppermute | solution.py:215
  43.3 2.9 %collective-permute-start.16 = (bf16[2,192,384]{2,1,0:T(8,128)(2,1)S(1)}, bf16[2,192,384]{2,1,0:T(8,128)(2,1)S(1)}, u32[]{:S(2)}, u32[]{:S(2)}) collective-permute-start(bf16[2,192,384]{2,1,0:T(8,128)(2,1)S(1)} %shard_map.47.refs_0_), channel_id=1, source_target_pairs={{0,1},{1,0},{2,3},{3,2},{4,5},{5,4},{6,7},{7,6},{8,9},{9,8},{10,11... | collective-permute-start | bytes 884744 | tf_op jit(solution)/shard_map/ppermute | solution.py:215
  46.2 0.0 copy-done
  46.2 1.1 %shard_map.49.own = f32[2,384,384]{2,1,0:T(8,128)S(1)} custom-call(bf16[384,384]{1,0:T(8,128)(2,1)S(1)} %bitcast.18, bf16[2,192,384]{2,1,0:T(8,128)(2,1)S(1)} %shard_map.47.refs_0_, bf16[2,192,384]{2,1,0:T(8,128)(2,1)S(1)} %shard_map.48.refs_1_), custom_call_target="tpu_custom_call" | custom-call | flops 452984832 | bytes 2064384 | tf_op jit(solution)/shard_map/pallas_call | solution.py:179
  47.3 0.0 collective-permute-done.19.refs_5_
  47.3 3.3 %collective-permute-done.17.refs_3_ = bf16[2,192,384]{2,1,0:T(8,128)(2,1)S(1)} collective-permute-done((bf16[2,192,384]{2,1,0:T(8,128)(2,1)S(1)}, bf16[2,192,384]{2,1,0:T(8,128)(2,1)S(1)}, u32[]{:S(2)}, u32[]{:S(2)}) %collective-permute-start.17) | collective-permute-done | bytes 294944 | tf_op jit(solution)/shard_map/ppermute | solution.py:215
  50.6 0.0 collective-permute-done.18.refs_4_
  50.6 4.8 %collective-permute-done.16.refs_2_ = bf16[2,192,384]{2,1,0:T(8,128)(2,1)S(1)} collective-permute-done((bf16[2,192,384]{2,1,0:T(8,128)(2,1)S(1)}, bf16[2,192,384]{2,1,0:T(8,128)(2,1)S(1)}, u32[]{:S(2)}, u32[]{:S(2)}) %collective-permute-start.16) | collective-permute-done | bytes 294944 | tf_op jit(solution)/shard_map/ppermute | solution.py:215
  55.4 0.0 copy-done.2
  55.4 2.0 %shard_map.50 = (bf16[2,48,384]{2,1,0:T(8,128)(2,1)S(1)}, bf16[2,48,384]{2,1,0:T(8,128)(2,1)S(1)}, bf16[2,48,384]{2,1,0:T(8,128)(2,1)S(1)}, bf16[2,48,384]{2,1,0...) custom-call(bf16[384,384]{1,0:T(8,128)(2,1)S(1)} %bitcast.21, ...), custom_call_target="tpu_custom_call" | custom-call | flops 905969664 | bytes 3833856 | tf_op jit(solution)/shard_map/pallas_call | solution.py:179
  57.4 0.1 collective-permute-start.20
  57.5 1.7 %collective-permute-start.21 = (bf16[2,48,384]{2,1,0:T(8,128)(2,1)S(1)}, bf16[2,48,384]{2,1,0:T(8,128)(2,1)S(1)}, u32[]{:S(2)}, u32[]{:S(2)}) collective-permute-start(bf16[2,48,384]{2,1,0:T(8,128)(2,1)S(1)} %get-tuple-element.38), channel_id=1, source_target_pairs={{0,8},{4,12},{8,0},{12,4},{16,24},{20,28},{24,16},{28,20},{1,9},{5... | collective-permute-start | bytes 221192 | tf_op jit(solution)/shard_map/ppermute | solution.py:208
  59.2 0.1 collective-permute-start.22
  59.3 2.1 %collective-permute-start.23 = (bf16[2,48,384]{2,1,0:T(8,128)(2,1)S(1)}, bf16[2,48,384]{2,1,0:T(8,128)(2,1)S(1)}, u32[]{:S(2)}, u32[]{:S(2)}) collective-permute-start(bf16[2,48,384]{2,1,0:T(8,128)(2,1)S(1)} %get-tuple-element.40), channel_id=1, source_target_pairs={{0,16},{4,20},{8,24},{12,28},{16,0},{20,4},{24,8},{28,12},{1,17},{... | collective-permute-start | bytes 221192 | tf_op jit(solution)/shard_map/ppermute | solution.py:208
  61.4 0.0 collective-permute-start.24
  61.4 0.0 collective-permute-done.20.refs_2_
  61.4 1.2 %collective-permute-start.25 = (bf16[2,48,384]{2,1,0:T(8,128)(2,1)S(1)}, bf16[2,48,384]{2,1,0:T(8,128)(2,1)S(1)}, u32[]{:S(2)}, u32[]{:S(2)}) collective-permute-start(bf16[2,48,384]{2,1,0:T(8,128)(2,1)S(1)} %get-tuple-element.42), channel_id=1, source_target_pairs={{0,24},{4,28},{8,16},{12,20},{16,8},{20,12},{24,0},{28,4},{1,25},{... | collective-permute-start | bytes 221192 | tf_op jit(solution)/shard_map/ppermute | solution.py:208
  62.7 0.0 collective-permute-done.21.refs_3_
  62.7 1.1 %collective-permute-start.26 = (bf16[2,48,384]{2,1,0:T(8,128)(2,1)S(1)}, bf16[2,48,384]{2,1,0:T(8,128)(2,1)S(1)}, u32[]{:S(2)}, u32[]{:S(2)}) collective-permute-start(bf16[2,48,384]{2,1,0:T(8,128)(2,1)S(1)} %get-tuple-element.43), channel_id=1, source_target_pairs={{0,28},{4,24},{8,20},{12,16},{16,12},{20,8},{24,4},{28,0},{1,29},{... | collective-permute-start | bytes 221192 | tf_op jit(solution)/shard_map/ppermute | solution.py:208
  63.8 0.0 collective-permute-done.22.refs_4_
  63.8 0.4 collective-permute-done.23.refs_5_
  64.2 4.7 %collective-permute-done.24.refs_6_ = bf16[2,48,384]{2,1,0:T(8,128)(2,1)S(1)} collective-permute-done((bf16[2,48,384]{2,1,0:T(8,128)(2,1)S(1)}, bf16[2,48,384]{2,1,0:T(8,128)(2,1)S(1)}, u32[]{:S(2)}, u32[]{:S(2)}) %collective-permute-start.24) | collective-permute-done | bytes 73760 | tf_op jit(solution)/shard_map/ppermute | solution.py:208
  68.9 0.0 collective-permute-done.25.refs_7_
  68.9 0.0 collective-permute-done.26.refs_8_
  68.9 2.6 %shard_map.51 = bf16[2,8,1,48,384]{4,3,2,1,0:T(8,128)(2,1)} custom-call(s32[8]{0:T(128)S(1)} %copy-done.1, bf16[2,48,384]{2,1,0:T(8,128)(2,1)S(1)} %get-tuple-element.36.refs_1_, bf16[2,48,384]{2,1,0:T(8,128)(2,1)S(1)} %collective-permute-done.20.refs_2_, bf16[2,48,384]{2,1,0:T(8,128)(2,1)S(1)} %collective-permute-done.21.refs_3_, ...), custom_call_target="tpu_custom_call" | custom-call | bytes 2359328 | tf_op jit(solution)/shard_map/pallas_call | solution.py:179
  (3 shorter events, 0.1 us)
Async XLA Ops:
  0.0 19.2 %collective-permute-start.1 = (bf16[384,384]{1,0:T(8,128)(2,1)}, bf16[384,384]{1,0:T(8,128)(2,1)S(1)}, u32[]{:S(2)}, u32[]{:S(2)}) collective-permute-start(bf16[384,384]{1,0:T(8,128)(2,1)} %bitcast.19), channel_id=1, source_target_pairs={{1,2},{2,1},{5,6},{6,5},{9,10},{10,9},{13,14},{14,13},{17,18},{18,... | collective-permute-start | bytes 884744 | tf_op jit(solution)/shard_map/ppermute | solution.py:215
  0.7 18.6 %collective-permute-start = (bf16[384,384]{1,0:T(8,128)(2,1)}, bf16[384,384]{1,0:T(8,128)(2,1)S(1)}, u32[]{:S(2)}, u32[]{:S(2)}) collective-permute-start(bf16[384,384]{1,0:T(8,128)(2,1)} %bitcast.20), channel_id=1, source_target_pairs={{0,1},{1,0},{2,3},{3,2},{4,5},{5,4},{6,7},{7,6},{8,9},{9,8},{10,11... | collective-permute-start | bytes 884744 | tf_op jit(solution)/shard_map/ppermute | solution.py:215
  6.6 21.6 %copy-start.1 = (s32[8]{0:T(128)S(1)}, s32[8]{0:T(128)}, u32[]{:S(2)}) copy-start(s32[8]{0:T(128)} %refs_0_.3) | copy-start | bytes 100
  8.1 7.1 %collective-permute-start.8 = (bf16[4,48,384]{2,1,0:T(8,128)(2,1)S(1)}, bf16[4,48,384]{2,1,0:T(8,128)(2,1)S(1)}, u32[]{:S(2)}, u32[]{:S(2)}) collective-permute-start(bf16[4,48,384]{2,1,0:T(8,128)(2,1)S(1)} %get-tuple-element.45), channel_id=1, source_target_pairs={{0,28},{4,24},{8,20},{12,16},{16,12},{20,8},{24,4},{28,0},{1,29},{... | collective-permute-start | bytes 442376 | tf_op jit(solution)/shard_map/ppermute | solution.py:208
  9.5 8.8 %collective-permute-start.6 = (bf16[4,48,384]{2,1,0:T(8,128)(2,1)S(1)}, bf16[4,48,384]{2,1,0:T(8,128)(2,1)S(1)}, u32[]{:S(2)}, u32[]{:S(2)}) collective-permute-start(bf16[4,48,384]{2,1,0:T(8,128)(2,1)S(1)} %get-tuple-element.46), channel_id=1, source_target_pairs={{0,20},{4,16},{8,28},{12,24},{16,4},{20,0},{24,12},{28,8},{1,21},{... | collective-permute-start | bytes 442376 | tf_op jit(solution)/shard_map/ppermute | solution.py:208
  10.8 10.7 %collective-permute-start.5 = (bf16[4,48,384]{2,1,0:T(8,128)(2,1)S(1)}, bf16[4,48,384]{2,1,0:T(8,128)(2,1)S(1)}, u32[]{:S(2)}, u32[]{:S(2)}) collective-permute-start(bf16[4,48,384]{2,1,0:T(8,128)(2,1)S(1)} %get-tuple-element.47), channel_id=1, source_target_pairs={{0,16},{4,20},{8,24},{12,28},{16,0},{20,4},{24,8},{28,12},{1,17},{... | collective-permute-start | bytes 442376 | tf_op jit(solution)/shard_map/ppermute | solution.py:208
  15.2 6.3 %collective-permute-start.4 = (bf16[4,48,384]{2,1,0:T(8,128)(2,1)S(1)}, bf16[4,48,384]{2,1,0:T(8,128)(2,1)S(1)}, u32[]{:S(2)}, u32[]{:S(2)}) collective-permute-start(bf16[4,48,384]{2,1,0:T(8,128)(2,1)S(1)} %get-tuple-element.48), channel_id=1, source_target_pairs={{0,12},{4,8},{8,4},{12,0},{16,28},{20,24},{24,20},{28,16},{1,13},{... | collective-permute-start | bytes 442376 | tf_op jit(solution)/shard_map/ppermute | solution.py:208
  18.3 6.7 %collective-permute-start.3 = (bf16[4,48,384]{2,1,0:T(8,128)(2,1)S(1)}, bf16[4,48,384]{2,1,0:T(8,128)(2,1)S(1)}, u32[]{:S(2)}, u32[]{:S(2)}) collective-permute-start(bf16[4,48,384]{2,1,0:T(8,128)(2,1)S(1)} %get-tuple-element.49), channel_id=1, source_target_pairs={{0,8},{4,12},{8,0},{12,4},{16,24},{20,28},{24,16},{28,20},{1,9},{5... | collective-permute-start | bytes 442376 | tf_op jit(solution)/shard_map/ppermute | solution.py:208
  19.2 5.8 %collective-permute-start.2 = (bf16[4,48,384]{2,1,0:T(8,128)(2,1)S(1)}, bf16[4,48,384]{2,1,0:T(8,128)(2,1)S(1)}, u32[]{:S(2)}, u32[]{:S(2)}) collective-permute-start(bf16[4,48,384]{2,1,0:T(8,128)(2,1)S(1)} %get-tuple-element.50), channel_id=1, source_target_pairs={{0,4},{4,0},{8,12},{12,8},{16,20},{20,16},{24,28},{28,24},{1,5},{5... | collective-permute-start | bytes 442376 | tf_op jit(solution)/shard_map/ppermute | solution.py:208
  19.2 8.9 %collective-permute-start.7 = (bf16[4,48,384]{2,1,0:T(8,128)(2,1)S(1)}, bf16[4,48,384]{2,1,0:T(8,128)(2,1)S(1)}, u32[]{:S(2)}, u32[]{:S(2)}) collective-permute-start(bf16[4,48,384]{2,1,0:T(8,128)(2,1)S(1)} %get-tuple-element.52), channel_id=1, source_target_pairs={{0,24},{4,28},{8,16},{12,20},{16,8},{20,12},{24,0},{28,4},{1,25},{... | collective-permute-start | bytes 442376 | tf_op jit(solution)/shard_map/ppermute | solution.py:208
  20.8 25.4 %copy-start = (bf16[1,384,384]{2,1,0:T(8,128)(2,1)S(1)}, bf16[1,384,384]{2,1,0:T(8,128)(2,1)}, u32[]{:S(2)}) copy-start(bf16[1,384,384]{2,1,0:T(8,128)(2,1)} %param.5) | copy-start | bytes 884740
  30.0 4.8 %collective-permute-start.12 = (bf16[2,48,384]{2,1,0:T(8,128)(2,1)S(1)}, bf16[2,48,384]{2,1,0:T(8,128)(2,1)S(1)}, u32[]{:S(2)}, u32[]{:S(2)}) collective-permute-start(bf16[2,48,384]{2,1,0:T(8,128)(2,1)S(1)} %get-tuple-element.30), channel_id=1, source_target_pairs={{0,16},{4,20},{8,24},{12,28},{16,0},{20,4},{24,8},{28,12},{1,17},{... | collective-permute-start | bytes 221192 | tf_op jit(solution)/shard_map/ppermute | solution.py:208
  31.0 5.3 %collective-permute-start.13 = (bf16[2,48,384]{2,1,0:T(8,128)(2,1)S(1)}, bf16[2,48,384]{2,1,0:T(8,128)(2,1)S(1)}, u32[]{:S(2)}, u32[]{:S(2)}) collective-permute-start(bf16[2,48,384]{2,1,0:T(8,128)(2,1)S(1)} %get-tuple-element.31), channel_id=1, source_target_pairs={{0,20},{4,16},{8,28},{12,24},{16,4},{20,0},{24,12},{28,8},{1,21},{... | collective-permute-start | bytes 221192 | tf_op jit(solution)/shard_map/ppermute | solution.py:208
  31.2 11.3 %collective-permute-start.9 = (bf16[2,48,384]{2,1,0:T(8,128)(2,1)S(1)}, bf16[2,48,384]{2,1,0:T(8,128)(2,1)S(1)}, u32[]{:S(2)}, u32[]{:S(2)}) collective-permute-start(bf16[2,48,384]{2,1,0:T(8,128)(2,1)S(1)} %get-tuple-element.27), channel_id=1, source_target_pairs={{0,4},{4,0},{8,12},{12,8},{16,20},{20,16},{24,28},{28,24},{1,5},{5... | collective-permute-start | bytes 221192 | tf_op jit(solution)/shard_map/ppermute | solution.py:208
  32.2 7.7 %collective-permute-start.14 = (bf16[2,48,384]{2,1,0:T(8,128)(2,1)S(1)}, bf16[2,48,384]{2,1,0:T(8,128)(2,1)S(1)}, u32[]{:S(2)}, u32[]{:S(2)}) collective-permute-start(bf16[2,48,384]{2,1,0:T(8,128)(2,1)S(1)} %get-tuple-element.32), channel_id=1, source_target_pairs={{0,24},{4,28},{8,16},{12,20},{16,8},{20,12},{24,0},{28,4},{1,25},{... | collective-permute-start | bytes 221192 | tf_op jit(solution)/shard_map/ppermute | solution.py:208
  33.4 6.6 %collective-permute-start.15 = (bf16[2,48,384]{2,1,0:T(8,128)(2,1)S(1)}, bf16[2,48,384]{2,1,0:T(8,128)(2,1)S(1)}, u32[]{:S(2)}, u32[]{:S(2)}) collective-permute-start(bf16[2,48,384]{2,1,0:T(8,128)(2,1)S(1)} %get-tuple-element.33), channel_id=1, source_target_pairs={{0,28},{4,24},{8,20},{12,16},{16,12},{20,8},{24,4},{28,0},{1,29},{... | collective-permute-start | bytes 221192 | tf_op jit(solution)/shard_map/ppermute | solution.py:208
  34.9 7.6 %collective-permute-start.10 = (bf16[2,48,384]{2,1,0:T(8,128)(2,1)S(1)}, bf16[2,48,384]{2,1,0:T(8,128)(2,1)S(1)}, u32[]{:S(2)}, u32[]{:S(2)}) collective-permute-start(bf16[2,48,384]{2,1,0:T(8,128)(2,1)S(1)} %get-tuple-element.28), channel_id=1, source_target_pairs={{0,8},{4,12},{8,0},{12,4},{16,24},{20,28},{24,16},{28,20},{1,9},{5... | collective-permute-start | bytes 221192 | tf_op jit(solution)/shard_map/ppermute | solution.py:208
  36.4 6.0 %collective-permute-start.11 = (bf16[2,48,384]{2,1,0:T(8,128)(2,1)S(1)}, bf16[2,48,384]{2,1,0:T(8,128)(2,1)S(1)}, u32[]{:S(2)}, u32[]{:S(2)}) collective-permute-start(bf16[2,48,384]{2,1,0:T(8,128)(2,1)S(1)} %get-tuple-element.29), channel_id=1, source_target_pairs={{0,12},{4,8},{8,4},{12,0},{16,28},{20,24},{24,20},{28,16},{1,13},{... | collective-permute-start | bytes 221192 | tf_op jit(solution)/shard_map/ppermute | solution.py:208
  40.0 7.3 %collective-permute-start.19 = (bf16[2,192,384]{2,1,0:T(8,128)(2,1)S(1)}, bf16[2,192,384]{2,1,0:T(8,128)(2,1)S(1)}, u32[]{:S(2)}, u32[]{:S(2)}) collective-permute-start(bf16[2,192,384]{2,1,0:T(8,128)(2,1)S(1)} %shard_map.48.refs_1_), channel_id=1, source_target_pairs={{1,2},{2,1},{5,6},{6,5},{9,10},{10,9},{13,14},{14,13},{17,18},{18,... | collective-permute-start | bytes 884744 | tf_op jit(solution)/shard_map/ppermute | solution.py:215
  40.7 9.9 %collective-permute-start.17 = (bf16[2,192,384]{2,1,0:T(8,128)(2,1)S(1)}, bf16[2,192,384]{2,1,0:T(8,128)(2,1)S(1)}, u32[]{:S(2)}, u32[]{:S(2)}) collective-permute-start(bf16[2,192,384]{2,1,0:T(8,128)(2,1)S(1)} %shard_map.48.refs_1_), channel_id=1, source_target_pairs={{0,1},{1,0},{2,3},{3,2},{4,5},{5,4},{6,7},{7,6},{8,9},{9,8},{10,11... | collective-permute-start | bytes 884744 | tf_op jit(solution)/shard_map/ppermute | solution.py:215
  42.5 12.9 %copy-start.2 = (bf16[1,384,384]{2,1,0:T(8,128)(2,1)S(1)}, bf16[1,384,384]{2,1,0:T(8,128)(2,1)}, u32[]{:S(2)}) copy-start(bf16[1,384,384]{2,1,0:T(8,128)(2,1)} %param.6) | copy-start | bytes 884740
  42.5 8.1 %collective-permute-start.18 = (bf16[2,192,384]{2,1,0:T(8,128)(2,1)S(1)}, bf16[2,192,384]{2,1,0:T(8,128)(2,1)S(1)}, u32[]{:S(2)}, u32[]{:S(2)}) collective-permute-start(bf16[2,192,384]{2,1,0:T(8,128)(2,1)S(1)} %shard_map.47.refs_0_), channel_id=1, source_target_pairs={{1,2},{2,1},{5,6},{6,5},{9,10},{10,9},{13,14},{14,13},{17,18},{18,... | collective-permute-start | bytes 884744 | tf_op jit(solution)/shard_map/ppermute | solution.py:215
  43.3 12.1 %collective-permute-start.16 = (bf16[2,192,384]{2,1,0:T(8,128)(2,1)S(1)}, bf16[2,192,384]{2,1,0:T(8,128)(2,1)S(1)}, u32[]{:S(2)}, u32[]{:S(2)}) collective-permute-start(bf16[2,192,384]{2,1,0:T(8,128)(2,1)S(1)} %shard_map.47.refs_0_), channel_id=1, source_target_pairs={{0,1},{1,0},{2,3},{3,2},{4,5},{5,4},{6,7},{7,6},{8,9},{9,8},{10,11... | collective-permute-start | bytes 884744 | tf_op jit(solution)/shard_map/ppermute | solution.py:215
  57.4 4.0 %collective-permute-start.20 = (bf16[2,48,384]{2,1,0:T(8,128)(2,1)S(1)}, bf16[2,48,384]{2,1,0:T(8,128)(2,1)S(1)}, u32[]{:S(2)}, u32[]{:S(2)}) collective-permute-start(bf16[2,48,384]{2,1,0:T(8,128)(2,1)S(1)} %get-tuple-element.37), channel_id=1, source_target_pairs={{0,4},{4,0},{8,12},{12,8},{16,20},{20,16},{24,28},{28,24},{1,5},{5... | collective-permute-start | bytes 221192 | tf_op jit(solution)/shard_map/ppermute | solution.py:208
  57.5 5.2 %collective-permute-start.21 = (bf16[2,48,384]{2,1,0:T(8,128)(2,1)S(1)}, bf16[2,48,384]{2,1,0:T(8,128)(2,1)S(1)}, u32[]{:S(2)}, u32[]{:S(2)}) collective-permute-start(bf16[2,48,384]{2,1,0:T(8,128)(2,1)S(1)} %get-tuple-element.38), channel_id=1, source_target_pairs={{0,8},{4,12},{8,0},{12,4},{16,24},{20,28},{24,16},{28,20},{1,9},{5... | collective-permute-start | bytes 221192 | tf_op jit(solution)/shard_map/ppermute | solution.py:208
  59.2 4.6 %collective-permute-start.22 = (bf16[2,48,384]{2,1,0:T(8,128)(2,1)S(1)}, bf16[2,48,384]{2,1,0:T(8,128)(2,1)S(1)}, u32[]{:S(2)}, u32[]{:S(2)}) collective-permute-start(bf16[2,48,384]{2,1,0:T(8,128)(2,1)S(1)} %get-tuple-element.39), channel_id=1, source_target_pairs={{0,12},{4,8},{8,4},{12,0},{16,28},{20,24},{24,20},{28,16},{1,13},{... | collective-permute-start | bytes 221192 | tf_op jit(solution)/shard_map/ppermute | solution.py:208
  59.3 4.9 %collective-permute-start.23 = (bf16[2,48,384]{2,1,0:T(8,128)(2,1)S(1)}, bf16[2,48,384]{2,1,0:T(8,128)(2,1)S(1)}, u32[]{:S(2)}, u32[]{:S(2)}) collective-permute-start(bf16[2,48,384]{2,1,0:T(8,128)(2,1)S(1)} %get-tuple-element.40), channel_id=1, source_target_pairs={{0,16},{4,20},{8,24},{12,28},{16,0},{20,4},{24,8},{28,12},{1,17},{... | collective-permute-start | bytes 221192 | tf_op jit(solution)/shard_map/ppermute | solution.py:208
  61.4 7.5 %collective-permute-start.24 = (bf16[2,48,384]{2,1,0:T(8,128)(2,1)S(1)}, bf16[2,48,384]{2,1,0:T(8,128)(2,1)S(1)}, u32[]{:S(2)}, u32[]{:S(2)}) collective-permute-start(bf16[2,48,384]{2,1,0:T(8,128)(2,1)S(1)} %get-tuple-element.41), channel_id=1, source_target_pairs={{0,20},{4,16},{8,28},{12,24},{16,4},{20,0},{24,12},{28,8},{1,21},{... | collective-permute-start | bytes 221192 | tf_op jit(solution)/shard_map/ppermute | solution.py:208
  61.4 7.5 %collective-permute-start.25 = (bf16[2,48,384]{2,1,0:T(8,128)(2,1)S(1)}, bf16[2,48,384]{2,1,0:T(8,128)(2,1)S(1)}, u32[]{:S(2)}, u32[]{:S(2)}) collective-permute-start(bf16[2,48,384]{2,1,0:T(8,128)(2,1)S(1)} %get-tuple-element.42), channel_id=1, source_target_pairs={{0,24},{4,28},{8,16},{12,20},{16,8},{20,12},{24,0},{28,4},{1,25},{... | collective-permute-start | bytes 221192 | tf_op jit(solution)/shard_map/ppermute | solution.py:208
  62.7 6.2 %collective-permute-start.26 = (bf16[2,48,384]{2,1,0:T(8,128)(2,1)S(1)}, bf16[2,48,384]{2,1,0:T(8,128)(2,1)S(1)}, u32[]{:S(2)}, u32[]{:S(2)}) collective-permute-start(bf16[2,48,384]{2,1,0:T(8,128)(2,1)S(1)} %get-tuple-element.43), channel_id=1, source_target_pairs={{0,28},{4,24},{8,20},{12,16},{16,12},{20,8},{24,4},{28,0},{1,29},{... | collective-permute-start | bytes 221192 | tf_op jit(solution)/shard_map/ppermute | solution.py:208
where the time goes:
time: 71.6 us; the launch traced here: 71.4 us
  starting transfers between devices  35.6 us (50%)
  waiting for transfers between devices  26.7 us (37%)
  Pallas kernels  7.59 us (11%)
  local copies, waits for them, and re-layouts  1.48 us (2%)
    ppermute x21, starting transfers between devices, swap(): lax.ppermute(pieces[j], 'energy', [(i, i ^ j) for i in range(parts)])  22.8 us
    ppermute x21, waiting for transfers between devices, swap(): lax.ppermute(pieces[j], 'energy', [(i, i ^ j) for i in range(parts)])  18.6 us
    ppermute x6, starting transfers between devices, meet(): lax.ppermute(value, 'space', [p for i in lows for p in ((i, i + 1), (i +...  12.7 us
    ppermute x6, waiting for transfers between devices, meet(): lax.ppermute(value, 'space', [p for i in lows for p in ((i, i + 1), (i +...  8.08 us
    pallas_call x6, Pallas kernels, call(): pl.pallas_call(kernel, out_shape=outs, in_specs=[smem()] * tables + [vmem...  7.59 us
    dynamic_slice x1, local copies, waits for them, and re-layouts, direct(): lax.dynamic_slice_in_dim(green[:, 0, 0], (me ^ j) * rows, rows, 1)  1.47 us
  transfers between devices with their start and end apart: 27, of which 10 were waited for; matrix products, arithmetic and copies ran while one was open for 2% of the time, Pallas kernels for 2%

commit v1 on v0

--- a/solution.py
+++ b/solution.py
@@ -41,6 +41,19 @@
         return carry
 
     lax.fori_loop(0, down * across, step, 0)
+
+
+def cut_kernel(order, partners, green, *refs):
+    outs, sems = refs[:-1], refs[-1]
+    rows = outs[0].shape[1]
+    copies = []
+    for i, (j, out) in enumerate(zip(partners, outs)):
+        at = pl.multiple_of(order(j) * rows, rows)
+        copies.append(pltpu.make_async_copy(green.at[:, 0, 0, pl.ds(at, rows)], out, sems.at[i]))
+    for copy in copies:
+        copy.start()
+    for copy in copies:
+        copy.wait()
 
 
 def polar_kernel(order, scaling, *refs):
@@ -197,7 +210,6 @@
     block, cols = green.shape[3:]
     rows = block // parts
     scaling = energies ** (-0.5)
-    me = lax.axis_index("energy")
 
     def order(j):
         return lax.axis_index("energy") ^ j
@@ -215,10 +227,21 @@
             out.append(lax.ppermute(value, "space", [p for i in lows for p in ((i, i + 1), (i + 1, i))]))
         return out
 
-    cut = [lax.dynamic_slice_in_dim(green[:, 0, 0], (me ^ j) * rows, rows, 1) for j in range(parts)]
+    def take(partners):
+        return pl.pallas_call(
+            functools.partial(cut_kernel, order, partners),
+            out_shape=[struct((green.shape[0], rows, cols))] * len(partners),
+            in_specs=[pl.BlockSpec(memory_space=pltpu.HBM)],
+            out_specs=[vmem()] * len(partners),
+            scratch_shapes=[pltpu.SemaphoreType.DMA((len(partners),))],
+            compiler_params=pltpu.CompilerParams(vmem_limit_bytes=VMEM_LIMIT),
+        )(pltpu.with_memory_space_constraint(green, pltpu.HBM))
+
+    first, later = sequence_far(parts)[:2], (*sequence_far(parts)[2:], 0)
+    cut = dict(zip(first + later, (*take(first), *take(later))))
+    cut = [cut[j] for j in range(parts)]
     arrived = swap(cut, range(1, parts))
     upper = meet(v_low[0])
-    arrived[0], *upper = lax.optimization_barrier((arrived[0], *upper))
     piece = struct((2, rows, cols))
     *polar_out, lesser = call(
         functools.partial(polar_kernel, order, scaling),
@@ -349,6 +372,10 @@
     return sigma[:, :, None]
 
 
+def sequence_far(parts):
+    return (*(j + core for j in (6, 4, 2) if j < parts for core in range(2)), *range(8, parts), 1)
+
+
 def solution(mesh):
     in_specs = (
         P(None, "energy", "space", None, None),

time: 71.6 us -> 69.2 us (0.966)
  waiting for transfers between devices: 26.7 us -> 24 us
  Pallas kernels: 7.59 us -> 9.92 us
  local copies, waits for them, and re-layouts: 1.48 us -> 0.01 us
    ppermute x21, waiting for transfers between devices: 18.6 us -> 13.4 us  [swap(): lax.ppermute(pieces[j], 'energy', [(i, i ^ j) for i in range(parts)])]
    ppermute x6, waiting for transfers between devices: 8.08 us -> 10.6 us  [meet(): lax.ppermute(value, 'space', [p for i in lows for p in ((i, i + 1), (i +...]
    pallas_call x0 -> x2, Pallas kernels: none -> 2.34 us  [take(): pl.pallas_call(functools.partial(cut_kernel, order, partners), out_shape=...]
    ppermute x6, starting transfers between devices: 12.7 us -> 10.5 us  [meet(): lax.ppermute(value, 'space', [p for i in lows for p in ((i, i + 1), (i +...]
    ppermute x21, starting transfers between devices: 22.8 us -> 24.4 us  [swap(): lax.ppermute(pieces[j], 'energy', [(i, i ^ j) for i in range(parts)])]
    dynamic_slice x1 -> x0, local copies, waits for them, and re-layouts: 1.47 us -> none  [direct(): lax.dynamic_slice_in_dim(green[:, 0, 0], (me ^ j) * rows, rows, 1)]
  transfers between devices with their start and end apart: 27 -> 27, of which waited for: 10 -> 12; matrix products, arithmetic and copies ran while one was open for 2% -> 0% of each run, Pallas kernels for 2% -> 6%
where the time goes in v1:
time: 69.2 us; the launch traced here: 69 us
  starting transfers between devices  34.9 us (50%)
  waiting for transfers between devices  24 us (35%)
  Pallas kernels  9.92 us (14%)
    ppermute x21, starting transfers between devices, swap(): lax.ppermute(pieces[j], 'energy', [(i, i ^ j) for i in range(parts)])  24.4 us
    ppermute x21, waiting for transfers between devices, swap(): lax.ppermute(pieces[j], 'energy', [(i, i ^ j) for i in range(parts)])  13.4 us
    ppermute x6, waiting for transfers between devices, meet(): lax.ppermute(value, 'space', [p for i in lows for p in ((i, i + 1), (i +...  10.6 us
    ppermute x6, starting transfers between devices, meet(): lax.ppermute(value, 'space', [p for i in lows for p in ((i, i + 1), (i +...  10.5 us
    pallas_call x6, Pallas kernels, call(): pl.pallas_call(kernel, out_shape=outs, in_specs=[smem()] * tables + [vmem...  7.59 us
    pallas_call x2, Pallas kernels, take(): pl.pallas_call(functools.partial(cut_kernel, order, partners), out_shape=...  2.34 us
  transfers between devices with their start and end apart: 27, of which 12 were waited for; matrix products, arithmetic and copies ran while one was open for 0% of the time, Pallas kernels for 6%

profile of v1, /device:TPU:0, one launch (start us, length us, event | category | flops | bytes accessed | tf_op | source)
XLA Modules:
  0.0 69.0 jit_solution(9318977897951500540)
XLA Ops:
  0.0 0.0 copy-start.2
  0.0 1.0 %shard_map.47 = (bf16[4,48,384]{2,1,0:T(8,128)(2,1)S(1)}, bf16[4,48,384]{2,1,0:T(8,128)(2,1)S(1)}) custom-call(bf16[4,1,1,384,384]{4,3,2,1,0:T(8,128)(2,1)} %green.3), custom_call_target="tpu_custom_call" | custom-call | tf_op jit(solution)/shard_map/pallas_call | solution.py:231
  1.1 4.0 %collective-permute-start.5 = (bf16[4,48,384]{2,1,0:T(8,128)(2,1)S(1)}, bf16[4,48,384]{2,1,0:T(8,128)(2,1)S(1)}, u32[]{:S(2)}, u32[]{:S(2)}) collective-permute-start(bf16[4,48,384]{2,1,0:T(8,128)(2,1)S(1)} %get-tuple-element.36), channel_id=1, source_target_pairs={{0,24},{4,28},{8,16},{12,20},{16,8},{20,12},{24,0},{28,4},{1,25},{... | collective-permute-start | bytes 442376 | tf_op jit(solution)/shard_map/ppermute | solution.py:220
  5.0 0.0 collective-permute-start.6
  5.0 1.3 %shard_map.46 = (bf16[4,48,384]{2,1,0:T(8,128)(2,1)S(1)}, bf16[4,48,384]{2,1,0:T(8,128)(2,1)S(1)}, bf16[4,48,384]{2,1,0:T(8,128)(2,1)S(1)}, bf16[4,48,384]{2,1,0...) custom-call(bf16[4,1,1,384,384]{4,3,2,1,0:T(8,128)(2,1)} %green.3), custom_call_target="tpu_custom_call" | custom-call | tf_op jit(solution)/shard_map/pallas_call | solution.py:231
  6.3 0.3 collective-permute-start
  6.6 1.9 %collective-permute-start.1 = (bf16[4,48,384]{2,1,0:T(8,128)(2,1)S(1)}, bf16[4,48,384]{2,1,0:T(8,128)(2,1)S(1)}, u32[]{:S(2)}, u32[]{:S(2)}) collective-permute-start(bf16[4,48,384]{2,1,0:T(8,128)(2,1)S(1)} %get-tuple-element.32), channel_id=1, source_target_pairs={{0,8},{4,12},{8,0},{12,4},{16,24},{20,28},{24,16},{28,20},{1,9},{5... | collective-permute-start | bytes 442376 | tf_op jit(solution)/shard_map/ppermute | solution.py:220
  8.5 0.0 collective-permute-start.2
  8.5 0.8 %collective-permute-done.5.refs_7_ = bf16[4,48,384]{2,1,0:T(8,128)(2,1)S(1)} collective-permute-done((bf16[4,48,384]{2,1,0:T(8,128)(2,1)S(1)}, bf16[4,48,384]{2,1,0:T(8,128)(2,1)S(1)}, u32[]{:S(2)}, u32[]{:S(2)}) %collective-permute-start.5) | collective-permute-done | bytes 147488 | tf_op jit(solution)/shard_map/ppermute | solution.py:220
  9.3 2.5 %collective-permute-start.3 = (bf16[4,48,384]{2,1,0:T(8,128)(2,1)S(1)}, bf16[4,48,384]{2,1,0:T(8,128)(2,1)S(1)}, u32[]{:S(2)}, u32[]{:S(2)}) collective-permute-start(bf16[4,48,384]{2,1,0:T(8,128)(2,1)S(1)} %get-tuple-element.34), channel_id=1, source_target_pairs={{0,16},{4,20},{8,24},{12,28},{16,0},{20,4},{24,8},{28,12},{1,17},{... | collective-permute-start | bytes 442376 | tf_op jit(solution)/shard_map/ppermute | solution.py:220
  11.7 0.7 %collective-permute-done.6.refs_8_ = bf16[4,48,384]{2,1,0:T(8,128)(2,1)S(1)} collective-permute-done((bf16[4,48,384]{2,1,0:T(8,128)(2,1)S(1)}, bf16[4,48,384]{2,1,0:T(8,128)(2,1)S(1)}, u32[]{:S(2)}, u32[]{:S(2)}) %collective-permute-start.6) | collective-permute-done | bytes 147488 | tf_op jit(solution)/shard_map/ppermute | solution.py:220
  12.4 1.9 %collective-permute-start.4 = (bf16[4,48,384]{2,1,0:T(8,128)(2,1)S(1)}, bf16[4,48,384]{2,1,0:T(8,128)(2,1)S(1)}, u32[]{:S(2)}, u32[]{:S(2)}) collective-permute-start(bf16[4,48,384]{2,1,0:T(8,128)(2,1)S(1)} %get-tuple-element.35), channel_id=1, source_target_pairs={{0,20},{4,16},{8,28},{12,24},{16,4},{20,0},{24,12},{28,8},{1,21},{... | collective-permute-start | bytes 442376 | tf_op jit(solution)/shard_map/ppermute | solution.py:220
  14.3 0.0 collective-permute-done.refs_2_
  14.3 0.0 copy-done.2
  14.3 0.7 collective-permute-start.15
  15.0 1.6 %collective-permute-done.1.refs_3_ = bf16[4,48,384]{2,1,0:T(8,128)(2,1)S(1)} collective-permute-done((bf16[4,48,384]{2,1,0:T(8,128)(2,1)S(1)}, bf16[4,48,384]{2,1,0:T(8,128)(2,1)S(1)}, u32[]{:S(2)}, u32[]{:S(2)}) %collective-permute-start.1) | collective-permute-done | bytes 147488 | tf_op jit(solution)/shard_map/ppermute | solution.py:220
  16.6 1.0 %collective-permute-done.2.refs_4_ = bf16[4,48,384]{2,1,0:T(8,128)(2,1)S(1)} collective-permute-done((bf16[4,48,384]{2,1,0:T(8,128)(2,1)S(1)}, bf16[4,48,384]{2,1,0:T(8,128)(2,1)S(1)}, u32[]{:S(2)}, u32[]{:S(2)}) %collective-permute-start.2) | collective-permute-done | bytes 147488 | tf_op jit(solution)/shard_map/ppermute | solution.py:220
  17.6 0.0 collective-permute-done.3.refs_5_
  17.6 0.8 %collective-permute-done.4.refs_6_ = bf16[4,48,384]{2,1,0:T(8,128)(2,1)S(1)} collective-permute-done((bf16[4,48,384]{2,1,0:T(8,128)(2,1)S(1)}, bf16[4,48,384]{2,1,0:T(8,128)(2,1)S(1)}, u32[]{:S(2)}, u32[]{:S(2)}) %collective-permute-start.4) | collective-permute-done | bytes 147488 | tf_op jit(solution)/shard_map/ppermute | solution.py:220
  18.5 0.0 copy-done.1
  18.5 1.9 %shard_map.48 = (bf16[2,48,384]{2,1,0:T(8,128)(2,1)S(1)}, bf16[2,48,384]{2,1,0:T(8,128)(2,1)S(1)}, bf16[2,48,384]{2,1,0:T(8,128)(2,1)S(1)}, bf16[2,48,384]{2,1,0...) custom-call(s32[8]{0:T(128)S(1)} %copy-done.1, ...), custom_call_target="tpu_custom_call" | custom-call | bytes 2949152 | tf_op jit(solution)/shard_map/pallas_call | solution.py:192
  20.3 0.8 %collective-permute-start.10 = (bf16[2,48,384]{2,1,0:T(8,128)(2,1)S(1)}, bf16[2,48,384]{2,1,0:T(8,128)(2,1)S(1)}, u32[]{:S(2)}, u32[]{:S(2)}) collective-permute-start(bf16[2,48,384]{2,1,0:T(8,128)(2,1)S(1)} %get-tuple-element.42), channel_id=1, source_target_pairs={{0,16},{4,20},{8,24},{12,28},{16,0},{20,4},{24,8},{28,12},{1,17},{... | collective-permute-start | bytes 221192 | tf_op jit(solution)/shard_map/ppermute | solution.py:220
  21.1 0.8 %collective-permute-start.11 = (bf16[2,48,384]{2,1,0:T(8,128)(2,1)S(1)}, bf16[2,48,384]{2,1,0:T(8,128)(2,1)S(1)}, u32[]{:S(2)}, u32[]{:S(2)}) collective-permute-start(bf16[2,48,384]{2,1,0:T(8,128)(2,1)S(1)} %get-tuple-element.43), channel_id=1, source_target_pairs={{0,20},{4,16},{8,28},{12,24},{16,4},{20,0},{24,12},{28,8},{1,21},{... | collective-permute-start | bytes 221192 | tf_op jit(solution)/shard_map/ppermute | solution.py:220
  21.9 2.6 %collective-permute-start.12 = (bf16[2,48,384]{2,1,0:T(8,128)(2,1)S(1)}, bf16[2,48,384]{2,1,0:T(8,128)(2,1)S(1)}, u32[]{:S(2)}, u32[]{:S(2)}) collective-permute-start(bf16[2,48,384]{2,1,0:T(8,128)(2,1)S(1)} %get-tuple-element.44), channel_id=1, source_target_pairs={{0,24},{4,28},{8,16},{12,20},{16,8},{20,12},{24,0},{28,4},{1,25},{... | collective-permute-start | bytes 221192 | tf_op jit(solution)/shard_map/ppermute | solution.py:220
  24.4 0.3 collective-permute-start.13
  24.8 0.6 collective-permute-done.10.refs_0_
  25.4 0.0 collective-permute-start.7
  25.4 2.9 %collective-permute-done.11.refs_1_ = bf16[2,48,384]{2,1,0:T(8,128)(2,1)S(1)} collective-permute-done((bf16[2,48,384]{2,1,0:T(8,128)(2,1)S(1)}, bf16[2,48,384]{2,1,0:T(8,128)(2,1)S(1)}, u32[]{:S(2)}, u32[]{:S(2)}) %collective-permute-start.11) | collective-permute-done | bytes 73760 | tf_op jit(solution)/shard_map/ppermute | solution.py:220
  28.3 1.7 %collective-permute-start.8 = (bf16[2,48,384]{2,1,0:T(8,128)(2,1)S(1)}, bf16[2,48,384]{2,1,0:T(8,128)(2,1)S(1)}, u32[]{:S(2)}, u32[]{:S(2)}) collective-permute-start(bf16[2,48,384]{2,1,0:T(8,128)(2,1)S(1)} %get-tuple-element.40), channel_id=1, source_target_pairs={{0,8},{4,12},{8,0},{12,4},{16,24},{20,28},{24,16},{28,20},{1,9},{5... | collective-permute-start | bytes 221192 | tf_op jit(solution)/shard_map/ppermute | solution.py:220
  30.0 0.0 collective-permute-done.12.refs_2_
  30.0 0.5 collective-permute-start.9
  30.5 0.0 collective-permute-done.13.refs_3_
  30.5 2.2 %collective-permute-start.14 = (bf16[384,384]{1,0:T(8,128)(2,1)S(1)}, bf16[384,384]{1,0:T(8,128)(2,1)S(1)}, u32[]{:S(2)}, u32[]{:S(2)}) collective-permute-start(bf16[384,384]{1,0:T(8,128)(2,1)S(1)} %bitcast.4), channel_id=1, source_target_pairs={{0,1},{1,0},{2,3},{3,2},{4,5},{5,4},{6,7},{7,6},{8,9},{9,8},{10,11... | collective-permute-start | bytes 884744 | tf_op jit(solution)/shard_map/ppermute | solution.py:227
  32.7 0.0 collective-permute-done.7.refs_1_
  32.7 0.7 collective-permute-start.19
  33.4 0.1 collective-permute-done.8.refs_2_
  33.4 4.4 %collective-permute-start.17 = (bf16[2,192,384]{2,1,0:T(8,128)(2,1)S(1)}, bf16[2,192,384]{2,1,0:T(8,128)(2,1)S(1)}, u32[]{:S(2)}, u32[]{:S(2)}) collective-permute-start(bf16[2,192,384]{2,1,0:T(8,128)(2,1)S(1)} %shard_map.50.refs_1_), channel_id=1, source_target_pairs={{0,1},{1,0},{2,3},{3,2},{4,5},{5,4},{6,7},{7,6},{8,9},{9,8},{10,11... | collective-permute-start | bytes 884744 | tf_op jit(solution)/shard_map/ppermute | solution.py:227
  37.8 0.0 collective-permute-done.9.refs_3_
  37.9 0.7 collective-permute-start.18
  38.6 0.0 collective-permute-done.15.refs_1_
  38.6 1.9 %collective-permute-start.16 = (bf16[2,192,384]{2,1,0:T(8,128)(2,1)S(1)}, bf16[2,192,384]{2,1,0:T(8,128)(2,1)S(1)}, u32[]{:S(2)}, u32[]{:S(2)}) collective-permute-start(bf16[2,192,384]{2,1,0:T(8,128)(2,1)S(1)} %shard_map.49.refs_0_), channel_id=1, source_target_pairs={{0,1},{1,0},{2,3},{3,2},{4,5},{5,4},{6,7},{7,6},{8,9},{9,8},{10,11... | collective-permute-start | bytes 884744 | tf_op jit(solution)/shard_map/ppermute | solution.py:227
  40.5 0.0 copy-done
  40.5 1.1 %shard_map.51.own = f32[2,384,384]{2,1,0:T(8,128)S(1)} custom-call(bf16[384,384]{1,0:T(8,128)(2,1)S(1)} %bitcast.2, bf16[2,192,384]{2,1,0:T(8,128)(2,1)S(1)} %shard_map.49.refs_0_, bf16[2,192,384]{2,1,0:T(8,128)(2,1)S(1)} %shard_map.50.refs_1_), custom_call_target="tpu_custom_call" | custom-call | flops 452984832 | bytes 2064384 | tf_op jit(solution)/shard_map/pallas_call | solution.py:192
  41.6 0.0 collective-permute-done.14.refs_0_
  41.6 0.0 collective-permute-done.19.refs_5_
  41.6 5.2 %collective-permute-done.17.refs_3_ = bf16[2,192,384]{2,1,0:T(8,128)(2,1)S(1)} collective-permute-done((bf16[2,192,384]{2,1,0:T(8,128)(2,1)S(1)}, bf16[2,192,384]{2,1,0:T(8,128)(2,1)S(1)}, u32[]{:S(2)}, u32[]{:S(2)}) %collective-permute-start.17) | collective-permute-done | bytes 294944 | tf_op jit(solution)/shard_map/ppermute | solution.py:227
  46.8 0.0 collective-permute-done.18.refs_4_
  46.8 5.4 %collective-permute-done.16.refs_2_ = bf16[2,192,384]{2,1,0:T(8,128)(2,1)S(1)} collective-permute-done((bf16[2,192,384]{2,1,0:T(8,128)(2,1)S(1)}, bf16[2,192,384]{2,1,0:T(8,128)(2,1)S(1)}, u32[]{:S(2)}, u32[]{:S(2)}) %collective-permute-start.16) | collective-permute-done | bytes 294944 | tf_op jit(solution)/shard_map/ppermute | solution.py:227
  52.2 2.0 %shard_map.52 = (bf16[2,48,384]{2,1,0:T(8,128)(2,1)S(1)}, bf16[2,48,384]{2,1,0:T(8,128)(2,1)S(1)}, bf16[2,48,384]{2,1,0:T(8,128)(2,1)S(1)}, bf16[2,48,384]{2,1,0...) custom-call(bf16[384,384]{1,0:T(8,128)(2,1)S(1)} %bitcast.5, ...), custom_call_target="tpu_custom_call" | custom-call | flops 905969664 | bytes 3833856 | tf_op jit(solution)/shard_map/pallas_call | solution.py:192
  54.2 0.1 collective-permute-start.20
  54.3 2.1 %collective-permute-start.21 = (bf16[2,48,384]{2,1,0:T(8,128)(2,1)S(1)}, bf16[2,48,384]{2,1,0:T(8,128)(2,1)S(1)}, u32[]{:S(2)}, u32[]{:S(2)}) collective-permute-start(bf16[2,48,384]{2,1,0:T(8,128)(2,1)S(1)} %get-tuple-element.48), channel_id=1, source_target_pairs={{0,8},{4,12},{8,0},{12,4},{16,24},{20,28},{24,16},{28,20},{1,9},{5... | collective-permute-start | bytes 221192 | tf_op jit(solution)/shard_map/ppermute | solution.py:220
  56.4 0.0 collective-permute-start.22
  56.4 2.2 %collective-permute-start.23 = (bf16[2,48,384]{2,1,0:T(8,128)(2,1)S(1)}, bf16[2,48,384]{2,1,0:T(8,128)(2,1)S(1)}, u32[]{:S(2)}, u32[]{:S(2)}) collective-permute-start(bf16[2,48,384]{2,1,0:T(8,128)(2,1)S(1)} %get-tuple-element.50), channel_id=1, source_target_pairs={{0,16},{4,20},{8,24},{12,28},{16,0},{20,4},{24,8},{28,12},{1,17},{... | collective-permute-start | bytes 221192 | tf_op jit(solution)/shard_map/ppermute | solution.py:220
  58.7 0.0 collective-permute-start.24
  58.7 0.0 collective-permute-done.20.refs_2_
  58.7 2.7 %collective-permute-start.25 = (bf16[2,48,384]{2,1,0:T(8,128)(2,1)S(1)}, bf16[2,48,384]{2,1,0:T(8,128)(2,1)S(1)}, u32[]{:S(2)}, u32[]{:S(2)}) collective-permute-start(bf16[2,48,384]{2,1,0:T(8,128)(2,1)S(1)} %get-tuple-element.52), channel_id=1, source_target_pairs={{0,24},{4,28},{8,16},{12,20},{16,8},{20,12},{24,0},{28,4},{1,25},{... | collective-permute-start | bytes 221192 | tf_op jit(solution)/shard_map/ppermute | solution.py:220
  61.3 0.0 collective-permute-done.21.refs_3_
  61.3 0.3 collective-permute-start.26
  61.6 0.0 collective-permute-done.22.refs_4_
  61.6 0.0 collective-permute-done.23.refs_5_
  61.6 3.9 %collective-permute-done.24.refs_6_ = bf16[2,48,384]{2,1,0:T(8,128)(2,1)S(1)} collective-permute-done((bf16[2,48,384]{2,1,0:T(8,128)(2,1)S(1)}, bf16[2,48,384]{2,1,0:T(8,128)(2,1)S(1)}, u32[]{:S(2)}, u32[]{:S(2)}) %collective-permute-start.24) | collective-permute-done | bytes 73760 | tf_op jit(solution)/shard_map/ppermute | solution.py:220
  65.5 0.0 collective-permute-done.25.refs_7_
  65.5 1.0 %collective-permute-done.26.refs_8_ = bf16[2,48,384]{2,1,0:T(8,128)(2,1)S(1)} collective-permute-done((bf16[2,48,384]{2,1,0:T(8,128)(2,1)S(1)}, bf16[2,48,384]{2,1,0:T(8,128)(2,1)S(1)}, u32[]{:S(2)}, u32[]{:S(2)}) %collective-permute-start.26) | collective-permute-done | bytes 73760 | tf_op jit(solution)/shard_map/ppermute | solution.py:220
  66.5 2.5 %shard_map.53 = bf16[2,8,1,48,384]{4,3,2,1,0:T(8,128)(2,1)} custom-call(s32[8]{0:T(128)S(1)} %copy-done.1, bf16[2,48,384]{2,1,0:T(8,128)(2,1)S(1)} %get-tuple-element.46.refs_1_, bf16[2,48,384]{2,1,0:T(8,128)(2,1)S(1)} %collective-permute-done.20.refs_2_, bf16[2,48,384]{2,1,0:T(8,128)(2,1)S(1)} %collective-permute-done.21.refs_3_, ...), custom_call_target="tpu_custom_call" | custom-call | bytes 2359328 | tf_op jit(solution)/shard_map/pallas_call | solution.py:192
  (4 shorter events, 0.1 us)
Async XLA Ops:
  0.0 14.3 %copy-start.2 = (bf16[1,384,384]{2,1,0:T(8,128)(2,1)S(1)}, bf16[1,384,384]{2,1,0:T(8,128)(2,1)}, u32[]{:S(2)}) copy-start(bf16[1,384,384]{2,1,0:T(8,128)(2,1)} %param.6) | copy-start | bytes 884740
  0.0 18.5 %copy-start.1 = (s32[8]{0:T(128)S(1)}, s32[8]{0:T(128)}, u32[]{:S(2)}) copy-start(s32[8]{0:T(128)} %refs_0_.3) | copy-start | bytes 100
  1.1 8.2 %collective-permute-start.5 = (bf16[4,48,384]{2,1,0:T(8,128)(2,1)S(1)}, bf16[4,48,384]{2,1,0:T(8,128)(2,1)S(1)}, u32[]{:S(2)}, u32[]{:S(2)}) collective-permute-start(bf16[4,48,384]{2,1,0:T(8,128)(2,1)S(1)} %get-tuple-element.36), channel_id=1, source_target_pairs={{0,24},{4,28},{8,16},{12,20},{16,8},{20,12},{24,0},{28,4},{1,25},{... | collective-permute-start | bytes 442376 | tf_op jit(solution)/shard_map/ppermute | solution.py:220
  5.0 7.4 %collective-permute-start.6 = (bf16[4,48,384]{2,1,0:T(8,128)(2,1)S(1)}, bf16[4,48,384]{2,1,0:T(8,128)(2,1)S(1)}, u32[]{:S(2)}, u32[]{:S(2)}) collective-permute-start(bf16[4,48,384]{2,1,0:T(8,128)(2,1)S(1)} %get-tuple-element.37), channel_id=1, source_target_pairs={{0,28},{4,24},{8,20},{12,16},{16,12},{20,8},{24,4},{28,0},{1,29},{... | collective-permute-start | bytes 442376 | tf_op jit(solution)/shard_map/ppermute | solution.py:220
  6.3 8.0 %collective-permute-start = (bf16[4,48,384]{2,1,0:T(8,128)(2,1)S(1)}, bf16[4,48,384]{2,1,0:T(8,128)(2,1)S(1)}, u32[]{:S(2)}, u32[]{:S(2)}) collective-permute-start(bf16[4,48,384]{2,1,0:T(8,128)(2,1)S(1)} %get-tuple-element.31), channel_id=1, source_target_pairs={{0,4},{4,0},{8,12},{12,8},{16,20},{20,16},{24,28},{28,24},{1,5},{5... | collective-permute-start | bytes 442376 | tf_op jit(solution)/shard_map/ppermute | solution.py:220
  6.6 10.0 %collective-permute-start.1 = (bf16[4,48,384]{2,1,0:T(8,128)(2,1)S(1)}, bf16[4,48,384]{2,1,0:T(8,128)(2,1)S(1)}, u32[]{:S(2)}, u32[]{:S(2)}) collective-permute-start(bf16[4,48,384]{2,1,0:T(8,128)(2,1)S(1)} %get-tuple-element.32), channel_id=1, source_target_pairs={{0,8},{4,12},{8,0},{12,4},{16,24},{20,28},{24,16},{28,20},{1,9},{5... | collective-permute-start | bytes 442376 | tf_op jit(solution)/shard_map/ppermute | solution.py:220
  8.5 9.1 %collective-permute-start.2 = (bf16[4,48,384]{2,1,0:T(8,128)(2,1)S(1)}, bf16[4,48,384]{2,1,0:T(8,128)(2,1)S(1)}, u32[]{:S(2)}, u32[]{:S(2)}) collective-permute-start(bf16[4,48,384]{2,1,0:T(8,128)(2,1)S(1)} %get-tuple-element.33), channel_id=1, source_target_pairs={{0,12},{4,8},{8,4},{12,0},{16,28},{20,24},{24,20},{28,16},{1,13},{... | collective-permute-start | bytes 442376 | tf_op jit(solution)/shard_map/ppermute | solution.py:220
  9.3 8.4 %collective-permute-start.3 = (bf16[4,48,384]{2,1,0:T(8,128)(2,1)S(1)}, bf16[4,48,384]{2,1,0:T(8,128)(2,1)S(1)}, u32[]{:S(2)}, u32[]{:S(2)}) collective-permute-start(bf16[4,48,384]{2,1,0:T(8,128)(2,1)S(1)} %get-tuple-element.34), channel_id=1, source_target_pairs={{0,16},{4,20},{8,24},{12,28},{16,0},{20,4},{24,8},{28,12},{1,17},{... | collective-permute-start | bytes 442376 | tf_op jit(solution)/shard_map/ppermute | solution.py:220
  12.4 6.0 %collective-permute-start.4 = (bf16[4,48,384]{2,1,0:T(8,128)(2,1)S(1)}, bf16[4,48,384]{2,1,0:T(8,128)(2,1)S(1)}, u32[]{:S(2)}, u32[]{:S(2)}) collective-permute-start(bf16[4,48,384]{2,1,0:T(8,128)(2,1)S(1)} %get-tuple-element.35), channel_id=1, source_target_pairs={{0,20},{4,16},{8,28},{12,24},{16,4},{20,0},{24,12},{28,8},{1,21},{... | collective-permute-start | bytes 442376 | tf_op jit(solution)/shard_map/ppermute | solution.py:220
  14.3 24.2 %collective-permute-start.15 = (bf16[384,384]{1,0:T(8,128)(2,1)S(1)}, bf16[384,384]{1,0:T(8,128)(2,1)S(1)}, u32[]{:S(2)}, u32[]{:S(2)}) collective-permute-start(bf16[384,384]{1,0:T(8,128)(2,1)S(1)} %bitcast.3), channel_id=1, source_target_pairs={{1,2},{2,1},{5,6},{6,5},{9,10},{10,9},{13,14},{14,13},{17,18},{18,... | collective-permute-start | bytes 884744 | tf_op jit(solution)/shard_map/ppermute | solution.py:227
  18.5 22.0 %copy-start = (bf16[1,384,384]{2,1,0:T(8,128)(2,1)S(1)}, bf16[1,384,384]{2,1,0:T(8,128)(2,1)}, u32[]{:S(2)}) copy-start(bf16[1,384,384]{2,1,0:T(8,128)(2,1)} %param.5) | copy-start | bytes 884740
  20.3 5.0 %collective-permute-start.10 = (bf16[2,48,384]{2,1,0:T(8,128)(2,1)S(1)}, bf16[2,48,384]{2,1,0:T(8,128)(2,1)S(1)}, u32[]{:S(2)}, u32[]{:S(2)}) collective-permute-start(bf16[2,48,384]{2,1,0:T(8,128)(2,1)S(1)} %get-tuple-element.42), channel_id=1, source_target_pairs={{0,16},{4,20},{8,24},{12,28},{16,0},{20,4},{24,8},{28,12},{1,17},{... | collective-permute-start | bytes 221192 | tf_op jit(solution)/shard_map/ppermute | solution.py:220
  21.1 7.2 %collective-permute-start.11 = (bf16[2,48,384]{2,1,0:T(8,128)(2,1)S(1)}, bf16[2,48,384]{2,1,0:T(8,128)(2,1)S(1)}, u32[]{:S(2)}, u32[]{:S(2)}) collective-permute-start(bf16[2,48,384]{2,1,0:T(8,128)(2,1)S(1)} %get-tuple-element.43), channel_id=1, source_target_pairs={{0,20},{4,16},{8,28},{12,24},{16,4},{20,0},{24,12},{28,8},{1,21},{... | collective-permute-start | bytes 221192 | tf_op jit(solution)/shard_map/ppermute | solution.py:220
  21.9 8.1 %collective-permute-start.12 = (bf16[2,48,384]{2,1,0:T(8,128)(2,1)S(1)}, bf16[2,48,384]{2,1,0:T(8,128)(2,1)S(1)}, u32[]{:S(2)}, u32[]{:S(2)}) collective-permute-start(bf16[2,48,384]{2,1,0:T(8,128)(2,1)S(1)} %get-tuple-element.44), channel_id=1, source_target_pairs={{0,24},{4,28},{8,16},{12,20},{16,8},{20,12},{24,0},{28,4},{1,25},{... | collective-permute-start | bytes 221192 | tf_op jit(solution)/shard_map/ppermute | solution.py:220
  24.4 6.0 %collective-permute-start.13 = (bf16[2,48,384]{2,1,0:T(8,128)(2,1)S(1)}, bf16[2,48,384]{2,1,0:T(8,128)(2,1)S(1)}, u32[]{:S(2)}, u32[]{:S(2)}) collective-permute-start(bf16[2,48,384]{2,1,0:T(8,128)(2,1)S(1)} %get-tuple-element.45), channel_id=1, source_target_pairs={{0,28},{4,24},{8,20},{12,16},{16,12},{20,8},{24,4},{28,0},{1,29},{... | collective-permute-start | bytes 221192 | tf_op jit(solution)/shard_map/ppermute | solution.py:220
  25.4 7.3 %collective-permute-start.7 = (bf16[2,48,384]{2,1,0:T(8,128)(2,1)S(1)}, bf16[2,48,384]{2,1,0:T(8,128)(2,1)S(1)}, u32[]{:S(2)}, u32[]{:S(2)}) collective-permute-start(bf16[2,48,384]{2,1,0:T(8,128)(2,1)S(1)} %get-tuple-element.39), channel_id=1, source_target_pairs={{0,4},{4,0},{8,12},{12,8},{16,20},{20,16},{24,28},{28,24},{1,5},{5... | collective-permute-start | bytes 221192 | tf_op jit(solution)/shard_map/ppermute | solution.py:220
  28.3 5.1 %collective-permute-start.8 = (bf16[2,48,384]{2,1,0:T(8,128)(2,1)S(1)}, bf16[2,48,384]{2,1,0:T(8,128)(2,1)S(1)}, u32[]{:S(2)}, u32[]{:S(2)}) collective-permute-start(bf16[2,48,384]{2,1,0:T(8,128)(2,1)S(1)} %get-tuple-element.40), channel_id=1, source_target_pairs={{0,8},{4,12},{8,0},{12,4},{16,24},{20,28},{24,16},{28,20},{1,9},{5... | collective-permute-start | bytes 221192 | tf_op jit(solution)/shard_map/ppermute | solution.py:220
  30.0 7.8 %collective-permute-start.9 = (bf16[2,48,384]{2,1,0:T(8,128)(2,1)S(1)}, bf16[2,48,384]{2,1,0:T(8,128)(2,1)S(1)}, u32[]{:S(2)}, u32[]{:S(2)}) collective-permute-start(bf16[2,48,384]{2,1,0:T(8,128)(2,1)S(1)} %get-tuple-element.41), channel_id=1, source_target_pairs={{0,12},{4,8},{8,4},{12,0},{16,28},{20,24},{24,20},{28,16},{1,13},{... | collective-permute-start | bytes 221192 | tf_op jit(solution)/shard_map/ppermute | solution.py:220
  30.5 11.1 %collective-permute-start.14 = (bf16[384,384]{1,0:T(8,128)(2,1)S(1)}, bf16[384,384]{1,0:T(8,128)(2,1)S(1)}, u32[]{:S(2)}, u32[]{:S(2)}) collective-permute-start(bf16[384,384]{1,0:T(8,128)(2,1)S(1)} %bitcast.4), channel_id=1, source_target_pairs={{0,1},{1,0},{2,3},{3,2},{4,5},{5,4},{6,7},{7,6},{8,9},{9,8},{10,11... | collective-permute-start | bytes 884744 | tf_op jit(solution)/shard_map/ppermute | solution.py:227
  32.7 8.9 %collective-permute-start.19 = (bf16[2,192,384]{2,1,0:T(8,128)(2,1)S(1)}, bf16[2,192,384]{2,1,0:T(8,128)(2,1)S(1)}, u32[]{:S(2)}, u32[]{:S(2)}) collective-permute-start(bf16[2,192,384]{2,1,0:T(8,128)(2,1)S(1)} %shard_map.50.refs_1_), channel_id=1, source_target_pairs={{1,2},{2,1},{5,6},{6,5},{9,10},{10,9},{13,14},{14,13},{17,18},{18,... | collective-permute-start | bytes 884744 | tf_op jit(solution)/shard_map/ppermute | solution.py:227
  33.4 13.4 %collective-permute-start.17 = (bf16[2,192,384]{2,1,0:T(8,128)(2,1)S(1)}, bf16[2,192,384]{2,1,0:T(8,128)(2,1)S(1)}, u32[]{:S(2)}, u32[]{:S(2)}) collective-permute-start(bf16[2,192,384]{2,1,0:T(8,128)(2,1)S(1)} %shard_map.50.refs_1_), channel_id=1, source_target_pairs={{0,1},{1,0},{2,3},{3,2},{4,5},{5,4},{6,7},{7,6},{8,9},{9,8},{10,11... | collective-permute-start | bytes 884744 | tf_op jit(solution)/shard_map/ppermute | solution.py:227
  37.9 8.9 %collective-permute-start.18 = (bf16[2,192,384]{2,1,0:T(8,128)(2,1)S(1)}, bf16[2,192,384]{2,1,0:T(8,128)(2,1)S(1)}, u32[]{:S(2)}, u32[]{:S(2)}) collective-permute-start(bf16[2,192,384]{2,1,0:T(8,128)(2,1)S(1)} %shard_map.49.refs_0_), channel_id=1, source_target_pairs={{1,2},{2,1},{5,6},{6,5},{9,10},{10,9},{13,14},{14,13},{17,18},{18,... | collective-permute-start | bytes 884744 | tf_op jit(solution)/shard_map/ppermute | solution.py:227
  38.6 13.6 %collective-permute-start.16 = (bf16[2,192,384]{2,1,0:T(8,128)(2,1)S(1)}, bf16[2,192,384]{2,1,0:T(8,128)(2,1)S(1)}, u32[]{:S(2)}, u32[]{:S(2)}) collective-permute-start(bf16[2,192,384]{2,1,0:T(8,128)(2,1)S(1)} %shard_map.49.refs_0_), channel_id=1, source_target_pairs={{0,1},{1,0},{2,3},{3,2},{4,5},{5,4},{6,7},{7,6},{8,9},{9,8},{10,11... | collective-permute-start | bytes 884744 | tf_op jit(solution)/shard_map/ppermute | solution.py:227
  54.2 4.4 %collective-permute-start.20 = (bf16[2,48,384]{2,1,0:T(8,128)(2,1)S(1)}, bf16[2,48,384]{2,1,0:T(8,128)(2,1)S(1)}, u32[]{:S(2)}, u32[]{:S(2)}) collective-permute-start(bf16[2,48,384]{2,1,0:T(8,128)(2,1)S(1)} %get-tuple-element.47), channel_id=1, source_target_pairs={{0,4},{4,0},{8,12},{12,8},{16,20},{20,16},{24,28},{28,24},{1,5},{5... | collective-permute-start | bytes 221192 | tf_op jit(solution)/shard_map/ppermute | solution.py:220
  54.3 7.0 %collective-permute-start.21 = (bf16[2,48,384]{2,1,0:T(8,128)(2,1)S(1)}, bf16[2,48,384]{2,1,0:T(8,128)(2,1)S(1)}, u32[]{:S(2)}, u32[]{:S(2)}) collective-permute-start(bf16[2,48,384]{2,1,0:T(8,128)(2,1)S(1)} %get-tuple-element.48), channel_id=1, source_target_pairs={{0,8},{4,12},{8,0},{12,4},{16,24},{20,28},{24,16},{28,20},{1,9},{5... | collective-permute-start | bytes 221192 | tf_op jit(solution)/shard_map/ppermute | solution.py:220
  56.4 5.2 %collective-permute-start.22 = (bf16[2,48,384]{2,1,0:T(8,128)(2,1)S(1)}, bf16[2,48,384]{2,1,0:T(8,128)(2,1)S(1)}, u32[]{:S(2)}, u32[]{:S(2)}) collective-permute-start(bf16[2,48,384]{2,1,0:T(8,128)(2,1)S(1)} %get-tuple-element.49), channel_id=1, source_target_pairs={{0,12},{4,8},{8,4},{12,0},{16,28},{20,24},{24,20},{28,16},{1,13},{... | collective-permute-start | bytes 221192 | tf_op jit(solution)/shard_map/ppermute | solution.py:220
  56.4 5.2 %collective-permute-start.23 = (bf16[2,48,384]{2,1,0:T(8,128)(2,1)S(1)}, bf16[2,48,384]{2,1,0:T(8,128)(2,1)S(1)}, u32[]{:S(2)}, u32[]{:S(2)}) collective-permute-start(bf16[2,48,384]{2,1,0:T(8,128)(2,1)S(1)} %get-tuple-element.50), channel_id=1, source_target_pairs={{0,16},{4,20},{8,24},{12,28},{16,0},{20,4},{24,8},{28,12},{1,17},{... | collective-permute-start | bytes 221192 | tf_op jit(solution)/shard_map/ppermute | solution.py:220
  58.7 6.8 %collective-permute-start.24 = (bf16[2,48,384]{2,1,0:T(8,128)(2,1)S(1)}, bf16[2,48,384]{2,1,0:T(8,128)(2,1)S(1)}, u32[]{:S(2)}, u32[]{:S(2)}) collective-permute-start(bf16[2,48,384]{2,1,0:T(8,128)(2,1)S(1)} %get-tuple-element.51), channel_id=1, source_target_pairs={{0,20},{4,16},{8,28},{12,24},{16,4},{20,0},{24,12},{28,8},{1,21},{... | collective-permute-start | bytes 221192 | tf_op jit(solution)/shard_map/ppermute | solution.py:220
  58.7 6.8 %collective-permute-start.25 = (bf16[2,48,384]{2,1,0:T(8,128)(2,1)S(1)}, bf16[2,48,384]{2,1,0:T(8,128)(2,1)S(1)}, u32[]{:S(2)}, u32[]{:S(2)}) collective-permute-start(bf16[2,48,384]{2,1,0:T(8,128)(2,1)S(1)} %get-tuple-element.52), channel_id=1, source_target_pairs={{0,24},{4,28},{8,16},{12,20},{16,8},{20,12},{24,0},{28,4},{1,25},{... | collective-permute-start | bytes 221192 | tf_op jit(solution)/shard_map/ppermute | solution.py:220
  61.3 5.1 %collective-permute-start.26 = (bf16[2,48,384]{2,1,0:T(8,128)(2,1)S(1)}, bf16[2,48,384]{2,1,0:T(8,128)(2,1)S(1)}, u32[]{:S(2)}, u32[]{:S(2)}) collective-permute-start(bf16[2,48,384]{2,1,0:T(8,128)(2,1)S(1)} %get-tuple-element.53), channel_id=1, source_target_pairs={{0,28},{4,24},{8,20},{12,16},{16,12},{20,8},{24,4},{28,0},{1,29},{... | collective-permute-start | bytes 221192 | tf_op jit(solution)/shard_map/ppermute | solution.py:220

commit v2 on v1

--- a/solution.py
+++ b/solution.py
@@ -14,7 +14,7 @@
 LANES = 128
 SUBLANES = 16
 PAIRED = 16
-VMEM_LIMIT = 16 * 2**20
+VMEM_LIMIT = 20 * 2**20
 
 
 def vmem():
@@ -29,18 +29,22 @@
     return 8 if rows % 8 == 0 else rows
 
 
-def for_tiles(rows, cols, body):
+def for_tiles(rows, cols, body, start=0):
     height = row_tile(rows)
     down = rows // height
     across = cols // LANES
 
     def step(index, carry):
-        row = pl.multiple_of((index // across) * height, height)
+        row = pl.multiple_of(start + (index // across) * height, height)
         col = pl.multiple_of((index % across) * LANES, LANES)
         body((pl.ds(row, height), pl.ds(col, LANES)))
         return carry
 
-    lax.fori_loop(0, down * across, step, 0)
+    lax.fori_loop(0, down * across, step, 0, unroll=2)
+
+
+def sum_of(terms):
+    return functools.reduce(lambda x, y: x + y, terms)
 
 
 def cut_kernel(order, partners, green, *refs):
@@ -74,16 +78,16 @@
         low_im = [lesser[(1, g) + tile] for g in range(energies)]
         high_re = [greater[(0, g) + tile] for g in range(energies)]
         high_im = [greater[(1, g) + tile] for g in range(energies)]
+        low_sum = [a + b for a, b in zip(low_re, low_im)]
+        high_sum = [c + d for c, d in zip(high_re, high_im)]
+        high_gap = [c - d for c, d in zip(high_re, high_im)]
         for w in range(energies):
-            real = imag = None
-            for g in range(energies - w):
-                a, b, c, d = low_re[g + w], low_im[g + w], high_re[g], high_im[g]
-                one = b * c - a * d
-                two = a * c + b * d
-                real = one if real is None else real + one
-                imag = two if imag is None else imag + two
-            polar[(w, 0) + tile] = real * scaling
-            polar[(w, 1) + tile] = imag * -scaling
+            shifted = range(energies - w)
+            one = sum_of(high_re[g] * low_sum[g + w] for g in shifted)
+            two = sum_of(low_re[g + w] * high_sum[g] for g in shifted)
+            three = sum_of(low_im[g + w] * high_gap[g] for g in shifted)
+            polar[(w, 0) + tile] = (one - two) * scaling
+            polar[(w, 1) + tile] = (one - three) * -scaling
 
     for_tiles(rows, cols, body)
     for j in range(count):
@@ -91,10 +95,10 @@
 
 
 def sigma_kernel(order, scaling, *refs):
-    count = len(refs) - 5
+    count = len(refs) - 7
     slot_ref = refs[0]
     pieces = refs[1 : 1 + count]
-    lesser, out, weight, total = refs[1 + count :]
+    lesser, out, weight, total, stage, sems = refs[1 + count :]
     energies, rows, cols = lesser.shape[1:]
     for j in range(count):
         weight[order(j)] = pieces[j][...].astype(F32)
@@ -104,21 +108,28 @@
         low_im = [lesser[(1, g) + tile] for g in range(energies)]
         w_re = [weight[(w, 0) + tile] for w in range(energies)]
         w_im = [weight[(w, 1) + tile] for w in range(energies)]
+        low_sum = [a + b for a, b in zip(low_re, low_im)]
+        w_sum = [c + d for c, d in zip(w_re, w_im)]
+        w_gap = [d - c for c, d in zip(w_re, w_im)]
         for e in range(energies):
-            real = imag = None
-            for w in range(e + 1):
-                a, b, c, d = low_re[e - w], low_im[e - w], w_re[w], w_im[w]
-                one = a * d + b * c
-                two = a * c - b * d
-                real = one if real is None else real + one
-                imag = two if imag is None else imag + two
-            total[(0, e) + tile] = real * -scaling
-            total[(1, e) + tile] = imag * scaling
-
-    for_tiles(rows, cols, body)
-    for s in range(energies):
-        for part in range(2):
-            out[part, s, 0] = total[part, slot_ref[s]].astype(BF16)
+            one = sum_of(w_re[w] * low_sum[e - w] for w in range(e + 1))
+            two = sum_of(low_re[e - w] * w_gap[w] for w in range(e + 1))
+            three = sum_of(low_im[e - w] * w_sum[w] for w in range(e + 1))
+            total[(0, e) + tile] = (one + two) * -scaling
+            total[(1, e) + tile] = (one - three) * scaling
+
+    copies = []
+    height = SUBLANES
+    for chunk in range(rows // height):
+        at = pl.ds(chunk * height, height)
+        for_tiles(height, cols, body, chunk * height)
+        for s in range(energies):
+            for part in range(2):
+                stage[part, s, at] = total[part, slot_ref[s], at].astype(BF16)
+        copies.append(pltpu.make_async_copy(stage.at[:, :, at], out.at[:, :, 0, at], sems.at[chunk]))
+        copies[-1].start()
+    for copy in copies:
+        copy.wait()
 
 
 def dot(a, b, dims):
@@ -127,7 +138,6 @@
 
 NN = ((1,), (0,))
 NT = ((1,), (1,))
-TN = ((0,), (0,))
 
 
 def gather_kernel(order, *refs):
@@ -156,30 +166,52 @@
         out[part] = dot(left, vd[...], NT)
 
 
-def screen_kernel(order, count, vl, own, *refs):
-    vu = refs[0:2]
-    polar = refs[2 : 2 + count], refs[2 + count : 2 + 2 * count]
-    outs, whole, total = refs[2 + 2 * count : -2], refs[-2], refs[-1]
-    for pair in range(2):
-        join(order, polar[pair], whole.at[pair])
+def couple_kernel(order, vl, up_even, up_odd, right, left_near, left_far):
+    size = vl.shape[0]
+    height = size // 2
     even = lax.axis_index("space") % 2 == 0
 
-    def screen(upper, below, above):
-        for part in range(2):
-            left = dot(vl[...], below[part], NN).astype(BF16)
-            lower = dot(left, vl[...], NT)
-            left = dot(upper[...], above[part], TN).astype(BF16)
-            raised = dot(left, upper[...], NN).astype(BF16).astype(F32)
-            total[part] = (own[part] + lower + raised).astype(BF16)
+    def fill(first, second):
+        right[pl.ds(0, size)] = first
+        right[pl.ds(size, size)] = second
 
     @pl.when(even)
     def _():
-        screen(vu[0], whole.at[1], whole.at[0])
+        fill(up_even[...], vl[...].T)
 
     @pl.when(jnp.logical_not(even))
     def _():
-        screen(vu[1], whole.at[0], whole.at[1])
-
+        fill(vl[...].T, up_odd[...])
+
+    mine = order(0) // (lax.axis_size("energy") // 2)
+    for pair in range(2):
+        for j, left in enumerate((left_near, left_far)):
+            at = pl.multiple_of(pair * size + (mine ^ j) * height, height)
+            left[pair] = right[pl.ds(at, height)].T
+
+
+def abreast(parts, wide):
+    cols = parts.shape[2]
+    for part in range(2):
+        wide[:, part * cols : (part + 1) * cols] = parts[part]
+
+
+def near_kernel(left, even, odd, out, wide):
+    for pair, met in enumerate((even, odd)):
+        abreast(met, wide)
+        out[pair] = dot(left[pair], wide[...], NN)
+
+
+def screen_kernel(order, right, left, begun, own, even, odd, *refs):
+    outs, wide, product, total = refs[:-3], *refs[-3:]
+    size, cols = total.shape[1:]
+    for pair, met in enumerate((even, odd)):
+        abreast(met, wide)
+        both = (begun[pair] + dot(left[pair], wide[...], NN)).astype(BF16)
+        for part in range(2):
+            product[part * size : (part + 1) * size, pair * size : (pair + 1) * size] = both[:, part * cols : (part + 1) * cols]
+    for part in range(2):
+        total[part] = (own[part] + dot(product[part * size : (part + 1) * size], right[...], NN)).astype(BF16)
     rows = outs[0].shape[1]
     for j, out in enumerate(outs):
         at = pl.multiple_of(order(j) * rows, rows)
@@ -268,21 +300,42 @@
         scratch=[pltpu.VMEM(whole.shape, BF16)],
         flops=2 * work,
     )[0]
+    left = struct((2, block, block // 2))
+    right, left_near, left_far = call(
+        functools.partial(couple_kernel, order),
+        [struct((2 * block, block)), left, left],
+        [v_low[0], *upper],
+    )
+    wide = pltpu.VMEM((block // 2, 2 * cols), BF16)
+    begun = call(
+        near_kernel,
+        [struct((2, block, 2 * cols), F32)],
+        [left_near, halves[0][0], halves[1][0]],
+        scratch=[wide],
+        flops=work,
+    )[0]
     screened_out = call(
-        functools.partial(screen_kernel, order, 2),
+        functools.partial(screen_kernel, order),
         [piece] * parts,
-        [v_low[0], own, *upper, *halves[0], *halves[1]],
-        scratch=[pltpu.VMEM((2, *whole.shape), BF16), pltpu.VMEM(whole.shape, BF16)],
-        flops=4 * work,
+        [right, left_far, begun, own, halves[0][1], halves[1][1]],
+        scratch=[wide, pltpu.VMEM((2 * block, 2 * block), BF16), pltpu.VMEM(whole.shape, BF16)],
+        flops=3 * work,
     )
     screened_in = swap(screened_out, range(1, parts))
-    return call(
+    return pl.pallas_call(
         functools.partial(sigma_kernel, order, scaling),
-        [struct((2, energies, 1, rows, cols))],
-        [energy_slot] + screened_in + [lesser],
-        tables=1,
-        scratch=[pltpu.VMEM((energies, 2, rows, cols), F32), pltpu.VMEM((2, energies, rows, cols), F32)],
-    )[0]
+        name="sigma",
+        out_shape=struct((2, energies, 1, rows, cols)),
+        in_specs=[smem()] + [vmem()] * (parts + 1),
+        out_specs=pl.BlockSpec(memory_space=pltpu.HBM),
+        scratch_shapes=[
+            pltpu.VMEM((energies, 2, rows, cols), F32),
+            pltpu.VMEM((2, energies, rows, cols), F32),
+            pltpu.VMEM((2, energies, rows, cols), BF16),
+            pltpu.SemaphoreType.DMA((rows // SUBLANES,)),
+        ],
+        compiler_params=pltpu.CompilerParams(vmem_limit_bytes=VMEM_LIMIT),
+    )(energy_slot, *screened_in, lesser)
 
 
 def shifted(value, axis, steps):

time: 69.2 us -> 67 us (0.968)
  the two profiles are of different devices: /device:TPU:0 before, /device:TPU:11 now
where the time goes in v2:
time: 67 us; the launch traced here: 66.8 us
  starting transfers between devices  30.1 us (45%)
  waiting for transfers between devices  27.3 us (41%)
  Pallas kernels  9.29 us (14%)
    ppermute x21, starting transfers between devices, swap(): lax.ppermute(pieces[j], 'energy', [(i, i ^ j) for i in range(parts)])  21.3 us
    ppermute x21, waiting for transfers between devices, swap(): lax.ppermute(pieces[j], 'energy', [(i, i ^ j) for i in range(parts)])  14.5 us
    ppermute x6, waiting for transfers between devices, meet(): lax.ppermute(value, 'space', [p for i in lows for p in ((i, i + 1), (i +...  12.7 us
    ppermute x6, starting transfers between devices, meet(): lax.ppermute(value, 'space', [p for i in lows for p in ((i, i + 1), (i +...  8.81 us
    pallas_call x7, Pallas kernels, call(): pl.pallas_call(kernel, out_shape=outs, in_specs=[smem()] * tables + [vmem...  4.8 us
    pallas_call x2, Pallas kernels, take(): pl.pallas_call(functools.partial(cut_kernel, order, partners), out_shape=...  2.33 us
    pallas_call x1, Pallas kernels, direct(): pl.pallas_call(functools.partial(sigma_kernel, order, scaling), name='sig...  2.17 us
  transfers between devices with their start and end apart: 27, of which 9 were waited for; matrix products, arithmetic and copies ran while one was open for 0% of the time, Pallas kernels for 7%

profile of v2, /device:TPU:11, one launch (start us, length us, event | category | flops | bytes accessed | tf_op | source)
XLA Modules:
  0.0 66.8 jit_solution(7395029469155206651)
XLA Ops:
  0.0 1.3 %shard_map.47 = (bf16[4,48,384]{2,1,0:T(8,128)(2,1)S(1)}, bf16[4,48,384]{2,1,0:T(8,128)(2,1)S(1)}, bf16[4,48,384]{2,1,0:T(8,128)(2,1)S(1)}, bf16[4,48,384]{2,1,0...) custom-call(bf16[4,1,1,384,384]{4,3,2,1,0:T(8,128)(2,1)} %green.3), custom_call_target="tpu_custom_call" | custom-call | tf_op jit(solution)/shard_map/pallas_call | solution.py:263
  1.3 0.7 %collective-permute-start.2 = (bf16[4,48,384]{2,1,0:T(8,128)(2,1)S(1)}, bf16[4,48,384]{2,1,0:T(8,128)(2,1)S(1)}, u32[]{:S(2)}, u32[]{:S(2)}) collective-permute-start(bf16[4,48,384]{2,1,0:T(8,128)(2,1)S(1)} %get-tuple-element.37), channel_id=1, source_target_pairs={{0,4},{4,0},{8,12},{12,8},{16,20},{20,16},{24,28},{28,24},{1,5},{5... | collective-permute-start | bytes 442376 | tf_op jit(solution)/shard_map/ppermute | solution.py:252
  2.1 0.3 collective-permute-start.3
  2.3 1.5 %collective-permute-start.4 = (bf16[4,48,384]{2,1,0:T(8,128)(2,1)S(1)}, bf16[4,48,384]{2,1,0:T(8,128)(2,1)S(1)}, u32[]{:S(2)}, u32[]{:S(2)}) collective-permute-start(bf16[4,48,384]{2,1,0:T(8,128)(2,1)S(1)} %get-tuple-element.39), channel_id=1, source_target_pairs={{0,12},{4,8},{8,4},{12,0},{16,28},{20,24},{24,20},{28,16},{1,13},{... | collective-permute-start | bytes 442376 | tf_op jit(solution)/shard_map/ppermute | solution.py:252
  3.8 1.2 %collective-permute-start.5 = (bf16[4,48,384]{2,1,0:T(8,128)(2,1)S(1)}, bf16[4,48,384]{2,1,0:T(8,128)(2,1)S(1)}, u32[]{:S(2)}, u32[]{:S(2)}) collective-permute-start(bf16[4,48,384]{2,1,0:T(8,128)(2,1)S(1)} %get-tuple-element.40), channel_id=1, source_target_pairs={{0,16},{4,20},{8,24},{12,28},{16,0},{20,4},{24,8},{28,12},{1,17},{... | collective-permute-start | bytes 442376 | tf_op jit(solution)/shard_map/ppermute | solution.py:252
  5.0 0.5 collective-permute-start.6
  5.6 1.0 %shard_map.48 = (bf16[4,48,384]{2,1,0:T(8,128)(2,1)S(1)}, bf16[4,48,384]{2,1,0:T(8,128)(2,1)S(1)}) custom-call(bf16[4,1,1,384,384]{4,3,2,1,0:T(8,128)(2,1)} %green.3), custom_call_target="tpu_custom_call" | custom-call | tf_op jit(solution)/shard_map/pallas_call | solution.py:263
  6.6 0.0 collective-permute-done.2.refs_2_
  6.6 1.3 %collective-permute-start.7 = (bf16[4,48,384]{2,1,0:T(8,128)(2,1)S(1)}, bf16[4,48,384]{2,1,0:T(8,128)(2,1)S(1)}, u32[]{:S(2)}, u32[]{:S(2)}) collective-permute-start(bf16[4,48,384]{2,1,0:T(8,128)(2,1)S(1)} %get-tuple-element.42), channel_id=1, source_target_pairs={{0,24},{4,28},{8,16},{12,20},{16,8},{20,12},{24,0},{28,4},{1,25},{... | collective-permute-start | bytes 442376 | tf_op jit(solution)/shard_map/ppermute | solution.py:252
  7.9 0.0 collective-permute-done.3.refs_3_
  7.9 2.1 %collective-permute-start.8 = (bf16[4,48,384]{2,1,0:T(8,128)(2,1)S(1)}, bf16[4,48,384]{2,1,0:T(8,128)(2,1)S(1)}, u32[]{:S(2)}, u32[]{:S(2)}) collective-permute-start(bf16[4,48,384]{2,1,0:T(8,128)(2,1)S(1)} %get-tuple-element.43), channel_id=1, source_target_pairs={{0,28},{4,24},{8,20},{12,16},{16,12},{20,8},{24,4},{28,0},{1,29},{... | collective-permute-start | bytes 442376 | tf_op jit(solution)/shard_map/ppermute | solution.py:252
  10.0 1.7 %collective-permute-done.4.refs_4_ = bf16[4,48,384]{2,1,0:T(8,128)(2,1)S(1)} collective-permute-done((bf16[4,48,384]{2,1,0:T(8,128)(2,1)S(1)}, bf16[4,48,384]{2,1,0:T(8,128)(2,1)S(1)}, u32[]{:S(2)}, u32[]{:S(2)}) %collective-permute-start.4) | collective-permute-done | bytes 147488 | tf_op jit(solution)/shard_map/ppermute | solution.py:252
  11.7 0.0 copy-done
  11.7 0.2 collective-permute-start
  11.8 0.0 collective-permute-done.5.refs_5_
  11.8 7.3 %collective-permute-done.6.refs_6_ = bf16[4,48,384]{2,1,0:T(8,128)(2,1)S(1)} collective-permute-done((bf16[4,48,384]{2,1,0:T(8,128)(2,1)S(1)}, bf16[4,48,384]{2,1,0:T(8,128)(2,1)S(1)}, u32[]{:S(2)}, u32[]{:S(2)}) %collective-permute-start.6) | collective-permute-done | bytes 147488 | tf_op jit(solution)/shard_map/ppermute | solution.py:252
  19.1 0.0 collective-permute-done.7.refs_7_
  19.1 0.0 collective-permute-done.8.refs_8_
  19.2 0.0 copy-start.1
  19.2 1.6 %shard_map.49 = (bf16[2,48,384]{2,1,0:T(8,128)(2,1)S(1)}, bf16[2,48,384]{2,1,0:T(8,128)(2,1)S(1)}, bf16[2,48,384]{2,1,0:T(8,128)(2,1)S(1)}, bf16[2,48,384]{2,1,0...) custom-call(s32[8]{0:T(128)S(1)} %copy-done.2, ...), custom_call_target="tpu_custom_call" | custom-call | bytes 2949152 | tf_op jit(solution)/shard_map/pallas_call | solution.py:224
  20.7 0.1 collective-permute-start.9
  20.8 0.3 collective-permute-start.10
  21.1 1.8 %collective-permute-start.11 = (bf16[2,48,384]{2,1,0:T(8,128)(2,1)S(1)}, bf16[2,48,384]{2,1,0:T(8,128)(2,1)S(1)}, u32[]{:S(2)}, u32[]{:S(2)}) collective-permute-start(bf16[2,48,384]{2,1,0:T(8,128)(2,1)S(1)} %get-tuple-element.47), channel_id=1, source_target_pairs={{0,12},{4,8},{8,4},{12,0},{16,28},{20,24},{24,20},{28,16},{1,13},{... | collective-permute-start | bytes 221192 | tf_op jit(solution)/shard_map/ppermute | solution.py:252
  22.9 1.2 %collective-permute-start.14 = (bf16[2,48,384]{2,1,0:T(8,128)(2,1)S(1)}, bf16[2,48,384]{2,1,0:T(8,128)(2,1)S(1)}, u32[]{:S(2)}, u32[]{:S(2)}) collective-permute-start(bf16[2,48,384]{2,1,0:T(8,128)(2,1)S(1)} %get-tuple-element.48), channel_id=1, source_target_pairs={{0,16},{4,20},{8,24},{12,28},{16,0},{20,4},{24,8},{28,12},{1,17},{... | collective-permute-start | bytes 221192 | tf_op jit(solution)/shard_map/ppermute | solution.py:252
  24.2 0.0 collective-permute-done.9.refs_1_
  24.2 0.2 collective-permute-start.15
  24.4 0.0 collective-permute-done.10.refs_2_
  24.4 1.3 %collective-permute-start.16 = (bf16[2,48,384]{2,1,0:T(8,128)(2,1)S(1)}, bf16[2,48,384]{2,1,0:T(8,128)(2,1)S(1)}, u32[]{:S(2)}, u32[]{:S(2)}) collective-permute-start(bf16[2,48,384]{2,1,0:T(8,128)(2,1)S(1)} %get-tuple-element.50), channel_id=1, source_target_pairs={{0,24},{4,28},{8,16},{12,20},{16,8},{20,12},{24,0},{28,4},{1,25},{... | collective-permute-start | bytes 221192 | tf_op jit(solution)/shard_map/ppermute | solution.py:252
  25.7 1.2 %collective-permute-done.11.refs_3_ = bf16[2,48,384]{2,1,0:T(8,128)(2,1)S(1)} collective-permute-done((bf16[2,48,384]{2,1,0:T(8,128)(2,1)S(1)}, bf16[2,48,384]{2,1,0:T(8,128)(2,1)S(1)}, u32[]{:S(2)}, u32[]{:S(2)}) %collective-permute-start.11) | collective-permute-done | bytes 73760 | tf_op jit(solution)/shard_map/ppermute | solution.py:252
  26.8 2.1 %collective-permute-start.17 = (bf16[2,48,384]{2,1,0:T(8,128)(2,1)S(1)}, bf16[2,48,384]{2,1,0:T(8,128)(2,1)S(1)}, u32[]{:S(2)}, u32[]{:S(2)}) collective-permute-start(bf16[2,48,384]{2,1,0:T(8,128)(2,1)S(1)} %get-tuple-element.51), channel_id=1, source_target_pairs={{0,28},{4,24},{8,20},{12,16},{16,12},{20,8},{24,4},{28,0},{1,29},{... | collective-permute-start | bytes 221192 | tf_op jit(solution)/shard_map/ppermute | solution.py:252
  29.0 0.0 collective-permute-done.14.refs_0_
  29.0 3.2 %collective-permute-start.1 = (bf16[384,384]{1,0:T(8,128)(2,1)S(1)}, bf16[384,384]{1,0:T(8,128)(2,1)S(1)}, u32[]{:S(2)}, u32[]{:S(2)}) collective-permute-start(bf16[384,384]{1,0:T(8,128)(2,1)S(1)} %bitcast.3), channel_id=1, source_target_pairs={{1,2},{2,1},{5,6},{6,5},{9,10},{10,9},{13,14},{14,13},{17,18},{18,... | collective-permute-start | bytes 884744 | tf_op jit(solution)/shard_map/ppermute | solution.py:259
  32.2 0.0 collective-permute-done.15.refs_1_
  32.2 0.1 collective-permute-start.12
  32.3 0.0 collective-permute-done.16.refs_2_
  32.3 2.1 %collective-permute-start.13 = (bf16[2,192,384]{2,1,0:T(8,128)(2,1)S(1)}, bf16[2,192,384]{2,1,0:T(8,128)(2,1)S(1)}, u32[]{:S(2)}, u32[]{:S(2)}) collective-permute-start(bf16[2,192,384]{2,1,0:T(8,128)(2,1)S(1)} %shard_map.50.refs_0_), channel_id=1, source_target_pairs={{1,2},{2,1},{5,6},{6,5},{9,10},{10,9},{13,14},{14,13},{17,18},{18,... | collective-permute-start | bytes 884744 | tf_op jit(solution)/shard_map/ppermute | solution.py:259
  34.4 0.0 collective-permute-done.17.refs_3_
  34.5 0.1 collective-permute-start.18
  34.6 0.0 collective-permute-done.up_even
  34.6 3.2 %collective-permute-start.19 = (bf16[2,192,384]{2,1,0:T(8,128)(2,1)S(1)}, bf16[2,192,384]{2,1,0:T(8,128)(2,1)S(1)}, u32[]{:S(2)}, u32[]{:S(2)}) collective-permute-start(bf16[2,192,384]{2,1,0:T(8,128)(2,1)S(1)} %shard_map.52.refs_1_), channel_id=1, source_target_pairs={{1,2},{2,1},{5,6},{6,5},{9,10},{10,9},{13,14},{14,13},{17,18},{18,... | collective-permute-start | bytes 884744 | tf_op jit(solution)/shard_map/ppermute | solution.py:259
  37.8 1.1 %shard_map.53.own = f32[2,384,384]{2,1,0:T(8,128)S(1)} custom-call(bf16[384,384]{1,0:T(8,128)(2,1)S(1)} %bitcast.5, bf16[2,192,384]{2,1,0:T(8,128)(2,1)S(1)} %shard_map.50.refs_0_, bf16[2,192,384]{2,1,0:T(8,128)(2,1)S(1)} %shard_map.52.refs_1_), custom_call_target="tpu_custom_call" | custom-call | flops 452984832 | bytes 2064384 | tf_op jit(solution)/shard_map/pallas_call | solution.py:224
  38.9 1.0 %collective-permute-done.1.up_odd = bf16[384,384]{1,0:T(8,128)(2,1)S(1)} collective-permute-done((bf16[384,384]{1,0:T(8,128)(2,1)S(1)}, bf16[384,384]{1,0:T(8,128)(2,1)S(1)}, u32[]{:S(2)}, u32[]{:S(2)}) %collective-permute-start.1) | collective-permute-done | bytes 294944 | tf_op jit(solution)/shard_map/ppermute | solution.py:259
  39.9 0.4 shard_map.46
  40.3 0.7 %collective-permute-done.12.even = bf16[2,192,384]{2,1,0:T(8,128)(2,1)S(1)} collective-permute-done((bf16[2,192,384]{2,1,0:T(8,128)(2,1)S(1)}, bf16[2,192,384]{2,1,0:T(8,128)(2,1)S(1)}, u32[]{:S(2)}, u32[]{:S(2)}) %collective-permute-start.12) | collective-permute-done | bytes 294944 | tf_op jit(solution)/shard_map/ppermute | solution.py:259
  41.0 5.2 %collective-permute-done.13.odd = bf16[2,192,384]{2,1,0:T(8,128)(2,1)S(1)} collective-permute-done((bf16[2,192,384]{2,1,0:T(8,128)(2,1)S(1)}, bf16[2,192,384]{2,1,0:T(8,128)(2,1)S(1)}, u32[]{:S(2)}, u32[]{:S(2)}) %collective-permute-start.13) | collective-permute-done | bytes 294944 | tf_op jit(solution)/shard_map/ppermute | solution.py:259
  46.2 0.5 shard_map.51.begun
  46.7 0.6 collective-permute-done.18.even
  47.3 5.2 %collective-permute-done.19.odd = bf16[2,192,384]{2,1,0:T(8,128)(2,1)S(1)} collective-permute-done((bf16[2,192,384]{2,1,0:T(8,128)(2,1)S(1)}, bf16[2,192,384]{2,1,0:T(8,128)(2,1)S(1)}, u32[]{:S(2)}, u32[]{:S(2)}) %collective-permute-start.19) | collective-permute-done | bytes 294944 | tf_op jit(solution)/shard_map/ppermute | solution.py:259
  52.5 1.2 %shard_map.54 = (bf16[2,48,384]{2,1,0:T(8,128)(2,1)S(1)}, bf16[2,48,384]{2,1,0:T(8,128)(2,1)S(1)}, bf16[2,48,384]{2,1,0:T(8,128)(2,1)S(1)}, bf16[2,48,384]{2,1,0...) custom-call(bf16[768,384]{1,0:T(8,128)(2,1)S(1)} %get-tuple-element., ...), custom_call_target="tpu_custom_call" | custom-call | flops 679477248 | bytes 5603328 | tf_op jit(solution)/shard_map/pallas_call | solution.py:224
  53.7 0.5 collective-permute-start.20
  54.2 0.0 collective-permute-start.21
  54.2 1.7 %collective-permute-start.22 = (bf16[2,48,384]{2,1,0:T(8,128)(2,1)S(1)}, bf16[2,48,384]{2,1,0:T(8,128)(2,1)S(1)}, u32[]{:S(2)}, u32[]{:S(2)}) collective-permute-start(bf16[2,48,384]{2,1,0:T(8,128)(2,1)S(1)} %get-tuple-element.55), channel_id=1, source_target_pairs={{0,12},{4,8},{8,4},{12,0},{16,28},{20,24},{24,20},{28,16},{1,13},{... | collective-permute-start | bytes 221192 | tf_op jit(solution)/shard_map/ppermute | solution.py:252
  55.9 0.3 collective-permute-start.23
  56.2 1.5 %collective-permute-start.24 = (bf16[2,48,384]{2,1,0:T(8,128)(2,1)S(1)}, bf16[2,48,384]{2,1,0:T(8,128)(2,1)S(1)}, u32[]{:S(2)}, u32[]{:S(2)}) collective-permute-start(bf16[2,48,384]{2,1,0:T(8,128)(2,1)S(1)} %get-tuple-element.57), channel_id=1, source_target_pairs={{0,20},{4,16},{8,28},{12,24},{16,4},{20,0},{24,12},{28,8},{1,21},{... | collective-permute-start | bytes 221192 | tf_op jit(solution)/shard_map/ppermute | solution.py:252
  57.7 0.0 collective-permute-done.20.refs_2_
  57.7 0.5 collective-permute-start.25
  58.2 0.0 collective-permute-done.21.refs_3_
  58.2 2.1 %collective-permute-start.26 = (bf16[2,48,384]{2,1,0:T(8,128)(2,1)S(1)}, bf16[2,48,384]{2,1,0:T(8,128)(2,1)S(1)}, u32[]{:S(2)}, u32[]{:S(2)}) collective-permute-start(bf16[2,48,384]{2,1,0:T(8,128)(2,1)S(1)} %get-tuple-element.59), channel_id=1, source_target_pairs={{0,28},{4,24},{8,20},{12,16},{16,12},{20,8},{24,4},{28,0},{1,29},{... | collective-permute-start | bytes 221192 | tf_op jit(solution)/shard_map/ppermute | solution.py:252
  60.3 0.0 collective-permute-done.22.refs_4_
  60.3 0.0 collective-permute-done.23.refs_5_
  60.3 4.3 %collective-permute-done.24.refs_6_ = bf16[2,48,384]{2,1,0:T(8,128)(2,1)S(1)} collective-permute-done((bf16[2,48,384]{2,1,0:T(8,128)(2,1)S(1)}, bf16[2,48,384]{2,1,0:T(8,128)(2,1)S(1)}, u32[]{:S(2)}, u32[]{:S(2)}) %collective-permute-start.24) | collective-permute-done | bytes 73760 | tf_op jit(solution)/shard_map/ppermute | solution.py:252
  64.7 0.0 collective-permute-done.25.refs_7_
  64.7 0.0 collective-permute-done.26.refs_8_
  64.7 2.2 %sigma.1 = bf16[2,8,1,48,384]{4,3,2,1,0:T(8,128)(2,1)} custom-call(s32[8]{0:T(128)S(1)} %copy-done.2, bf16[2,48,384]{2,1,0:T(8,128)(2,1)S(1)} %get-tuple-element.52.refs_1_, bf16[2,48,384]{2,1,0:T(8,128)(2,1)S(1)} %collective-permute-done.20.refs_2_, bf16[2,48,384]{2,1,0:T(8,128)(2,1)S(1)} %collective-permute-done.21.refs_3_, ...), custom_call_target="tpu_custom_call" | custom-call | tf_op jit(solution)/shard_map/sigma/pallas_call | solution.py:325
  (6 shorter events, 0.1 us)
Async XLA Ops:
  0.0 11.7 %copy-start = (bf16[1,384,384]{2,1,0:T(8,128)(2,1)S(1)}, bf16[1,384,384]{2,1,0:T(8,128)(2,1)}, u32[]{:S(2)}) copy-start(bf16[1,384,384]{2,1,0:T(8,128)(2,1)} %param.6) | copy-start | bytes 884740
  0.0 19.2 %copy-start.2 = (s32[8]{0:T(128)S(1)}, s32[8]{0:T(128)}, u32[]{:S(2)}) copy-start(s32[8]{0:T(128)} %refs_0_.3) | copy-start | bytes 100
  1.3 5.2 %collective-permute-start.2 = (bf16[4,48,384]{2,1,0:T(8,128)(2,1)S(1)}, bf16[4,48,384]{2,1,0:T(8,128)(2,1)S(1)}, u32[]{:S(2)}, u32[]{:S(2)}) collective-permute-start(bf16[4,48,384]{2,1,0:T(8,128)(2,1)S(1)} %get-tuple-element.37), channel_id=1, source_target_pairs={{0,4},{4,0},{8,12},{12,8},{16,20},{20,16},{24,28},{28,24},{1,5},{5... | collective-permute-start | bytes 442376 | tf_op jit(solution)/shard_map/ppermute | solution.py:252
  2.1 5.8 %collective-permute-start.3 = (bf16[4,48,384]{2,1,0:T(8,128)(2,1)S(1)}, bf16[4,48,384]{2,1,0:T(8,128)(2,1)S(1)}, u32[]{:S(2)}, u32[]{:S(2)}) collective-permute-start(bf16[4,48,384]{2,1,0:T(8,128)(2,1)S(1)} %get-tuple-element.38), channel_id=1, source_target_pairs={{0,8},{4,12},{8,0},{12,4},{16,24},{20,28},{24,16},{28,20},{1,9},{5... | collective-permute-start | bytes 442376 | tf_op jit(solution)/shard_map/ppermute | solution.py:252
  2.3 9.3 %collective-permute-start.4 = (bf16[4,48,384]{2,1,0:T(8,128)(2,1)S(1)}, bf16[4,48,384]{2,1,0:T(8,128)(2,1)S(1)}, u32[]{:S(2)}, u32[]{:S(2)}) collective-permute-start(bf16[4,48,384]{2,1,0:T(8,128)(2,1)S(1)} %get-tuple-element.39), channel_id=1, source_target_pairs={{0,12},{4,8},{8,4},{12,0},{16,28},{20,24},{24,20},{28,16},{1,13},{... | collective-permute-start | bytes 442376 | tf_op jit(solution)/shard_map/ppermute | solution.py:252
  3.8 8.0 %collective-permute-start.5 = (bf16[4,48,384]{2,1,0:T(8,128)(2,1)S(1)}, bf16[4,48,384]{2,1,0:T(8,128)(2,1)S(1)}, u32[]{:S(2)}, u32[]{:S(2)}) collective-permute-start(bf16[4,48,384]{2,1,0:T(8,128)(2,1)S(1)} %get-tuple-element.40), channel_id=1, source_target_pairs={{0,16},{4,20},{8,24},{12,28},{16,0},{20,4},{24,8},{28,12},{1,17},{... | collective-permute-start | bytes 442376 | tf_op jit(solution)/shard_map/ppermute | solution.py:252
  5.0 14.1 %collective-permute-start.6 = (bf16[4,48,384]{2,1,0:T(8,128)(2,1)S(1)}, bf16[4,48,384]{2,1,0:T(8,128)(2,1)S(1)}, u32[]{:S(2)}, u32[]{:S(2)}) collective-permute-start(bf16[4,48,384]{2,1,0:T(8,128)(2,1)S(1)} %get-tuple-element.41), channel_id=1, source_target_pairs={{0,20},{4,16},{8,28},{12,24},{16,4},{20,0},{24,12},{28,8},{1,21},{... | collective-permute-start | bytes 442376 | tf_op jit(solution)/shard_map/ppermute | solution.py:252
  6.6 12.6 %collective-permute-start.7 = (bf16[4,48,384]{2,1,0:T(8,128)(2,1)S(1)}, bf16[4,48,384]{2,1,0:T(8,128)(2,1)S(1)}, u32[]{:S(2)}, u32[]{:S(2)}) collective-permute-start(bf16[4,48,384]{2,1,0:T(8,128)(2,1)S(1)} %get-tuple-element.42), channel_id=1, source_target_pairs={{0,24},{4,28},{8,16},{12,20},{16,8},{20,12},{24,0},{28,4},{1,25},{... | collective-permute-start | bytes 442376 | tf_op jit(solution)/shard_map/ppermute | solution.py:252
  7.9 11.3 %collective-permute-start.8 = (bf16[4,48,384]{2,1,0:T(8,128)(2,1)S(1)}, bf16[4,48,384]{2,1,0:T(8,128)(2,1)S(1)}, u32[]{:S(2)}, u32[]{:S(2)}) collective-permute-start(bf16[4,48,384]{2,1,0:T(8,128)(2,1)S(1)} %get-tuple-element.43), channel_id=1, source_target_pairs={{0,28},{4,24},{8,20},{12,16},{16,12},{20,8},{24,4},{28,0},{1,29},{... | collective-permute-start | bytes 442376 | tf_op jit(solution)/shard_map/ppermute | solution.py:252
  11.7 22.9 %collective-permute-start = (bf16[384,384]{1,0:T(8,128)(2,1)S(1)}, bf16[384,384]{1,0:T(8,128)(2,1)S(1)}, u32[]{:S(2)}, u32[]{:S(2)}) collective-permute-start(bf16[384,384]{1,0:T(8,128)(2,1)S(1)} %bitcast.2), channel_id=1, source_target_pairs={{0,1},{1,0},{2,3},{3,2},{4,5},{5,4},{6,7},{7,6},{8,9},{9,8},{10,11... | collective-permute-start | bytes 884744 | tf_op jit(solution)/shard_map/ppermute | solution.py:259
  19.2 18.6 %copy-start.1 = (bf16[1,384,384]{2,1,0:T(8,128)(2,1)S(1)}, bf16[1,384,384]{2,1,0:T(8,128)(2,1)}, u32[]{:S(2)}) copy-start(bf16[1,384,384]{2,1,0:T(8,128)(2,1)} %param.5) | copy-start | bytes 884740
  20.7 3.5 %collective-permute-start.9 = (bf16[2,48,384]{2,1,0:T(8,128)(2,1)S(1)}, bf16[2,48,384]{2,1,0:T(8,128)(2,1)S(1)}, u32[]{:S(2)}, u32[]{:S(2)}) collective-permute-start(bf16[2,48,384]{2,1,0:T(8,128)(2,1)S(1)} %get-tuple-element.45), channel_id=1, source_target_pairs={{0,4},{4,0},{8,12},{12,8},{16,20},{20,16},{24,28},{28,24},{1,5},{5... | collective-permute-start | bytes 221192 | tf_op jit(solution)/shard_map/ppermute | solution.py:252
  20.8 3.6 %collective-permute-start.10 = (bf16[2,48,384]{2,1,0:T(8,128)(2,1)S(1)}, bf16[2,48,384]{2,1,0:T(8,128)(2,1)S(1)}, u32[]{:S(2)}, u32[]{:S(2)}) collective-permute-start(bf16[2,48,384]{2,1,0:T(8,128)(2,1)S(1)} %get-tuple-element.46), channel_id=1, source_target_pairs={{0,8},{4,12},{8,0},{12,4},{16,24},{20,28},{24,16},{28,20},{1,9},{5... | collective-permute-start | bytes 221192 | tf_op jit(solution)/shard_map/ppermute | solution.py:252
  21.1 5.7 %collective-permute-start.11 = (bf16[2,48,384]{2,1,0:T(8,128)(2,1)S(1)}, bf16[2,48,384]{2,1,0:T(8,128)(2,1)S(1)}, u32[]{:S(2)}, u32[]{:S(2)}) collective-permute-start(bf16[2,48,384]{2,1,0:T(8,128)(2,1)S(1)} %get-tuple-element.47), channel_id=1, source_target_pairs={{0,12},{4,8},{8,4},{12,0},{16,28},{20,24},{24,20},{28,16},{1,13},{... | collective-permute-start | bytes 221192 | tf_op jit(solution)/shard_map/ppermute | solution.py:252
  22.9 6.1 %collective-permute-start.14 = (bf16[2,48,384]{2,1,0:T(8,128)(2,1)S(1)}, bf16[2,48,384]{2,1,0:T(8,128)(2,1)S(1)}, u32[]{:S(2)}, u32[]{:S(2)}) collective-permute-start(bf16[2,48,384]{2,1,0:T(8,128)(2,1)S(1)} %get-tuple-element.48), channel_id=1, source_target_pairs={{0,16},{4,20},{8,24},{12,28},{16,0},{20,4},{24,8},{28,12},{1,17},{... | collective-permute-start | bytes 221192 | tf_op jit(solution)/shard_map/ppermute | solution.py:252
  24.2 8.0 %collective-permute-start.15 = (bf16[2,48,384]{2,1,0:T(8,128)(2,1)S(1)}, bf16[2,48,384]{2,1,0:T(8,128)(2,1)S(1)}, u32[]{:S(2)}, u32[]{:S(2)}) collective-permute-start(bf16[2,48,384]{2,1,0:T(8,128)(2,1)S(1)} %get-tuple-element.49), channel_id=1, source_target_pairs={{0,20},{4,16},{8,28},{12,24},{16,4},{20,0},{24,12},{28,8},{1,21},{... | collective-permute-start | bytes 221192 | tf_op jit(solution)/shard_map/ppermute | solution.py:252
  24.4 7.9 %collective-permute-start.16 = (bf16[2,48,384]{2,1,0:T(8,128)(2,1)S(1)}, bf16[2,48,384]{2,1,0:T(8,128)(2,1)S(1)}, u32[]{:S(2)}, u32[]{:S(2)}) collective-permute-start(bf16[2,48,384]{2,1,0:T(8,128)(2,1)S(1)} %get-tuple-element.50), channel_id=1, source_target_pairs={{0,24},{4,28},{8,16},{12,20},{16,8},{20,12},{24,0},{28,4},{1,25},{... | collective-permute-start | bytes 221192 | tf_op jit(solution)/shard_map/ppermute | solution.py:252
  26.8 7.6 %collective-permute-start.17 = (bf16[2,48,384]{2,1,0:T(8,128)(2,1)S(1)}, bf16[2,48,384]{2,1,0:T(8,128)(2,1)S(1)}, u32[]{:S(2)}, u32[]{:S(2)}) collective-permute-start(bf16[2,48,384]{2,1,0:T(8,128)(2,1)S(1)} %get-tuple-element.51), channel_id=1, source_target_pairs={{0,28},{4,24},{8,20},{12,16},{16,12},{20,8},{24,4},{28,0},{1,29},{... | collective-permute-start | bytes 221192 | tf_op jit(solution)/shard_map/ppermute | solution.py:252
  29.0 10.9 %collective-permute-start.1 = (bf16[384,384]{1,0:T(8,128)(2,1)S(1)}, bf16[384,384]{1,0:T(8,128)(2,1)S(1)}, u32[]{:S(2)}, u32[]{:S(2)}) collective-permute-start(bf16[384,384]{1,0:T(8,128)(2,1)S(1)} %bitcast.3), channel_id=1, source_target_pairs={{1,2},{2,1},{5,6},{6,5},{9,10},{10,9},{13,14},{14,13},{17,18},{18,... | collective-permute-start | bytes 884744 | tf_op jit(solution)/shard_map/ppermute | solution.py:259
  32.2 8.8 %collective-permute-start.12 = (bf16[2,192,384]{2,1,0:T(8,128)(2,1)S(1)}, bf16[2,192,384]{2,1,0:T(8,128)(2,1)S(1)}, u32[]{:S(2)}, u32[]{:S(2)}) collective-permute-start(bf16[2,192,384]{2,1,0:T(8,128)(2,1)S(1)} %shard_map.50.refs_0_), channel_id=1, source_target_pairs={{0,1},{1,0},{2,3},{3,2},{4,5},{5,4},{6,7},{7,6},{8,9},{9,8},{10,11... | collective-permute-start | bytes 884744 | tf_op jit(solution)/shard_map/ppermute | solution.py:259
  32.3 13.9 %collective-permute-start.13 = (bf16[2,192,384]{2,1,0:T(8,128)(2,1)S(1)}, bf16[2,192,384]{2,1,0:T(8,128)(2,1)S(1)}, u32[]{:S(2)}, u32[]{:S(2)}) collective-permute-start(bf16[2,192,384]{2,1,0:T(8,128)(2,1)S(1)} %shard_map.50.refs_0_), channel_id=1, source_target_pairs={{1,2},{2,1},{5,6},{6,5},{9,10},{10,9},{13,14},{14,13},{17,18},{18,... | collective-permute-start | bytes 884744 | tf_op jit(solution)/shard_map/ppermute | solution.py:259
  34.5 12.8 %collective-permute-start.18 = (bf16[2,192,384]{2,1,0:T(8,128)(2,1)S(1)}, bf16[2,192,384]{2,1,0:T(8,128)(2,1)S(1)}, u32[]{:S(2)}, u32[]{:S(2)}) collective-permute-start(bf16[2,192,384]{2,1,0:T(8,128)(2,1)S(1)} %shard_map.52.refs_1_), channel_id=1, source_target_pairs={{0,1},{1,0},{2,3},{3,2},{4,5},{5,4},{6,7},{7,6},{8,9},{9,8},{10,11... | collective-permute-start | bytes 884744 | tf_op jit(solution)/shard_map/ppermute | solution.py:259
  34.6 18.0 %collective-permute-start.19 = (bf16[2,192,384]{2,1,0:T(8,128)(2,1)S(1)}, bf16[2,192,384]{2,1,0:T(8,128)(2,1)S(1)}, u32[]{:S(2)}, u32[]{:S(2)}) collective-permute-start(bf16[2,192,384]{2,1,0:T(8,128)(2,1)S(1)} %shard_map.52.refs_1_), channel_id=1, source_target_pairs={{1,2},{2,1},{5,6},{6,5},{9,10},{10,9},{13,14},{14,13},{17,18},{18,... | collective-permute-start | bytes 884744 | tf_op jit(solution)/shard_map/ppermute | solution.py:259
  53.7 4.0 %collective-permute-start.20 = (bf16[2,48,384]{2,1,0:T(8,128)(2,1)S(1)}, bf16[2,48,384]{2,1,0:T(8,128)(2,1)S(1)}, u32[]{:S(2)}, u32[]{:S(2)}) collective-permute-start(bf16[2,48,384]{2,1,0:T(8,128)(2,1)S(1)} %get-tuple-element.53), channel_id=1, source_target_pairs={{0,4},{4,0},{8,12},{12,8},{16,20},{20,16},{24,28},{28,24},{1,5},{5... | collective-permute-start | bytes 221192 | tf_op jit(solution)/shard_map/ppermute | solution.py:252
  54.2 4.0 %collective-permute-start.21 = (bf16[2,48,384]{2,1,0:T(8,128)(2,1)S(1)}, bf16[2,48,384]{2,1,0:T(8,128)(2,1)S(1)}, u32[]{:S(2)}, u32[]{:S(2)}) collective-permute-start(bf16[2,48,384]{2,1,0:T(8,128)(2,1)S(1)} %get-tuple-element.54), channel_id=1, source_target_pairs={{0,8},{4,12},{8,0},{12,4},{16,24},{20,28},{24,16},{28,20},{1,9},{5... | collective-permute-start | bytes 221192 | tf_op jit(solution)/shard_map/ppermute | solution.py:252
  54.2 6.1 %collective-permute-start.22 = (bf16[2,48,384]{2,1,0:T(8,128)(2,1)S(1)}, bf16[2,48,384]{2,1,0:T(8,128)(2,1)S(1)}, u32[]{:S(2)}, u32[]{:S(2)}) collective-permute-start(bf16[2,48,384]{2,1,0:T(8,128)(2,1)S(1)} %get-tuple-element.55), channel_id=1, source_target_pairs={{0,12},{4,8},{8,4},{12,0},{16,28},{20,24},{24,20},{28,16},{1,13},{... | collective-permute-start | bytes 221192 | tf_op jit(solution)/shard_map/ppermute | solution.py:252
  55.9 4.4 %collective-permute-start.23 = (bf16[2,48,384]{2,1,0:T(8,128)(2,1)S(1)}, bf16[2,48,384]{2,1,0:T(8,128)(2,1)S(1)}, u32[]{:S(2)}, u32[]{:S(2)}) collective-permute-start(bf16[2,48,384]{2,1,0:T(8,128)(2,1)S(1)} %get-tuple-element.56), channel_id=1, source_target_pairs={{0,16},{4,20},{8,24},{12,28},{16,0},{20,4},{24,8},{28,12},{1,17},{... | collective-permute-start | bytes 221192 | tf_op jit(solution)/shard_map/ppermute | solution.py:252
  56.2 8.4 %collective-permute-start.24 = (bf16[2,48,384]{2,1,0:T(8,128)(2,1)S(1)}, bf16[2,48,384]{2,1,0:T(8,128)(2,1)S(1)}, u32[]{:S(2)}, u32[]{:S(2)}) collective-permute-start(bf16[2,48,384]{2,1,0:T(8,128)(2,1)S(1)} %get-tuple-element.57), channel_id=1, source_target_pairs={{0,20},{4,16},{8,28},{12,24},{16,4},{20,0},{24,12},{28,8},{1,21},{... | collective-permute-start | bytes 221192 | tf_op jit(solution)/shard_map/ppermute | solution.py:252
  57.7 7.0 %collective-permute-start.25 = (bf16[2,48,384]{2,1,0:T(8,128)(2,1)S(1)}, bf16[2,48,384]{2,1,0:T(8,128)(2,1)S(1)}, u32[]{:S(2)}, u32[]{:S(2)}) collective-permute-start(bf16[2,48,384]{2,1,0:T(8,128)(2,1)S(1)} %get-tuple-element.58), channel_id=1, source_target_pairs={{0,24},{4,28},{8,16},{12,20},{16,8},{20,12},{24,0},{28,4},{1,25},{... | collective-permute-start | bytes 221192 | tf_op jit(solution)/shard_map/ppermute | solution.py:252
  58.2 6.5 %collective-permute-start.26 = (bf16[2,48,384]{2,1,0:T(8,128)(2,1)S(1)}, bf16[2,48,384]{2,1,0:T(8,128)(2,1)S(1)}, u32[]{:S(2)}, u32[]{:S(2)}) collective-permute-start(bf16[2,48,384]{2,1,0:T(8,128)(2,1)S(1)} %get-tuple-element.59), channel_id=1, source_target_pairs={{0,28},{4,24},{8,20},{12,16},{16,12},{20,8},{24,4},{28,0},{1,29},{... | collective-permute-start | bytes 221192 | tf_op jit(solution)/shard_map/ppermute | solution.py:252

commit v3 on v2

--- a/solution.py
+++ b/solution.py
@@ -45,6 +45,19 @@
 
 def sum_of(terms):
     return functools.reduce(lambda x, y: x + y, terms)
+
+
+def frequency(device, parts):
+    core, chip = device % 2, device // 2
+    parity = chip
+    for bit in range(1, parts.bit_length()):
+        parity = parity ^ (chip >> bit)
+    return 2 * chip + ((parity + core) & 1)
+
+
+def on_core(core, run):
+    for value in range(2):
+        pl.when(core == value)(functools.partial(run, value))
 
 
 def cut_kernel(order, partners, green, *refs):
@@ -91,43 +104,74 @@
 
     for_tiles(rows, cols, body)
     for j in range(count):
-        outs[j][...] = polar[order(j)].astype(BF16)
-
-
-def sigma_kernel(order, scaling, *refs):
-    count = len(refs) - 7
-    slot_ref = refs[0]
-    pieces = refs[1 : 1 + count]
-    lesser, out, weight, total, stage, sems = refs[1 + count :]
+        outs[j][...] = polar[frequency(order(j), energies)].astype(BF16)
+
+
+def lag_sums(lesser, weight, tile, energies, held):
+    low_re = [lesser[(0, g) + tile] for g in range(energies)]
+    low_im = [lesser[(1, g) + tile] for g in range(energies)]
+    w_re = [weight[(i, 0) + tile] for i in range(len(held))]
+    w_im = [weight[(i, 1) + tile] for i in range(len(held))]
+    low_sum = [a + b for a, b in zip(low_re, low_im)]
+    w_sum = [c + d for c, d in zip(w_re, w_im)]
+    w_gap = [d - c for c, d in zip(w_re, w_im)]
+    for e in range(energies):
+        pairs = [(i, e - w) for i, w in enumerate(held) if w <= e]
+        if not pairs:
+            yield e, None, None
+            continue
+        one = sum_of(w_re[i] * low_sum[g] for i, g in pairs)
+        two = sum_of(low_re[g] * w_gap[i] for i, g in pairs)
+        three = sum_of(low_im[g] * w_sum[i] for i, g in pairs)
+        yield e, one - three, one + two
+
+
+def held_by(core, parts):
+    return [frequency(2 * chip + core, parts) for chip in range(parts // 2)]
+
+
+def early_kernel(order, lesser, *refs):
+    pieces, (part, weight) = refs[:-2], refs[-2:]
     energies, rows, cols = lesser.shape[1:]
-    for j in range(count):
-        weight[order(j)] = pieces[j][...].astype(F32)
-
-    def body(tile):
-        low_re = [lesser[(0, g) + tile] for g in range(energies)]
-        low_im = [lesser[(1, g) + tile] for g in range(energies)]
-        w_re = [weight[(w, 0) + tile] for w in range(energies)]
-        w_im = [weight[(w, 1) + tile] for w in range(energies)]
-        low_sum = [a + b for a, b in zip(low_re, low_im)]
-        w_sum = [c + d for c, d in zip(w_re, w_im)]
-        w_gap = [d - c for c, d in zip(w_re, w_im)]
-        for e in range(energies):
-            one = sum_of(w_re[w] * low_sum[e - w] for w in range(e + 1))
-            two = sum_of(low_re[e - w] * w_gap[w] for w in range(e + 1))
-            three = sum_of(low_im[e - w] * w_sum[w] for w in range(e + 1))
-            total[(0, e) + tile] = (one + two) * -scaling
-            total[(1, e) + tile] = (one - three) * scaling
-
-    copies = []
-    height = SUBLANES
-    for chunk in range(rows // height):
-        at = pl.ds(chunk * height, height)
-        for_tiles(height, cols, body, chunk * height)
-        for s in range(energies):
-            for part in range(2):
-                stage[part, s, at] = total[part, slot_ref[s], at].astype(BF16)
-        copies.append(pltpu.make_async_copy(stage.at[:, :, at], out.at[:, :, 0, at], sems.at[chunk]))
-        copies[-1].start()
+    for i, piece in enumerate(pieces):
+        weight[order(2 * i) // 2] = piece[...].astype(F32)
+
+    def run(core):
+        def body(tile):
+            for e, real, imag in lag_sums(lesser, weight, tile, energies, held_by(core, energies)):
+                part[(0, e) + tile] = jnp.zeros_like(lesser[(0, e) + tile]) if real is None else real
+                part[(1, e) + tile] = jnp.zeros_like(lesser[(0, e) + tile]) if imag is None else imag
+
+        for_tiles(rows, cols, body)
+
+    on_core(order(0) % 2, run)
+
+
+def sigma_kernel(order, scaling, slot_ref, lesser, part, *refs):
+    pieces, (out, weight, total, stage, sems) = refs[:-5], refs[-5:]
+    energies, rows, cols = lesser.shape[1:]
+    for i, piece in enumerate(pieces):
+        weight[order(2 * i + 1) // 2] = piece[...].astype(F32)
+    chunks = [pl.ds(start, SUBLANES) for start in range(0, rows, SUBLANES)]
+    copies = [
+        pltpu.make_async_copy(stage.at[:, :, at], out.at[:, :, 0, at], sems.at[i]) for i, at in enumerate(chunks)
+    ]
+
+    def run(core):
+        def body(tile):
+            for e, real, imag in lag_sums(lesser, weight, tile, energies, held_by(1 - core, energies)):
+                begun_re, begun_im = part[(0, e) + tile], part[(1, e) + tile]
+                total[(0, e) + tile] = (begun_im if imag is None else begun_im + imag) * -scaling
+                total[(1, e) + tile] = (begun_re if real is None else begun_re + real) * scaling
+
+        for copy, at in zip(copies, chunks):
+            for_tiles(at.size, cols, body, at.start)
+            for s in range(energies):
+                for c in range(2):
+                    stage[c, s, at] = total[c, slot_ref[s], at].astype(BF16)
+            copy.start()
+
+    on_core(order(0) % 2, run)
     for copy in copies:
         copy.wait()
 
@@ -302,9 +346,7 @@
     )[0]
     left = struct((2, block, block // 2))
     right, left_near, left_far = call(
-        functools.partial(couple_kernel, order),
-        [struct((2 * block, block)), left, left],
-        [v_low[0], *upper],
+        functools.partial(couple_kernel, order), [struct((2 * block, block)), left, left], [v_low[0], *upper]
     )
     wide = pltpu.VMEM((block // 2, 2 * cols), BF16)
     begun = call(
@@ -322,20 +364,27 @@
         flops=3 * work,
     )
     screened_in = swap(screened_out, range(1, parts))
+    weights = pltpu.VMEM((half, 2, rows, cols), F32)
+    part = call(
+        functools.partial(early_kernel, order),
+        [struct((2, energies, rows, cols), F32)],
+        [lesser, *screened_in[::2]],
+        scratch=[weights],
+    )[0]
     return pl.pallas_call(
         functools.partial(sigma_kernel, order, scaling),
         name="sigma",
         out_shape=struct((2, energies, 1, rows, cols)),
-        in_specs=[smem()] + [vmem()] * (parts + 1),
+        in_specs=[smem()] + [vmem()] * (half + 2),
         out_specs=pl.BlockSpec(memory_space=pltpu.HBM),
         scratch_shapes=[
-            pltpu.VMEM((energies, 2, rows, cols), F32),
+            weights,
             pltpu.VMEM((2, energies, rows, cols), F32),
             pltpu.VMEM((2, energies, rows, cols), BF16),
             pltpu.SemaphoreType.DMA((rows // SUBLANES,)),
         ],
         compiler_params=pltpu.CompilerParams(vmem_limit_bytes=VMEM_LIMIT),
-    )(energy_slot, *screened_in, lesser)
+    )(energy_slot, lesser, part, *screened_in[1::2])
 
 
 def shifted(value, axis, steps):
@@ -438,7 +487,7 @@
     )
     out_specs = P(None, None, "space", "energy", None)
     parts = mesh.shape["energy"]
-    paired = parts & (parts - 1) == 0 and 1 < parts <= PAIRED and mesh.shape["space"] > 2
+    paired = parts & (parts - 1) == 0 and 4 <= parts <= PAIRED and mesh.shape["space"] > 2
 
     def whole(green, v_diag, v_low, energy_slot):
         rows = green.shape[3] // parts

time: 67 us -> 67.8 us (1.012)
  the two profiles are of different devices: /device:TPU:11 before, /device:TPU:16 now
where the time goes in v3:
time: 67.8 us; the launch traced here: 67.6 us
  starting transfers between devices  30.8 us (45%)
  waiting for transfers between devices  26.9 us (40%)
  Pallas kernels  9.6 us (14%)
    ppermute x21, starting transfers between devices, swap(): lax.ppermute(pieces[j], 'energy', [(i, i ^ j) for i in range(parts)])  20.6 us
    ppermute x21, waiting for transfers between devices, swap(): lax.ppermute(pieces[j], 'energy', [(i, i ^ j) for i in range(parts)])  14.7 us
    ppermute x6, waiting for transfers between devices, meet(): lax.ppermute(value, 'space', [p for i in lows for p in ((i, i + 1), (i +...  12.3 us
    ppermute x6, starting transfers between devices, meet(): lax.ppermute(value, 'space', [p for i in lows for p in ((i, i + 1), (i +...  10.2 us
    pallas_call x8, Pallas kernels, call(): pl.pallas_call(kernel, out_shape=outs, in_specs=[smem()] * tables + [vmem...  5.35 us
    pallas_call x2, Pallas kernels, take(): pl.pallas_call(functools.partial(cut_kernel, order, partners), out_shape=...  2.33 us
    pallas_call x1, Pallas kernels, direct(): pl.pallas_call(functools.partial(sigma_kernel, order, scaling), name='sig...  1.92 us
  transfers between devices with their start and end apart: 27, of which 10 were waited for; matrix products, arithmetic and copies ran while one was open for 0% of the time, Pallas kernels for 8%

profile of v3, /device:TPU:16, one launch (start us, length us, event | category | flops | bytes accessed | tf_op | source)
XLA Modules:
  0.0 67.6 jit_solution(6989685769922727773)
XLA Ops:
  0.0 1.3 %shard_map.46 = (bf16[4,48,384]{2,1,0:T(8,128)(2,1)S(1)}, bf16[4,48,384]{2,1,0:T(8,128)(2,1)S(1)}, bf16[4,48,384]{2,1,0:T(8,128)(2,1)S(1)}, bf16[4,48,384]{2,1,0...) custom-call(bf16[4,1,1,384,384]{4,3,2,1,0:T(8,128)(2,1)} %green.3), custom_call_target="tpu_custom_call" | custom-call | tf_op jit(solution)/shard_map/pallas_call | solution.py:307
  1.3 0.1 collective-permute-start
  1.4 1.6 %collective-permute-start.1 = (bf16[4,48,384]{2,1,0:T(8,128)(2,1)S(1)}, bf16[4,48,384]{2,1,0:T(8,128)(2,1)S(1)}, u32[]{:S(2)}, u32[]{:S(2)}) collective-permute-start(bf16[4,48,384]{2,1,0:T(8,128)(2,1)S(1)} %get-tuple-element.35), channel_id=1, source_target_pairs={{0,8},{4,12},{8,0},{12,4},{16,24},{20,28},{24,16},{28,20},{1,9},{5... | collective-permute-start | bytes 442376 | tf_op jit(solution)/shard_map/ppermute | solution.py:296
  3.0 0.3 collective-permute-start.2
  3.3 1.5 %collective-permute-start.3 = (bf16[4,48,384]{2,1,0:T(8,128)(2,1)S(1)}, bf16[4,48,384]{2,1,0:T(8,128)(2,1)S(1)}, u32[]{:S(2)}, u32[]{:S(2)}) collective-permute-start(bf16[4,48,384]{2,1,0:T(8,128)(2,1)S(1)} %get-tuple-element.37), channel_id=1, source_target_pairs={{0,16},{4,20},{8,24},{12,28},{16,0},{20,4},{24,8},{28,12},{1,17},{... | collective-permute-start | bytes 442376 | tf_op jit(solution)/shard_map/ppermute | solution.py:296
  4.8 0.2 collective-permute-start.4
  5.0 1.0 %shard_map.47 = (bf16[4,48,384]{2,1,0:T(8,128)(2,1)S(1)}, bf16[4,48,384]{2,1,0:T(8,128)(2,1)S(1)}) custom-call(bf16[4,1,1,384,384]{4,3,2,1,0:T(8,128)(2,1)} %green.3), custom_call_target="tpu_custom_call" | custom-call | tf_op jit(solution)/shard_map/pallas_call | solution.py:307
  6.0 0.0 collective-permute-done.refs_2_
  6.0 2.5 %collective-permute-start.5 = (bf16[4,48,384]{2,1,0:T(8,128)(2,1)S(1)}, bf16[4,48,384]{2,1,0:T(8,128)(2,1)S(1)}, u32[]{:S(2)}, u32[]{:S(2)}) collective-permute-start(bf16[4,48,384]{2,1,0:T(8,128)(2,1)S(1)} %get-tuple-element.39), channel_id=1, source_target_pairs={{0,24},{4,28},{8,16},{12,20},{16,8},{20,12},{24,0},{28,4},{1,25},{... | collective-permute-start | bytes 442376 | tf_op jit(solution)/shard_map/ppermute | solution.py:296
  8.5 0.0 collective-permute-done.1.refs_3_
  8.5 0.8 %collective-permute-start.6 = (bf16[4,48,384]{2,1,0:T(8,128)(2,1)S(1)}, bf16[4,48,384]{2,1,0:T(8,128)(2,1)S(1)}, u32[]{:S(2)}, u32[]{:S(2)}) collective-permute-start(bf16[4,48,384]{2,1,0:T(8,128)(2,1)S(1)} %get-tuple-element.40), channel_id=1, source_target_pairs={{0,28},{4,24},{8,20},{12,16},{16,12},{20,8},{24,4},{28,0},{1,29},{... | collective-permute-start | bytes 442376 | tf_op jit(solution)/shard_map/ppermute | solution.py:296
  9.3 1.1 %collective-permute-done.2.refs_4_ = bf16[4,48,384]{2,1,0:T(8,128)(2,1)S(1)} collective-permute-done((bf16[4,48,384]{2,1,0:T(8,128)(2,1)S(1)}, bf16[4,48,384]{2,1,0:T(8,128)(2,1)S(1)}, u32[]{:S(2)}, u32[]{:S(2)}) %collective-permute-start.2) | collective-permute-done | bytes 147488 | tf_op jit(solution)/shard_map/ppermute | solution.py:296
  10.4 1.6 %collective-permute-start.7 = (bf16[384,384]{1,0:T(8,128)(2,1)S(1)}, bf16[384,384]{1,0:T(8,128)(2,1)S(1)}, u32[]{:S(2)}, u32[]{:S(2)}) collective-permute-start(bf16[384,384]{1,0:T(8,128)(2,1)S(1)} %bitcast.2), channel_id=1, source_target_pairs={{0,1},{1,0},{2,3},{3,2},{4,5},{5,4},{6,7},{7,6},{8,9},{9,8},{10,11... | collective-permute-start | bytes 884744 | tf_op jit(solution)/shard_map/ppermute | solution.py:303
  12.0 0.0 collective-permute-done.3.refs_5_
  12.0 6.3 %collective-permute-done.4.refs_6_ = bf16[4,48,384]{2,1,0:T(8,128)(2,1)S(1)} collective-permute-done((bf16[4,48,384]{2,1,0:T(8,128)(2,1)S(1)}, bf16[4,48,384]{2,1,0:T(8,128)(2,1)S(1)}, u32[]{:S(2)}, u32[]{:S(2)}) %collective-permute-start.4) | collective-permute-done | bytes 147488 | tf_op jit(solution)/shard_map/ppermute | solution.py:296
  18.3 0.0 collective-permute-done.5.refs_7_
  18.3 0.0 collective-permute-done.6.refs_8_
  18.3 0.0 copy-start.1
  18.3 1.6 %shard_map.48 = (bf16[2,48,384]{2,1,0:T(8,128)(2,1)S(1)}, bf16[2,48,384]{2,1,0:T(8,128)(2,1)S(1)}, bf16[2,48,384]{2,1,0:T(8,128)(2,1)S(1)}, bf16[2,48,384]{2,1,0...) custom-call(s32[8]{0:T(128)S(1)} %copy-done.2, ...), custom_call_target="tpu_custom_call" | custom-call | bytes 2949152 | tf_op jit(solution)/shard_map/pallas_call | solution.py:268
  19.9 0.8 %collective-permute-start.9 = (bf16[2,48,384]{2,1,0:T(8,128)(2,1)S(1)}, bf16[2,48,384]{2,1,0:T(8,128)(2,1)S(1)}, u32[]{:S(2)}, u32[]{:S(2)}) collective-permute-start(bf16[2,48,384]{2,1,0:T(8,128)(2,1)S(1)} %get-tuple-element.46), channel_id=1, source_target_pairs={{0,4},{4,0},{8,12},{12,8},{16,20},{20,16},{24,28},{28,24},{1,5},{5... | collective-permute-start | bytes 221192 | tf_op jit(solution)/shard_map/ppermute | solution.py:296
  20.7 1.5 %collective-permute-start.10 = (bf16[2,48,384]{2,1,0:T(8,128)(2,1)S(1)}, bf16[2,48,384]{2,1,0:T(8,128)(2,1)S(1)}, u32[]{:S(2)}, u32[]{:S(2)}) collective-permute-start(bf16[2,48,384]{2,1,0:T(8,128)(2,1)S(1)} %get-tuple-element.47), channel_id=1, source_target_pairs={{0,8},{4,12},{8,0},{12,4},{16,24},{20,28},{24,16},{28,20},{1,9},{5... | collective-permute-start | bytes 221192 | tf_op jit(solution)/shard_map/ppermute | solution.py:296
  22.1 0.0 collective-permute-start.11
  22.1 1.5 %collective-permute-start.14 = (bf16[2,48,384]{2,1,0:T(8,128)(2,1)S(1)}, bf16[2,48,384]{2,1,0:T(8,128)(2,1)S(1)}, u32[]{:S(2)}, u32[]{:S(2)}) collective-permute-start(bf16[2,48,384]{2,1,0:T(8,128)(2,1)S(1)} %get-tuple-element.49), channel_id=1, source_target_pairs={{0,16},{4,20},{8,24},{12,28},{16,0},{20,4},{24,8},{28,12},{1,17},{... | collective-permute-start | bytes 221192 | tf_op jit(solution)/shard_map/ppermute | solution.py:296
  23.7 0.0 collective-permute-done.9.refs_1_
  23.7 0.5 collective-permute-start.15
  24.2 0.9 %collective-permute-done.10.refs_2_ = bf16[2,48,384]{2,1,0:T(8,128)(2,1)S(1)} collective-permute-done((bf16[2,48,384]{2,1,0:T(8,128)(2,1)S(1)}, bf16[2,48,384]{2,1,0:T(8,128)(2,1)S(1)}, u32[]{:S(2)}, u32[]{:S(2)}) %collective-permute-start.10) | collective-permute-done | bytes 73760 | tf_op jit(solution)/shard_map/ppermute | solution.py:296
  25.0 3.2 %collective-permute-start.16 = (bf16[2,48,384]{2,1,0:T(8,128)(2,1)S(1)}, bf16[2,48,384]{2,1,0:T(8,128)(2,1)S(1)}, u32[]{:S(2)}, u32[]{:S(2)}) collective-permute-start(bf16[2,48,384]{2,1,0:T(8,128)(2,1)S(1)} %get-tuple-element.51), channel_id=1, source_target_pairs={{0,24},{4,28},{8,16},{12,20},{16,8},{20,12},{24,0},{28,4},{1,25},{... | collective-permute-start | bytes 221192 | tf_op jit(solution)/shard_map/ppermute | solution.py:296
  28.2 0.0 collective-permute-done.11.refs_3_
  28.2 0.5 collective-permute-start.17
  28.8 0.0 collective-permute-done.14.refs_0_
  28.8 2.4 %collective-permute-start.8 = (bf16[384,384]{1,0:T(8,128)(2,1)S(1)}, bf16[384,384]{1,0:T(8,128)(2,1)S(1)}, u32[]{:S(2)}, u32[]{:S(2)}) collective-permute-start(bf16[384,384]{1,0:T(8,128)(2,1)S(1)} %bitcast.3), channel_id=1, source_target_pairs={{1,2},{2,1},{5,6},{6,5},{9,10},{10,9},{13,14},{14,13},{17,18},{18,... | collective-permute-start | bytes 884744 | tf_op jit(solution)/shard_map/ppermute | solution.py:303
  31.1 0.0 collective-permute-done.15.refs_1_
  31.1 0.1 collective-permute-start.12
  31.2 0.0 collective-permute-done.16.refs_2_
  31.2 3.5 %collective-permute-start.13 = (bf16[2,192,384]{2,1,0:T(8,128)(2,1)S(1)}, bf16[2,192,384]{2,1,0:T(8,128)(2,1)S(1)}, u32[]{:S(2)}, u32[]{:S(2)}) collective-permute-start(bf16[2,192,384]{2,1,0:T(8,128)(2,1)S(1)} %shard_map.50.refs_0_), channel_id=1, source_target_pairs={{1,2},{2,1},{5,6},{6,5},{9,10},{10,9},{13,14},{14,13},{17,18},{18,... | collective-permute-start | bytes 884744 | tf_op jit(solution)/shard_map/ppermute | solution.py:303
  34.7 0.0 collective-permute-done.17.refs_3_
  34.8 0.1 collective-permute-start.18
  34.9 0.0 collective-permute-done.7.up_even
  34.9 2.6 %collective-permute-start.19 = (bf16[2,192,384]{2,1,0:T(8,128)(2,1)S(1)}, bf16[2,192,384]{2,1,0:T(8,128)(2,1)S(1)}, u32[]{:S(2)}, u32[]{:S(2)}) collective-permute-start(bf16[2,192,384]{2,1,0:T(8,128)(2,1)S(1)} %shard_map.52.refs_1_), channel_id=1, source_target_pairs={{1,2},{2,1},{5,6},{6,5},{9,10},{10,9},{13,14},{14,13},{17,18},{18,... | collective-permute-start | bytes 884744 | tf_op jit(solution)/shard_map/ppermute | solution.py:303
  37.5 1.1 %shard_map.53.own = f32[2,384,384]{2,1,0:T(8,128)S(1)} custom-call(bf16[384,384]{1,0:T(8,128)(2,1)S(1)} %bitcast.5, bf16[2,192,384]{2,1,0:T(8,128)(2,1)S(1)} %shard_map.50.refs_0_, bf16[2,192,384]{2,1,0:T(8,128)(2,1)S(1)} %shard_map.52.refs_1_), custom_call_target="tpu_custom_call" | custom-call | flops 452984832 | bytes 2064384 | tf_op jit(solution)/shard_map/pallas_call | solution.py:268
  38.6 1.9 %collective-permute-done.8.up_odd = bf16[384,384]{1,0:T(8,128)(2,1)S(1)} collective-permute-done((bf16[384,384]{1,0:T(8,128)(2,1)S(1)}, bf16[384,384]{1,0:T(8,128)(2,1)S(1)}, u32[]{:S(2)}, u32[]{:S(2)}) %collective-permute-start.8) | collective-permute-done | bytes 294944 | tf_op jit(solution)/shard_map/ppermute | solution.py:303
  40.5 0.4 shard_map.49
  41.0 0.1 collective-permute-done.12.even
  41.1 5.8 %collective-permute-done.13.odd = bf16[2,192,384]{2,1,0:T(8,128)(2,1)S(1)} collective-permute-done((bf16[2,192,384]{2,1,0:T(8,128)(2,1)S(1)}, bf16[2,192,384]{2,1,0:T(8,128)(2,1)S(1)}, u32[]{:S(2)}, u32[]{:S(2)}) %collective-permute-start.13) | collective-permute-done | bytes 294944 | tf_op jit(solution)/shard_map/ppermute | solution.py:303
  46.9 0.5 shard_map.51.begun
  47.4 0.0 collective-permute-done.18.even
  47.4 4.5 %collective-permute-done.19.odd = bf16[2,192,384]{2,1,0:T(8,128)(2,1)S(1)} collective-permute-done((bf16[2,192,384]{2,1,0:T(8,128)(2,1)S(1)}, bf16[2,192,384]{2,1,0:T(8,128)(2,1)S(1)}, u32[]{:S(2)}, u32[]{:S(2)}) %collective-permute-start.19) | collective-permute-done | bytes 294944 | tf_op jit(solution)/shard_map/ppermute | solution.py:303
  51.8 1.2 %shard_map.54 = (bf16[2,48,384]{2,1,0:T(8,128)(2,1)S(1)}, bf16[2,48,384]{2,1,0:T(8,128)(2,1)S(1)}, bf16[2,48,384]{2,1,0:T(8,128)(2,1)S(1)}, bf16[2,48,384]{2,1,0...) custom-call(bf16[768,384]{1,0:T(8,128)(2,1)S(1)} %get-tuple-element., ...), custom_call_target="tpu_custom_call" | custom-call | flops 679477248 | bytes 5603328 | tf_op jit(solution)/shard_map/pallas_call | solution.py:268
  53.0 2.0 %collective-permute-start.20 = (bf16[2,48,384]{2,1,0:T(8,128)(2,1)S(1)}, bf16[2,48,384]{2,1,0:T(8,128)(2,1)S(1)}, u32[]{:S(2)}, u32[]{:S(2)}) collective-permute-start(bf16[2,48,384]{2,1,0:T(8,128)(2,1)S(1)} %get-tuple-element.54), channel_id=1, source_target_pairs={{0,8},{4,12},{8,0},{12,4},{16,24},{20,28},{24,16},{28,20},{1,9},{5... | collective-permute-start | bytes 221192 | tf_op jit(solution)/shard_map/ppermute | solution.py:296
  55.0 0.2 collective-permute-start.21
  55.2 1.4 %collective-permute-start.22 = (bf16[2,48,384]{2,1,0:T(8,128)(2,1)S(1)}, bf16[2,48,384]{2,1,0:T(8,128)(2,1)S(1)}, u32[]{:S(2)}, u32[]{:S(2)}) collective-permute-start(bf16[2,48,384]{2,1,0:T(8,128)(2,1)S(1)} %get-tuple-element.56), channel_id=1, source_target_pairs={{0,24},{4,28},{8,16},{12,20},{16,8},{20,12},{24,0},{28,4},{1,25},{... | collective-permute-start | bytes 221192 | tf_op jit(solution)/shard_map/ppermute | solution.py:296
  56.6 0.0 collective-permute-start.23
  56.6 2.1 %collective-permute-start.24 = (bf16[2,48,384]{2,1,0:T(8,128)(2,1)S(1)}, bf16[2,48,384]{2,1,0:T(8,128)(2,1)S(1)}, u32[]{:S(2)}, u32[]{:S(2)}) collective-permute-start(bf16[2,48,384]{2,1,0:T(8,128)(2,1)S(1)} %get-tuple-element.58), channel_id=1, source_target_pairs={{0,12},{4,8},{8,4},{12,0},{16,28},{20,24},{24,20},{28,16},{1,13},{... | collective-permute-start | bytes 221192 | tf_op jit(solution)/shard_map/ppermute | solution.py:296
  58.6 0.0 collective-permute-done.20.refs_1_
  58.6 0.0 collective-permute-start.25
  58.6 2.3 %collective-permute-done.21.refs_2_ = bf16[2,48,384]{2,1,0:T(8,128)(2,1)S(1)} collective-permute-done((bf16[2,48,384]{2,1,0:T(8,128)(2,1)S(1)}, bf16[2,48,384]{2,1,0:T(8,128)(2,1)S(1)}, u32[]{:S(2)}, u32[]{:S(2)}) %collective-permute-start.21) | collective-permute-done | bytes 73760 | tf_op jit(solution)/shard_map/ppermute | solution.py:296
  61.0 0.0 collective-permute-start.26
  61.0 0.0 collective-permute-done.22.refs_3_
  61.0 0.5 shard_map.55.part
  61.5 0.0 collective-permute-done.23.refs_0_
  61.6 0.0 collective-permute-done.24.refs_1_
  61.6 1.5 %collective-permute-done.25.refs_2_ = bf16[2,48,384]{2,1,0:T(8,128)(2,1)S(1)} collective-permute-done((bf16[2,48,384]{2,1,0:T(8,128)(2,1)S(1)}, bf16[2,48,384]{2,1,0:T(8,128)(2,1)S(1)}, u32[]{:S(2)}, u32[]{:S(2)}) %collective-permute-start.25) | collective-permute-done | bytes 73760 | tf_op jit(solution)/shard_map/ppermute | solution.py:296
  63.0 2.6 %collective-permute-done.26.refs_3_ = bf16[2,48,384]{2,1,0:T(8,128)(2,1)S(1)} collective-permute-done((bf16[2,48,384]{2,1,0:T(8,128)(2,1)S(1)}, bf16[2,48,384]{2,1,0:T(8,128)(2,1)S(1)}, u32[]{:S(2)}, u32[]{:S(2)}) %collective-permute-start.26) | collective-permute-done | bytes 73760 | tf_op jit(solution)/shard_map/ppermute | solution.py:296
  65.6 1.9 %sigma.1 = bf16[2,8,1,48,384]{4,3,2,1,0:T(8,128)(2,1)} custom-call(s32[8]{0:T(128)S(1)} %copy-done.2, f32[2,8,48,384]{3,2,1,0:T(8,128)S(1)} %get-tuple-element.41.lesser, f32[2,8,48,384]{3,2,1,0:T(8,128)S(1)} %shard_map.55.part, bf16[2,48,384]{2,1,0:T(8,128)(2,1)S(1)} %collective-permute-done.23.refs_0_, ...), custom_call_target="tpu_custom_call" | custom-call | tf_op jit(solution)/shard_map/sigma/pallas_call | solution.py:374
  (7 shorter events, 0.1 us)
Async XLA Ops:
  0.0 10.4 %copy-start = (bf16[1,384,384]{2,1,0:T(8,128)(2,1)S(1)}, bf16[1,384,384]{2,1,0:T(8,128)(2,1)}, u32[]{:S(2)}) copy-start(bf16[1,384,384]{2,1,0:T(8,128)(2,1)} %param.6) | copy-start | bytes 884740
  0.0 18.3 %copy-start.2 = (s32[8]{0:T(128)S(1)}, s32[8]{0:T(128)}, u32[]{:S(2)}) copy-start(s32[8]{0:T(128)} %slot_ref.1) | copy-start | bytes 100
  1.3 4.6 %collective-permute-start = (bf16[4,48,384]{2,1,0:T(8,128)(2,1)S(1)}, bf16[4,48,384]{2,1,0:T(8,128)(2,1)S(1)}, u32[]{:S(2)}, u32[]{:S(2)}) collective-permute-start(bf16[4,48,384]{2,1,0:T(8,128)(2,1)S(1)} %get-tuple-element.34), channel_id=1, source_target_pairs={{0,4},{4,0},{8,12},{12,8},{16,20},{20,16},{24,28},{28,24},{1,5},{5... | collective-permute-start | bytes 442376 | tf_op jit(solution)/shard_map/ppermute | solution.py:296
  1.4 7.1 %collective-permute-start.1 = (bf16[4,48,384]{2,1,0:T(8,128)(2,1)S(1)}, bf16[4,48,384]{2,1,0:T(8,128)(2,1)S(1)}, u32[]{:S(2)}, u32[]{:S(2)}) collective-permute-start(bf16[4,48,384]{2,1,0:T(8,128)(2,1)S(1)} %get-tuple-element.35), channel_id=1, source_target_pairs={{0,8},{4,12},{8,0},{12,4},{16,24},{20,28},{24,16},{28,20},{1,9},{5... | collective-permute-start | bytes 442376 | tf_op jit(solution)/shard_map/ppermute | solution.py:296
  3.0 7.4 %collective-permute-start.2 = (bf16[4,48,384]{2,1,0:T(8,128)(2,1)S(1)}, bf16[4,48,384]{2,1,0:T(8,128)(2,1)S(1)}, u32[]{:S(2)}, u32[]{:S(2)}) collective-permute-start(bf16[4,48,384]{2,1,0:T(8,128)(2,1)S(1)} %get-tuple-element.36), channel_id=1, source_target_pairs={{0,12},{4,8},{8,4},{12,0},{16,28},{20,24},{24,20},{28,16},{1,13},{... | collective-permute-start | bytes 442376 | tf_op jit(solution)/shard_map/ppermute | solution.py:296
  3.3 8.7 %collective-permute-start.3 = (bf16[4,48,384]{2,1,0:T(8,128)(2,1)S(1)}, bf16[4,48,384]{2,1,0:T(8,128)(2,1)S(1)}, u32[]{:S(2)}, u32[]{:S(2)}) collective-permute-start(bf16[4,48,384]{2,1,0:T(8,128)(2,1)S(1)} %get-tuple-element.37), channel_id=1, source_target_pairs={{0,16},{4,20},{8,24},{12,28},{16,0},{20,4},{24,8},{28,12},{1,17},{... | collective-permute-start | bytes 442376 | tf_op jit(solution)/shard_map/ppermute | solution.py:296
  4.8 13.5 %collective-permute-start.4 = (bf16[4,48,384]{2,1,0:T(8,128)(2,1)S(1)}, bf16[4,48,384]{2,1,0:T(8,128)(2,1)S(1)}, u32[]{:S(2)}, u32[]{:S(2)}) collective-permute-start(bf16[4,48,384]{2,1,0:T(8,128)(2,1)S(1)} %get-tuple-element.38), channel_id=1, source_target_pairs={{0,20},{4,16},{8,28},{12,24},{16,4},{20,0},{24,12},{28,8},{1,21},{... | collective-permute-start | bytes 442376 | tf_op jit(solution)/shard_map/ppermute | solution.py:296
  6.0 12.3 %collective-permute-start.5 = (bf16[4,48,384]{2,1,0:T(8,128)(2,1)S(1)}, bf16[4,48,384]{2,1,0:T(8,128)(2,1)S(1)}, u32[]{:S(2)}, u32[]{:S(2)}) collective-permute-start(bf16[4,48,384]{2,1,0:T(8,128)(2,1)S(1)} %get-tuple-element.39), channel_id=1, source_target_pairs={{0,24},{4,28},{8,16},{12,20},{16,8},{20,12},{24,0},{28,4},{1,25},{... | collective-permute-start | bytes 442376 | tf_op jit(solution)/shard_map/ppermute | solution.py:296
  8.5 9.7 %collective-permute-start.6 = (bf16[4,48,384]{2,1,0:T(8,128)(2,1)S(1)}, bf16[4,48,384]{2,1,0:T(8,128)(2,1)S(1)}, u32[]{:S(2)}, u32[]{:S(2)}) collective-permute-start(bf16[4,48,384]{2,1,0:T(8,128)(2,1)S(1)} %get-tuple-element.40), channel_id=1, source_target_pairs={{0,28},{4,24},{8,20},{12,16},{16,12},{20,8},{24,4},{28,0},{1,29},{... | collective-permute-start | bytes 442376 | tf_op jit(solution)/shard_map/ppermute | solution.py:296
  10.4 24.5 %collective-permute-start.7 = (bf16[384,384]{1,0:T(8,128)(2,1)S(1)}, bf16[384,384]{1,0:T(8,128)(2,1)S(1)}, u32[]{:S(2)}, u32[]{:S(2)}) collective-permute-start(bf16[384,384]{1,0:T(8,128)(2,1)S(1)} %bitcast.2), channel_id=1, source_target_pairs={{0,1},{1,0},{2,3},{3,2},{4,5},{5,4},{6,7},{7,6},{8,9},{9,8},{10,11... | collective-permute-start | bytes 884744 | tf_op jit(solution)/shard_map/ppermute | solution.py:303
  18.3 19.3 %copy-start.1 = (bf16[1,384,384]{2,1,0:T(8,128)(2,1)S(1)}, bf16[1,384,384]{2,1,0:T(8,128)(2,1)}, u32[]{:S(2)}) copy-start(bf16[1,384,384]{2,1,0:T(8,128)(2,1)} %param.5) | copy-start | bytes 884740
  19.9 3.8 %collective-permute-start.9 = (bf16[2,48,384]{2,1,0:T(8,128)(2,1)S(1)}, bf16[2,48,384]{2,1,0:T(8,128)(2,1)S(1)}, u32[]{:S(2)}, u32[]{:S(2)}) collective-permute-start(bf16[2,48,384]{2,1,0:T(8,128)(2,1)S(1)} %get-tuple-element.46), channel_id=1, source_target_pairs={{0,4},{4,0},{8,12},{12,8},{16,20},{20,16},{24,28},{28,24},{1,5},{5... | collective-permute-start | bytes 221192 | tf_op jit(solution)/shard_map/ppermute | solution.py:296
  20.7 4.4 %collective-permute-start.10 = (bf16[2,48,384]{2,1,0:T(8,128)(2,1)S(1)}, bf16[2,48,384]{2,1,0:T(8,128)(2,1)S(1)}, u32[]{:S(2)}, u32[]{:S(2)}) collective-permute-start(bf16[2,48,384]{2,1,0:T(8,128)(2,1)S(1)} %get-tuple-element.47), channel_id=1, source_target_pairs={{0,8},{4,12},{8,0},{12,4},{16,24},{20,28},{24,16},{28,20},{1,9},{5... | collective-permute-start | bytes 221192 | tf_op jit(solution)/shard_map/ppermute | solution.py:296
  22.1 6.1 %collective-permute-start.11 = (bf16[2,48,384]{2,1,0:T(8,128)(2,1)S(1)}, bf16[2,48,384]{2,1,0:T(8,128)(2,1)S(1)}, u32[]{:S(2)}, u32[]{:S(2)}) collective-permute-start(bf16[2,48,384]{2,1,0:T(8,128)(2,1)S(1)} %get-tuple-element.48), channel_id=1, source_target_pairs={{0,12},{4,8},{8,4},{12,0},{16,28},{20,24},{24,20},{28,16},{1,13},{... | collective-permute-start | bytes 221192 | tf_op jit(solution)/shard_map/ppermute | solution.py:296
  22.1 6.6 %collective-permute-start.14 = (bf16[2,48,384]{2,1,0:T(8,128)(2,1)S(1)}, bf16[2,48,384]{2,1,0:T(8,128)(2,1)S(1)}, u32[]{:S(2)}, u32[]{:S(2)}) collective-permute-start(bf16[2,48,384]{2,1,0:T(8,128)(2,1)S(1)} %get-tuple-element.49), channel_id=1, source_target_pairs={{0,16},{4,20},{8,24},{12,28},{16,0},{20,4},{24,8},{28,12},{1,17},{... | collective-permute-start | bytes 221192 | tf_op jit(solution)/shard_map/ppermute | solution.py:296
  23.7 7.5 %collective-permute-start.15 = (bf16[2,48,384]{2,1,0:T(8,128)(2,1)S(1)}, bf16[2,48,384]{2,1,0:T(8,128)(2,1)S(1)}, u32[]{:S(2)}, u32[]{:S(2)}) collective-permute-start(bf16[2,48,384]{2,1,0:T(8,128)(2,1)S(1)} %get-tuple-element.50), channel_id=1, source_target_pairs={{0,20},{4,16},{8,28},{12,24},{16,4},{20,0},{24,12},{28,8},{1,21},{... | collective-permute-start | bytes 221192 | tf_op jit(solution)/shard_map/ppermute | solution.py:296
  25.0 6.2 %collective-permute-start.16 = (bf16[2,48,384]{2,1,0:T(8,128)(2,1)S(1)}, bf16[2,48,384]{2,1,0:T(8,128)(2,1)S(1)}, u32[]{:S(2)}, u32[]{:S(2)}) collective-permute-start(bf16[2,48,384]{2,1,0:T(8,128)(2,1)S(1)} %get-tuple-element.51), channel_id=1, source_target_pairs={{0,24},{4,28},{8,16},{12,20},{16,8},{20,12},{24,0},{28,4},{1,25},{... | collective-permute-start | bytes 221192 | tf_op jit(solution)/shard_map/ppermute | solution.py:296
  28.2 6.5 %collective-permute-start.17 = (bf16[2,48,384]{2,1,0:T(8,128)(2,1)S(1)}, bf16[2,48,384]{2,1,0:T(8,128)(2,1)S(1)}, u32[]{:S(2)}, u32[]{:S(2)}) collective-permute-start(bf16[2,48,384]{2,1,0:T(8,128)(2,1)S(1)} %get-tuple-element.52), channel_id=1, source_target_pairs={{0,28},{4,24},{8,20},{12,16},{16,12},{20,8},{24,4},{28,0},{1,29},{... | collective-permute-start | bytes 221192 | tf_op jit(solution)/shard_map/ppermute | solution.py:296
  28.8 11.8 %collective-permute-start.8 = (bf16[384,384]{1,0:T(8,128)(2,1)S(1)}, bf16[384,384]{1,0:T(8,128)(2,1)S(1)}, u32[]{:S(2)}, u32[]{:S(2)}) collective-permute-start(bf16[384,384]{1,0:T(8,128)(2,1)S(1)} %bitcast.3), channel_id=1, source_target_pairs={{1,2},{2,1},{5,6},{6,5},{9,10},{10,9},{13,14},{14,13},{17,18},{18,... | collective-permute-start | bytes 884744 | tf_op jit(solution)/shard_map/ppermute | solution.py:303
  31.1 9.9 %collective-permute-start.12 = (bf16[2,192,384]{2,1,0:T(8,128)(2,1)S(1)}, bf16[2,192,384]{2,1,0:T(8,128)(2,1)S(1)}, u32[]{:S(2)}, u32[]{:S(2)}) collective-permute-start(bf16[2,192,384]{2,1,0:T(8,128)(2,1)S(1)} %shard_map.50.refs_0_), channel_id=1, source_target_pairs={{0,1},{1,0},{2,3},{3,2},{4,5},{5,4},{6,7},{7,6},{8,9},{9,8},{10,11... | collective-permute-start | bytes 884744 | tf_op jit(solution)/shard_map/ppermute | solution.py:303
  31.2 15.6 %collective-permute-start.13 = (bf16[2,192,384]{2,1,0:T(8,128)(2,1)S(1)}, bf16[2,192,384]{2,1,0:T(8,128)(2,1)S(1)}, u32[]{:S(2)}, u32[]{:S(2)}) collective-permute-start(bf16[2,192,384]{2,1,0:T(8,128)(2,1)S(1)} %shard_map.50.refs_0_), channel_id=1, source_target_pairs={{1,2},{2,1},{5,6},{6,5},{9,10},{10,9},{13,14},{14,13},{17,18},{18,... | collective-permute-start | bytes 884744 | tf_op jit(solution)/shard_map/ppermute | solution.py:303
  34.8 12.6 %collective-permute-start.18 = (bf16[2,192,384]{2,1,0:T(8,128)(2,1)S(1)}, bf16[2,192,384]{2,1,0:T(8,128)(2,1)S(1)}, u32[]{:S(2)}, u32[]{:S(2)}) collective-permute-start(bf16[2,192,384]{2,1,0:T(8,128)(2,1)S(1)} %shard_map.52.refs_1_), channel_id=1, source_target_pairs={{0,1},{1,0},{2,3},{3,2},{4,5},{5,4},{6,7},{7,6},{8,9},{9,8},{10,11... | collective-permute-start | bytes 884744 | tf_op jit(solution)/shard_map/ppermute | solution.py:303
  34.9 16.9 %collective-permute-start.19 = (bf16[2,192,384]{2,1,0:T(8,128)(2,1)S(1)}, bf16[2,192,384]{2,1,0:T(8,128)(2,1)S(1)}, u32[]{:S(2)}, u32[]{:S(2)}) collective-permute-start(bf16[2,192,384]{2,1,0:T(8,128)(2,1)S(1)} %shard_map.52.refs_1_), channel_id=1, source_target_pairs={{1,2},{2,1},{5,6},{6,5},{9,10},{10,9},{13,14},{14,13},{17,18},{18,... | collective-permute-start | bytes 884744 | tf_op jit(solution)/shard_map/ppermute | solution.py:303
  53.0 5.6 %collective-permute-start.20 = (bf16[2,48,384]{2,1,0:T(8,128)(2,1)S(1)}, bf16[2,48,384]{2,1,0:T(8,128)(2,1)S(1)}, u32[]{:S(2)}, u32[]{:S(2)}) collective-permute-start(bf16[2,48,384]{2,1,0:T(8,128)(2,1)S(1)} %get-tuple-element.54), channel_id=1, source_target_pairs={{0,8},{4,12},{8,0},{12,4},{16,24},{20,28},{24,16},{28,20},{1,9},{5... | collective-permute-start | bytes 221192 | tf_op jit(solution)/shard_map/ppermute | solution.py:296
  55.0 5.9 %collective-permute-start.21 = (bf16[2,48,384]{2,1,0:T(8,128)(2,1)S(1)}, bf16[2,48,384]{2,1,0:T(8,128)(2,1)S(1)}, u32[]{:S(2)}, u32[]{:S(2)}) collective-permute-start(bf16[2,48,384]{2,1,0:T(8,128)(2,1)S(1)} %get-tuple-element.55), channel_id=1, source_target_pairs={{0,16},{4,20},{8,24},{12,28},{16,0},{20,4},{24,8},{28,12},{1,17},{... | collective-permute-start | bytes 221192 | tf_op jit(solution)/shard_map/ppermute | solution.py:296
  55.2 5.8 %collective-permute-start.22 = (bf16[2,48,384]{2,1,0:T(8,128)(2,1)S(1)}, bf16[2,48,384]{2,1,0:T(8,128)(2,1)S(1)}, u32[]{:S(2)}, u32[]{:S(2)}) collective-permute-start(bf16[2,48,384]{2,1,0:T(8,128)(2,1)S(1)} %get-tuple-element.56), channel_id=1, source_target_pairs={{0,24},{4,28},{8,16},{12,20},{16,8},{20,12},{24,0},{28,4},{1,25},{... | collective-permute-start | bytes 221192 | tf_op jit(solution)/shard_map/ppermute | solution.py:296
  56.6 5.0 %collective-permute-start.23 = (bf16[2,48,384]{2,1,0:T(8,128)(2,1)S(1)}, bf16[2,48,384]{2,1,0:T(8,128)(2,1)S(1)}, u32[]{:S(2)}, u32[]{:S(2)}) collective-permute-start(bf16[2,48,384]{2,1,0:T(8,128)(2,1)S(1)} %get-tuple-element.57), channel_id=1, source_target_pairs={{0,4},{4,0},{8,12},{12,8},{16,20},{20,16},{24,28},{28,24},{1,5},{5... | collective-permute-start | bytes 221192 | tf_op jit(solution)/shard_map/ppermute | solution.py:296
  56.6 5.0 %collective-permute-start.24 = (bf16[2,48,384]{2,1,0:T(8,128)(2,1)S(1)}, bf16[2,48,384]{2,1,0:T(8,128)(2,1)S(1)}, u32[]{:S(2)}, u32[]{:S(2)}) collective-permute-start(bf16[2,48,384]{2,1,0:T(8,128)(2,1)S(1)} %get-tuple-element.58), channel_id=1, source_target_pairs={{0,12},{4,8},{8,4},{12,0},{16,28},{20,24},{24,20},{28,16},{1,13},{... | collective-permute-start | bytes 221192 | tf_op jit(solution)/shard_map/ppermute | solution.py:296
  58.6 4.4 %collective-permute-start.25 = (bf16[2,48,384]{2,1,0:T(8,128)(2,1)S(1)}, bf16[2,48,384]{2,1,0:T(8,128)(2,1)S(1)}, u32[]{:S(2)}, u32[]{:S(2)}) collective-permute-start(bf16[2,48,384]{2,1,0:T(8,128)(2,1)S(1)} %get-tuple-element.59), channel_id=1, source_target_pairs={{0,20},{4,16},{8,28},{12,24},{16,4},{20,0},{24,12},{28,8},{1,21},{... | collective-permute-start | bytes 221192 | tf_op jit(solution)/shard_map/ppermute | solution.py:296
  61.0 4.7 %collective-permute-start.26 = (bf16[2,48,384]{2,1,0:T(8,128)(2,1)S(1)}, bf16[2,48,384]{2,1,0:T(8,128)(2,1)S(1)}, u32[]{:S(2)}, u32[]{:S(2)}) collective-permute-start(bf16[2,48,384]{2,1,0:T(8,128)(2,1)S(1)} %get-tuple-element.60), channel_id=1, source_target_pairs={{0,28},{4,24},{8,20},{12,16},{16,12},{20,8},{24,4},{28,0},{1,29},{... | collective-permute-start | bytes 221192 | tf_op jit(solution)/shard_map/ppermute | solution.py:296

commit v4 on v3

--- a/solution.py
+++ b/solution.py
@@ -13,6 +13,7 @@
 BF16 = jnp.bfloat16
 LANES = 128
 SUBLANES = 16
+TILE = 8
 PAIRED = 16
 VMEM_LIMIT = 20 * 2**20
 
@@ -26,7 +27,7 @@
 
 
 def row_tile(rows):
-    return 8 if rows % 8 == 0 else rows
+    return TILE if rows % TILE == 0 else rows
 
 
 def for_tiles(rows, cols, body, start=0):
@@ -40,7 +41,7 @@
         body((pl.ds(row, height), pl.ds(col, LANES)))
         return carry
 
-    lax.fori_loop(0, down * across, step, 0, unroll=2)
+    lax.fori_loop(0, down * across, step, 0, unroll=across if down == 1 else 2)
 
 
 def sum_of(terms):
@@ -152,7 +153,7 @@
     energies, rows, cols = lesser.shape[1:]
     for i, piece in enumerate(pieces):
         weight[order(2 * i + 1) // 2] = piece[...].astype(F32)
-    chunks = [pl.ds(start, SUBLANES) for start in range(0, rows, SUBLANES)]
+    chunks = [pl.ds(start, TILE) for start in range(0, rows, TILE)]
     copies = [
         pltpu.make_async_copy(stage.at[:, :, at], out.at[:, :, 0, at], sems.at[i]) for i, at in enumerate(chunks)
     ]
@@ -381,7 +382,7 @@
             weights,
             pltpu.VMEM((2, energies, rows, cols), F32),
             pltpu.VMEM((2, energies, rows, cols), BF16),
-            pltpu.SemaphoreType.DMA((rows // SUBLANES,)),
+            pltpu.SemaphoreType.DMA((rows // TILE,)),
         ],
         compiler_params=pltpu.CompilerParams(vmem_limit_bytes=VMEM_LIMIT),
     )(energy_slot, lesser, part, *screened_in[1::2])

time: 67.8 us -> 67.6 us (level)
  no operation moved by 1% of the time
where the time goes in v4:
time: 67.6 us; the launch traced here: 67.4 us
  starting transfers between devices  30.8 us (46%)
  waiting for transfers between devices  26.9 us (40%)
  Pallas kernels  9.42 us (14%)
    ppermute x21, starting transfers between devices, swap(): lax.ppermute(pieces[j], 'energy', [(i, i ^ j) for i in range(parts)])  20.6 us
    ppermute x21, waiting for transfers between devices, swap(): lax.ppermute(pieces[j], 'energy', [(i, i ^ j) for i in range(parts)])  14.7 us
    ppermute x6, waiting for transfers between devices, meet(): lax.ppermute(value, 'space', [p for i in lows for p in ((i, i + 1), (i +...  12.3 us
    ppermute x6, starting transfers between devices, meet(): lax.ppermute(value, 'space', [p for i in lows for p in ((i, i + 1), (i +...  10.2 us
    pallas_call x8, Pallas kernels, call(): pl.pallas_call(kernel, out_shape=outs, in_specs=[smem()] * tables + [vmem...  5.35 us
    pallas_call x2, Pallas kernels, take(): pl.pallas_call(functools.partial(cut_kernel, order, partners), out_shape=...  2.33 us
    pallas_call x1, Pallas kernels, direct(): pl.pallas_call(functools.partial(sigma_kernel, order, scaling), name='sig...  1.74 us
  transfers between devices with their start and end apart: 27, of which 10 were waited for; matrix products, arithmetic and copies ran while one was open for 0% of the time, Pallas kernels for 8%

profile of v4, /device:TPU:16, one launch (start us, length us, event | category | flops | bytes accessed | tf_op | source)
XLA Modules:
  0.0 67.4 jit_solution(11514728123395171101)
XLA Ops:
  0.0 1.3 %shard_map.46 = (bf16[4,48,384]{2,1,0:T(8,128)(2,1)S(1)}, bf16[4,48,384]{2,1,0:T(8,128)(2,1)S(1)}, bf16[4,48,384]{2,1,0:T(8,128)(2,1)S(1)}, bf16[4,48,384]{2,1,0...) custom-call(bf16[4,1,1,384,384]{4,3,2,1,0:T(8,128)(2,1)} %green.3), custom_call_target="tpu_custom_call" | custom-call | tf_op jit(solution)/shard_map/pallas_call | solution.py:308
  1.3 0.1 collective-permute-start
  1.4 1.6 %collective-permute-start.1 = (bf16[4,48,384]{2,1,0:T(8,128)(2,1)S(1)}, bf16[4,48,384]{2,1,0:T(8,128)(2,1)S(1)}, u32[]{:S(2)}, u32[]{:S(2)}) collective-permute-start(bf16[4,48,384]{2,1,0:T(8,128)(2,1)S(1)} %get-tuple-element.35), channel_id=1, source_target_pairs={{0,8},{4,12},{8,0},{12,4},{16,24},{20,28},{24,16},{28,20},{1,9},{5... | collective-permute-start | bytes 442376 | tf_op jit(solution)/shard_map/ppermute | solution.py:297
  3.0 0.3 collective-permute-start.2
  3.3 1.5 %collective-permute-start.3 = (bf16[4,48,384]{2,1,0:T(8,128)(2,1)S(1)}, bf16[4,48,384]{2,1,0:T(8,128)(2,1)S(1)}, u32[]{:S(2)}, u32[]{:S(2)}) collective-permute-start(bf16[4,48,384]{2,1,0:T(8,128)(2,1)S(1)} %get-tuple-element.37), channel_id=1, source_target_pairs={{0,16},{4,20},{8,24},{12,28},{16,0},{20,4},{24,8},{28,12},{1,17},{... | collective-permute-start | bytes 442376 | tf_op jit(solution)/shard_map/ppermute | solution.py:297
  4.8 0.2 collective-permute-start.4
  5.0 1.0 %shard_map.47 = (bf16[4,48,384]{2,1,0:T(8,128)(2,1)S(1)}, bf16[4,48,384]{2,1,0:T(8,128)(2,1)S(1)}) custom-call(bf16[4,1,1,384,384]{4,3,2,1,0:T(8,128)(2,1)} %green.3), custom_call_target="tpu_custom_call" | custom-call | tf_op jit(solution)/shard_map/pallas_call | solution.py:308
  6.0 0.0 collective-permute-done.refs_2_
  6.0 2.5 %collective-permute-start.5 = (bf16[4,48,384]{2,1,0:T(8,128)(2,1)S(1)}, bf16[4,48,384]{2,1,0:T(8,128)(2,1)S(1)}, u32[]{:S(2)}, u32[]{:S(2)}) collective-permute-start(bf16[4,48,384]{2,1,0:T(8,128)(2,1)S(1)} %get-tuple-element.39), channel_id=1, source_target_pairs={{0,24},{4,28},{8,16},{12,20},{16,8},{20,12},{24,0},{28,4},{1,25},{... | collective-permute-start | bytes 442376 | tf_op jit(solution)/shard_map/ppermute | solution.py:297
  8.5 0.0 collective-permute-done.1.refs_3_
  8.5 0.8 %collective-permute-start.6 = (bf16[4,48,384]{2,1,0:T(8,128)(2,1)S(1)}, bf16[4,48,384]{2,1,0:T(8,128)(2,1)S(1)}, u32[]{:S(2)}, u32[]{:S(2)}) collective-permute-start(bf16[4,48,384]{2,1,0:T(8,128)(2,1)S(1)} %get-tuple-element.40), channel_id=1, source_target_pairs={{0,28},{4,24},{8,20},{12,16},{16,12},{20,8},{24,4},{28,0},{1,29},{... | collective-permute-start | bytes 442376 | tf_op jit(solution)/shard_map/ppermute | solution.py:297
  9.3 1.1 %collective-permute-done.2.refs_4_ = bf16[4,48,384]{2,1,0:T(8,128)(2,1)S(1)} collective-permute-done((bf16[4,48,384]{2,1,0:T(8,128)(2,1)S(1)}, bf16[4,48,384]{2,1,0:T(8,128)(2,1)S(1)}, u32[]{:S(2)}, u32[]{:S(2)}) %collective-permute-start.2) | collective-permute-done | bytes 147488 | tf_op jit(solution)/shard_map/ppermute | solution.py:297
  10.4 1.6 %collective-permute-start.7 = (bf16[384,384]{1,0:T(8,128)(2,1)S(1)}, bf16[384,384]{1,0:T(8,128)(2,1)S(1)}, u32[]{:S(2)}, u32[]{:S(2)}) collective-permute-start(bf16[384,384]{1,0:T(8,128)(2,1)S(1)} %bitcast.2), channel_id=1, source_target_pairs={{0,1},{1,0},{2,3},{3,2},{4,5},{5,4},{6,7},{7,6},{8,9},{9,8},{10,11... | collective-permute-start | bytes 884744 | tf_op jit(solution)/shard_map/ppermute | solution.py:304
  12.0 0.0 collective-permute-done.3.refs_5_
  12.0 6.3 %collective-permute-done.4.refs_6_ = bf16[4,48,384]{2,1,0:T(8,128)(2,1)S(1)} collective-permute-done((bf16[4,48,384]{2,1,0:T(8,128)(2,1)S(1)}, bf16[4,48,384]{2,1,0:T(8,128)(2,1)S(1)}, u32[]{:S(2)}, u32[]{:S(2)}) %collective-permute-start.4) | collective-permute-done | bytes 147488 | tf_op jit(solution)/shard_map/ppermute | solution.py:297
  18.3 0.0 collective-permute-done.5.refs_7_
  18.3 0.0 collective-permute-done.6.refs_8_
  18.3 0.0 copy-start.1
  18.3 1.6 %shard_map.48 = (bf16[2,48,384]{2,1,0:T(8,128)(2,1)S(1)}, bf16[2,48,384]{2,1,0:T(8,128)(2,1)S(1)}, bf16[2,48,384]{2,1,0:T(8,128)(2,1)S(1)}, bf16[2,48,384]{2,1,0...) custom-call(s32[8]{0:T(128)S(1)} %copy-done.2, ...), custom_call_target="tpu_custom_call" | custom-call | bytes 2949152 | tf_op jit(solution)/shard_map/pallas_call | solution.py:269
  19.9 0.8 %collective-permute-start.9 = (bf16[2,48,384]{2,1,0:T(8,128)(2,1)S(1)}, bf16[2,48,384]{2,1,0:T(8,128)(2,1)S(1)}, u32[]{:S(2)}, u32[]{:S(2)}) collective-permute-start(bf16[2,48,384]{2,1,0:T(8,128)(2,1)S(1)} %get-tuple-element.46), channel_id=1, source_target_pairs={{0,4},{4,0},{8,12},{12,8},{16,20},{20,16},{24,28},{28,24},{1,5},{5... | collective-permute-start | bytes 221192 | tf_op jit(solution)/shard_map/ppermute | solution.py:297
  20.7 1.5 %collective-permute-start.10 = (bf16[2,48,384]{2,1,0:T(8,128)(2,1)S(1)}, bf16[2,48,384]{2,1,0:T(8,128)(2,1)S(1)}, u32[]{:S(2)}, u32[]{:S(2)}) collective-permute-start(bf16[2,48,384]{2,1,0:T(8,128)(2,1)S(1)} %get-tuple-element.47), channel_id=1, source_target_pairs={{0,8},{4,12},{8,0},{12,4},{16,24},{20,28},{24,16},{28,20},{1,9},{5... | collective-permute-start | bytes 221192 | tf_op jit(solution)/shard_map/ppermute | solution.py:297
  22.1 0.0 collective-permute-start.11
  22.1 1.5 %collective-permute-start.14 = (bf16[2,48,384]{2,1,0:T(8,128)(2,1)S(1)}, bf16[2,48,384]{2,1,0:T(8,128)(2,1)S(1)}, u32[]{:S(2)}, u32[]{:S(2)}) collective-permute-start(bf16[2,48,384]{2,1,0:T(8,128)(2,1)S(1)} %get-tuple-element.49), channel_id=1, source_target_pairs={{0,16},{4,20},{8,24},{12,28},{16,0},{20,4},{24,8},{28,12},{1,17},{... | collective-permute-start | bytes 221192 | tf_op jit(solution)/shard_map/ppermute | solution.py:297
  23.7 0.0 collective-permute-done.9.refs_1_
  23.7 0.5 collective-permute-start.15
  24.2 0.9 %collective-permute-done.10.refs_2_ = bf16[2,48,384]{2,1,0:T(8,128)(2,1)S(1)} collective-permute-done((bf16[2,48,384]{2,1,0:T(8,128)(2,1)S(1)}, bf16[2,48,384]{2,1,0:T(8,128)(2,1)S(1)}, u32[]{:S(2)}, u32[]{:S(2)}) %collective-permute-start.10) | collective-permute-done | bytes 73760 | tf_op jit(solution)/shard_map/ppermute | solution.py:297
  25.0 3.2 %collective-permute-start.16 = (bf16[2,48,384]{2,1,0:T(8,128)(2,1)S(1)}, bf16[2,48,384]{2,1,0:T(8,128)(2,1)S(1)}, u32[]{:S(2)}, u32[]{:S(2)}) collective-permute-start(bf16[2,48,384]{2,1,0:T(8,128)(2,1)S(1)} %get-tuple-element.51), channel_id=1, source_target_pairs={{0,24},{4,28},{8,16},{12,20},{16,8},{20,12},{24,0},{28,4},{1,25},{... | collective-permute-start | bytes 221192 | tf_op jit(solution)/shard_map/ppermute | solution.py:297
  28.2 0.0 collective-permute-done.11.refs_3_
  28.2 0.5 collective-permute-start.17
  28.8 0.0 collective-permute-done.14.refs_0_
  28.8 2.4 %collective-permute-start.8 = (bf16[384,384]{1,0:T(8,128)(2,1)S(1)}, bf16[384,384]{1,0:T(8,128)(2,1)S(1)}, u32[]{:S(2)}, u32[]{:S(2)}) collective-permute-start(bf16[384,384]{1,0:T(8,128)(2,1)S(1)} %bitcast.3), channel_id=1, source_target_pairs={{1,2},{2,1},{5,6},{6,5},{9,10},{10,9},{13,14},{14,13},{17,18},{18,... | collective-permute-start | bytes 884744 | tf_op jit(solution)/shard_map/ppermute | solution.py:304
  31.1 0.0 collective-permute-done.15.refs_1_
  31.1 0.1 collective-permute-start.12
  31.2 0.0 collective-permute-done.16.refs_2_
  31.2 3.5 %collective-permute-start.13 = (bf16[2,192,384]{2,1,0:T(8,128)(2,1)S(1)}, bf16[2,192,384]{2,1,0:T(8,128)(2,1)S(1)}, u32[]{:S(2)}, u32[]{:S(2)}) collective-permute-start(bf16[2,192,384]{2,1,0:T(8,128)(2,1)S(1)} %shard_map.50.refs_0_), channel_id=1, source_target_pairs={{1,2},{2,1},{5,6},{6,5},{9,10},{10,9},{13,14},{14,13},{17,18},{18,... | collective-permute-start | bytes 884744 | tf_op jit(solution)/shard_map/ppermute | solution.py:304
  34.7 0.0 collective-permute-done.17.refs_3_
  34.8 0.1 collective-permute-start.18
  34.9 0.0 collective-permute-done.7.up_even
  34.9 2.6 %collective-permute-start.19 = (bf16[2,192,384]{2,1,0:T(8,128)(2,1)S(1)}, bf16[2,192,384]{2,1,0:T(8,128)(2,1)S(1)}, u32[]{:S(2)}, u32[]{:S(2)}) collective-permute-start(bf16[2,192,384]{2,1,0:T(8,128)(2,1)S(1)} %shard_map.52.refs_1_), channel_id=1, source_target_pairs={{1,2},{2,1},{5,6},{6,5},{9,10},{10,9},{13,14},{14,13},{17,18},{18,... | collective-permute-start | bytes 884744 | tf_op jit(solution)/shard_map/ppermute | solution.py:304
  37.5 1.1 %shard_map.53.own = f32[2,384,384]{2,1,0:T(8,128)S(1)} custom-call(bf16[384,384]{1,0:T(8,128)(2,1)S(1)} %bitcast.5, bf16[2,192,384]{2,1,0:T(8,128)(2,1)S(1)} %shard_map.50.refs_0_, bf16[2,192,384]{2,1,0:T(8,128)(2,1)S(1)} %shard_map.52.refs_1_), custom_call_target="tpu_custom_call" | custom-call | flops 452984832 | bytes 2064384 | tf_op jit(solution)/shard_map/pallas_call | solution.py:269
  38.6 1.9 %collective-permute-done.8.up_odd = bf16[384,384]{1,0:T(8,128)(2,1)S(1)} collective-permute-done((bf16[384,384]{1,0:T(8,128)(2,1)S(1)}, bf16[384,384]{1,0:T(8,128)(2,1)S(1)}, u32[]{:S(2)}, u32[]{:S(2)}) %collective-permute-start.8) | collective-permute-done | bytes 294944 | tf_op jit(solution)/shard_map/ppermute | solution.py:304
  40.5 0.4 shard_map.49
  41.0 0.1 collective-permute-done.12.even
  41.1 5.8 %collective-permute-done.13.odd = bf16[2,192,384]{2,1,0:T(8,128)(2,1)S(1)} collective-permute-done((bf16[2,192,384]{2,1,0:T(8,128)(2,1)S(1)}, bf16[2,192,384]{2,1,0:T(8,128)(2,1)S(1)}, u32[]{:S(2)}, u32[]{:S(2)}) %collective-permute-start.13) | collective-permute-done | bytes 294944 | tf_op jit(solution)/shard_map/ppermute | solution.py:304
  46.9 0.5 shard_map.51.begun
  47.4 0.0 collective-permute-done.18.even
  47.4 4.5 %collective-permute-done.19.odd = bf16[2,192,384]{2,1,0:T(8,128)(2,1)S(1)} collective-permute-done((bf16[2,192,384]{2,1,0:T(8,128)(2,1)S(1)}, bf16[2,192,384]{2,1,0:T(8,128)(2,1)S(1)}, u32[]{:S(2)}, u32[]{:S(2)}) %collective-permute-start.19) | collective-permute-done | bytes 294944 | tf_op jit(solution)/shard_map/ppermute | solution.py:304
  51.8 1.2 %shard_map.54 = (bf16[2,48,384]{2,1,0:T(8,128)(2,1)S(1)}, bf16[2,48,384]{2,1,0:T(8,128)(2,1)S(1)}, bf16[2,48,384]{2,1,0:T(8,128)(2,1)S(1)}, bf16[2,48,384]{2,1,0...) custom-call(bf16[768,384]{1,0:T(8,128)(2,1)S(1)} %get-tuple-element., ...), custom_call_target="tpu_custom_call" | custom-call | flops 679477248 | bytes 5603328 | tf_op jit(solution)/shard_map/pallas_call | solution.py:269
  53.0 2.0 %collective-permute-start.20 = (bf16[2,48,384]{2,1,0:T(8,128)(2,1)S(1)}, bf16[2,48,384]{2,1,0:T(8,128)(2,1)S(1)}, u32[]{:S(2)}, u32[]{:S(2)}) collective-permute-start(bf16[2,48,384]{2,1,0:T(8,128)(2,1)S(1)} %get-tuple-element.54), channel_id=1, source_target_pairs={{0,8},{4,12},{8,0},{12,4},{16,24},{20,28},{24,16},{28,20},{1,9},{5... | collective-permute-start | bytes 221192 | tf_op jit(solution)/shard_map/ppermute | solution.py:297
  55.0 0.2 collective-permute-start.21
  55.2 1.4 %collective-permute-start.22 = (bf16[2,48,384]{2,1,0:T(8,128)(2,1)S(1)}, bf16[2,48,384]{2,1,0:T(8,128)(2,1)S(1)}, u32[]{:S(2)}, u32[]{:S(2)}) collective-permute-start(bf16[2,48,384]{2,1,0:T(8,128)(2,1)S(1)} %get-tuple-element.56), channel_id=1, source_target_pairs={{0,24},{4,28},{8,16},{12,20},{16,8},{20,12},{24,0},{28,4},{1,25},{... | collective-permute-start | bytes 221192 | tf_op jit(solution)/shard_map/ppermute | solution.py:297
  56.6 0.0 collective-permute-start.23
  56.6 2.1 %collective-permute-start.24 = (bf16[2,48,384]{2,1,0:T(8,128)(2,1)S(1)}, bf16[2,48,384]{2,1,0:T(8,128)(2,1)S(1)}, u32[]{:S(2)}, u32[]{:S(2)}) collective-permute-start(bf16[2,48,384]{2,1,0:T(8,128)(2,1)S(1)} %get-tuple-element.58), channel_id=1, source_target_pairs={{0,12},{4,8},{8,4},{12,0},{16,28},{20,24},{24,20},{28,16},{1,13},{... | collective-permute-start | bytes 221192 | tf_op jit(solution)/shard_map/ppermute | solution.py:297
  58.6 0.0 collective-permute-done.20.refs_1_
  58.6 0.0 collective-permute-start.25
  58.6 2.3 %collective-permute-done.21.refs_2_ = bf16[2,48,384]{2,1,0:T(8,128)(2,1)S(1)} collective-permute-done((bf16[2,48,384]{2,1,0:T(8,128)(2,1)S(1)}, bf16[2,48,384]{2,1,0:T(8,128)(2,1)S(1)}, u32[]{:S(2)}, u32[]{:S(2)}) %collective-permute-start.21) | collective-permute-done | bytes 73760 | tf_op jit(solution)/shard_map/ppermute | solution.py:297
  61.0 0.0 collective-permute-start.26
  61.0 0.0 collective-permute-done.22.refs_3_
  61.0 0.5 shard_map.55.part
  61.5 0.0 collective-permute-done.23.refs_0_
  61.6 0.0 collective-permute-done.24.refs_1_
  61.6 1.5 %collective-permute-done.25.refs_2_ = bf16[2,48,384]{2,1,0:T(8,128)(2,1)S(1)} collective-permute-done((bf16[2,48,384]{2,1,0:T(8,128)(2,1)S(1)}, bf16[2,48,384]{2,1,0:T(8,128)(2,1)S(1)}, u32[]{:S(2)}, u32[]{:S(2)}) %collective-permute-start.25) | collective-permute-done | bytes 73760 | tf_op jit(solution)/shard_map/ppermute | solution.py:297
  63.0 2.6 %collective-permute-done.26.refs_3_ = bf16[2,48,384]{2,1,0:T(8,128)(2,1)S(1)} collective-permute-done((bf16[2,48,384]{2,1,0:T(8,128)(2,1)S(1)}, bf16[2,48,384]{2,1,0:T(8,128)(2,1)S(1)}, u32[]{:S(2)}, u32[]{:S(2)}) %collective-permute-start.26) | collective-permute-done | bytes 73760 | tf_op jit(solution)/shard_map/ppermute | solution.py:297
  65.6 1.7 %sigma.1 = bf16[2,8,1,48,384]{4,3,2,1,0:T(8,128)(2,1)} custom-call(s32[8]{0:T(128)S(1)} %copy-done.2, f32[2,8,48,384]{3,2,1,0:T(8,128)S(1)} %get-tuple-element.41.lesser, f32[2,8,48,384]{3,2,1,0:T(8,128)S(1)} %shard_map.55.part, bf16[2,48,384]{2,1,0:T(8,128)(2,1)S(1)} %collective-permute-done.23.refs_0_, ...), custom_call_target="tpu_custom_call" | custom-call | tf_op jit(solution)/shard_map/sigma/pallas_call | solution.py:375
  (7 shorter events, 0.1 us)
Async XLA Ops:
  0.0 10.4 %copy-start = (bf16[1,384,384]{2,1,0:T(8,128)(2,1)S(1)}, bf16[1,384,384]{2,1,0:T(8,128)(2,1)}, u32[]{:S(2)}) copy-start(bf16[1,384,384]{2,1,0:T(8,128)(2,1)} %param.6) | copy-start | bytes 884740
  0.0 18.3 %copy-start.2 = (s32[8]{0:T(128)S(1)}, s32[8]{0:T(128)}, u32[]{:S(2)}) copy-start(s32[8]{0:T(128)} %slot_ref.1) | copy-start | bytes 100
  1.3 4.6 %collective-permute-start = (bf16[4,48,384]{2,1,0:T(8,128)(2,1)S(1)}, bf16[4,48,384]{2,1,0:T(8,128)(2,1)S(1)}, u32[]{:S(2)}, u32[]{:S(2)}) collective-permute-start(bf16[4,48,384]{2,1,0:T(8,128)(2,1)S(1)} %get-tuple-element.34), channel_id=1, source_target_pairs={{0,4},{4,0},{8,12},{12,8},{16,20},{20,16},{24,28},{28,24},{1,5},{5... | collective-permute-start | bytes 442376 | tf_op jit(solution)/shard_map/ppermute | solution.py:297
  1.4 7.1 %collective-permute-start.1 = (bf16[4,48,384]{2,1,0:T(8,128)(2,1)S(1)}, bf16[4,48,384]{2,1,0:T(8,128)(2,1)S(1)}, u32[]{:S(2)}, u32[]{:S(2)}) collective-permute-start(bf16[4,48,384]{2,1,0:T(8,128)(2,1)S(1)} %get-tuple-element.35), channel_id=1, source_target_pairs={{0,8},{4,12},{8,0},{12,4},{16,24},{20,28},{24,16},{28,20},{1,9},{5... | collective-permute-start | bytes 442376 | tf_op jit(solution)/shard_map/ppermute | solution.py:297
  3.0 7.4 %collective-permute-start.2 = (bf16[4,48,384]{2,1,0:T(8,128)(2,1)S(1)}, bf16[4,48,384]{2,1,0:T(8,128)(2,1)S(1)}, u32[]{:S(2)}, u32[]{:S(2)}) collective-permute-start(bf16[4,48,384]{2,1,0:T(8,128)(2,1)S(1)} %get-tuple-element.36), channel_id=1, source_target_pairs={{0,12},{4,8},{8,4},{12,0},{16,28},{20,24},{24,20},{28,16},{1,13},{... | collective-permute-start | bytes 442376 | tf_op jit(solution)/shard_map/ppermute | solution.py:297
  3.3 8.7 %collective-permute-start.3 = (bf16[4,48,384]{2,1,0:T(8,128)(2,1)S(1)}, bf16[4,48,384]{2,1,0:T(8,128)(2,1)S(1)}, u32[]{:S(2)}, u32[]{:S(2)}) collective-permute-start(bf16[4,48,384]{2,1,0:T(8,128)(2,1)S(1)} %get-tuple-element.37), channel_id=1, source_target_pairs={{0,16},{4,20},{8,24},{12,28},{16,0},{20,4},{24,8},{28,12},{1,17},{... | collective-permute-start | bytes 442376 | tf_op jit(solution)/shard_map/ppermute | solution.py:297
  4.8 13.5 %collective-permute-start.4 = (bf16[4,48,384]{2,1,0:T(8,128)(2,1)S(1)}, bf16[4,48,384]{2,1,0:T(8,128)(2,1)S(1)}, u32[]{:S(2)}, u32[]{:S(2)}) collective-permute-start(bf16[4,48,384]{2,1,0:T(8,128)(2,1)S(1)} %get-tuple-element.38), channel_id=1, source_target_pairs={{0,20},{4,16},{8,28},{12,24},{16,4},{20,0},{24,12},{28,8},{1,21},{... | collective-permute-start | bytes 442376 | tf_op jit(solution)/shard_map/ppermute | solution.py:297
  6.0 12.3 %collective-permute-start.5 = (bf16[4,48,384]{2,1,0:T(8,128)(2,1)S(1)}, bf16[4,48,384]{2,1,0:T(8,128)(2,1)S(1)}, u32[]{:S(2)}, u32[]{:S(2)}) collective-permute-start(bf16[4,48,384]{2,1,0:T(8,128)(2,1)S(1)} %get-tuple-element.39), channel_id=1, source_target_pairs={{0,24},{4,28},{8,16},{12,20},{16,8},{20,12},{24,0},{28,4},{1,25},{... | collective-permute-start | bytes 442376 | tf_op jit(solution)/shard_map/ppermute | solution.py:297
  8.5 9.7 %collective-permute-start.6 = (bf16[4,48,384]{2,1,0:T(8,128)(2,1)S(1)}, bf16[4,48,384]{2,1,0:T(8,128)(2,1)S(1)}, u32[]{:S(2)}, u32[]{:S(2)}) collective-permute-start(bf16[4,48,384]{2,1,0:T(8,128)(2,1)S(1)} %get-tuple-element.40), channel_id=1, source_target_pairs={{0,28},{4,24},{8,20},{12,16},{16,12},{20,8},{24,4},{28,0},{1,29},{... | collective-permute-start | bytes 442376 | tf_op jit(solution)/shard_map/ppermute | solution.py:297
  10.4 24.5 %collective-permute-start.7 = (bf16[384,384]{1,0:T(8,128)(2,1)S(1)}, bf16[384,384]{1,0:T(8,128)(2,1)S(1)}, u32[]{:S(2)}, u32[]{:S(2)}) collective-permute-start(bf16[384,384]{1,0:T(8,128)(2,1)S(1)} %bitcast.2), channel_id=1, source_target_pairs={{0,1},{1,0},{2,3},{3,2},{4,5},{5,4},{6,7},{7,6},{8,9},{9,8},{10,11... | collective-permute-start | bytes 884744 | tf_op jit(solution)/shard_map/ppermute | solution.py:304
  18.3 19.3 %copy-start.1 = (bf16[1,384,384]{2,1,0:T(8,128)(2,1)S(1)}, bf16[1,384,384]{2,1,0:T(8,128)(2,1)}, u32[]{:S(2)}) copy-start(bf16[1,384,384]{2,1,0:T(8,128)(2,1)} %param.5) | copy-start | bytes 884740
  19.9 3.8 %collective-permute-start.9 = (bf16[2,48,384]{2,1,0:T(8,128)(2,1)S(1)}, bf16[2,48,384]{2,1,0:T(8,128)(2,1)S(1)}, u32[]{:S(2)}, u32[]{:S(2)}) collective-permute-start(bf16[2,48,384]{2,1,0:T(8,128)(2,1)S(1)} %get-tuple-element.46), channel_id=1, source_target_pairs={{0,4},{4,0},{8,12},{12,8},{16,20},{20,16},{24,28},{28,24},{1,5},{5... | collective-permute-start | bytes 221192 | tf_op jit(solution)/shard_map/ppermute | solution.py:297
  20.7 4.4 %collective-permute-start.10 = (bf16[2,48,384]{2,1,0:T(8,128)(2,1)S(1)}, bf16[2,48,384]{2,1,0:T(8,128)(2,1)S(1)}, u32[]{:S(2)}, u32[]{:S(2)}) collective-permute-start(bf16[2,48,384]{2,1,0:T(8,128)(2,1)S(1)} %get-tuple-element.47), channel_id=1, source_target_pairs={{0,8},{4,12},{8,0},{12,4},{16,24},{20,28},{24,16},{28,20},{1,9},{5... | collective-permute-start | bytes 221192 | tf_op jit(solution)/shard_map/ppermute | solution.py:297
  22.1 6.1 %collective-permute-start.11 = (bf16[2,48,384]{2,1,0:T(8,128)(2,1)S(1)}, bf16[2,48,384]{2,1,0:T(8,128)(2,1)S(1)}, u32[]{:S(2)}, u32[]{:S(2)}) collective-permute-start(bf16[2,48,384]{2,1,0:T(8,128)(2,1)S(1)} %get-tuple-element.48), channel_id=1, source_target_pairs={{0,12},{4,8},{8,4},{12,0},{16,28},{20,24},{24,20},{28,16},{1,13},{... | collective-permute-start | bytes 221192 | tf_op jit(solution)/shard_map/ppermute | solution.py:297
  22.1 6.6 %collective-permute-start.14 = (bf16[2,48,384]{2,1,0:T(8,128)(2,1)S(1)}, bf16[2,48,384]{2,1,0:T(8,128)(2,1)S(1)}, u32[]{:S(2)}, u32[]{:S(2)}) collective-permute-start(bf16[2,48,384]{2,1,0:T(8,128)(2,1)S(1)} %get-tuple-element.49), channel_id=1, source_target_pairs={{0,16},{4,20},{8,24},{12,28},{16,0},{20,4},{24,8},{28,12},{1,17},{... | collective-permute-start | bytes 221192 | tf_op jit(solution)/shard_map/ppermute | solution.py:297
  23.7 7.5 %collective-permute-start.15 = (bf16[2,48,384]{2,1,0:T(8,128)(2,1)S(1)}, bf16[2,48,384]{2,1,0:T(8,128)(2,1)S(1)}, u32[]{:S(2)}, u32[]{:S(2)}) collective-permute-start(bf16[2,48,384]{2,1,0:T(8,128)(2,1)S(1)} %get-tuple-element.50), channel_id=1, source_target_pairs={{0,20},{4,16},{8,28},{12,24},{16,4},{20,0},{24,12},{28,8},{1,21},{... | collective-permute-start | bytes 221192 | tf_op jit(solution)/shard_map/ppermute | solution.py:297
  25.0 6.2 %collective-permute-start.16 = (bf16[2,48,384]{2,1,0:T(8,128)(2,1)S(1)}, bf16[2,48,384]{2,1,0:T(8,128)(2,1)S(1)}, u32[]{:S(2)}, u32[]{:S(2)}) collective-permute-start(bf16[2,48,384]{2,1,0:T(8,128)(2,1)S(1)} %get-tuple-element.51), channel_id=1, source_target_pairs={{0,24},{4,28},{8,16},{12,20},{16,8},{20,12},{24,0},{28,4},{1,25},{... | collective-permute-start | bytes 221192 | tf_op jit(solution)/shard_map/ppermute | solution.py:297
  28.2 6.5 %collective-permute-start.17 = (bf16[2,48,384]{2,1,0:T(8,128)(2,1)S(1)}, bf16[2,48,384]{2,1,0:T(8,128)(2,1)S(1)}, u32[]{:S(2)}, u32[]{:S(2)}) collective-permute-start(bf16[2,48,384]{2,1,0:T(8,128)(2,1)S(1)} %get-tuple-element.52), channel_id=1, source_target_pairs={{0,28},{4,24},{8,20},{12,16},{16,12},{20,8},{24,4},{28,0},{1,29},{... | collective-permute-start | bytes 221192 | tf_op jit(solution)/shard_map/ppermute | solution.py:297
  28.8 11.8 %collective-permute-start.8 = (bf16[384,384]{1,0:T(8,128)(2,1)S(1)}, bf16[384,384]{1,0:T(8,128)(2,1)S(1)}, u32[]{:S(2)}, u32[]{:S(2)}) collective-permute-start(bf16[384,384]{1,0:T(8,128)(2,1)S(1)} %bitcast.3), channel_id=1, source_target_pairs={{1,2},{2,1},{5,6},{6,5},{9,10},{10,9},{13,14},{14,13},{17,18},{18,... | collective-permute-start | bytes 884744 | tf_op jit(solution)/shard_map/ppermute | solution.py:304
  31.1 9.9 %collective-permute-start.12 = (bf16[2,192,384]{2,1,0:T(8,128)(2,1)S(1)}, bf16[2,192,384]{2,1,0:T(8,128)(2,1)S(1)}, u32[]{:S(2)}, u32[]{:S(2)}) collective-permute-start(bf16[2,192,384]{2,1,0:T(8,128)(2,1)S(1)} %shard_map.50.refs_0_), channel_id=1, source_target_pairs={{0,1},{1,0},{2,3},{3,2},{4,5},{5,4},{6,7},{7,6},{8,9},{9,8},{10,11... | collective-permute-start | bytes 884744 | tf_op jit(solution)/shard_map/ppermute | solution.py:304
  31.2 15.6 %collective-permute-start.13 = (bf16[2,192,384]{2,1,0:T(8,128)(2,1)S(1)}, bf16[2,192,384]{2,1,0:T(8,128)(2,1)S(1)}, u32[]{:S(2)}, u32[]{:S(2)}) collective-permute-start(bf16[2,192,384]{2,1,0:T(8,128)(2,1)S(1)} %shard_map.50.refs_0_), channel_id=1, source_target_pairs={{1,2},{2,1},{5,6},{6,5},{9,10},{10,9},{13,14},{14,13},{17,18},{18,... | collective-permute-start | bytes 884744 | tf_op jit(solution)/shard_map/ppermute | solution.py:304
  34.8 12.6 %collective-permute-start.18 = (bf16[2,192,384]{2,1,0:T(8,128)(2,1)S(1)}, bf16[2,192,384]{2,1,0:T(8,128)(2,1)S(1)}, u32[]{:S(2)}, u32[]{:S(2)}) collective-permute-start(bf16[2,192,384]{2,1,0:T(8,128)(2,1)S(1)} %shard_map.52.refs_1_), channel_id=1, source_target_pairs={{0,1},{1,0},{2,3},{3,2},{4,5},{5,4},{6,7},{7,6},{8,9},{9,8},{10,11... | collective-permute-start | bytes 884744 | tf_op jit(solution)/shard_map/ppermute | solution.py:304
  34.9 16.9 %collective-permute-start.19 = (bf16[2,192,384]{2,1,0:T(8,128)(2,1)S(1)}, bf16[2,192,384]{2,1,0:T(8,128)(2,1)S(1)}, u32[]{:S(2)}, u32[]{:S(2)}) collective-permute-start(bf16[2,192,384]{2,1,0:T(8,128)(2,1)S(1)} %shard_map.52.refs_1_), channel_id=1, source_target_pairs={{1,2},{2,1},{5,6},{6,5},{9,10},{10,9},{13,14},{14,13},{17,18},{18,... | collective-permute-start | bytes 884744 | tf_op jit(solution)/shard_map/ppermute | solution.py:304
  53.0 5.6 %collective-permute-start.20 = (bf16[2,48,384]{2,1,0:T(8,128)(2,1)S(1)}, bf16[2,48,384]{2,1,0:T(8,128)(2,1)S(1)}, u32[]{:S(2)}, u32[]{:S(2)}) collective-permute-start(bf16[2,48,384]{2,1,0:T(8,128)(2,1)S(1)} %get-tuple-element.54), channel_id=1, source_target_pairs={{0,8},{4,12},{8,0},{12,4},{16,24},{20,28},{24,16},{28,20},{1,9},{5... | collective-permute-start | bytes 221192 | tf_op jit(solution)/shard_map/ppermute | solution.py:297
  55.0 5.9 %collective-permute-start.21 = (bf16[2,48,384]{2,1,0:T(8,128)(2,1)S(1)}, bf16[2,48,384]{2,1,0:T(8,128)(2,1)S(1)}, u32[]{:S(2)}, u32[]{:S(2)}) collective-permute-start(bf16[2,48,384]{2,1,0:T(8,128)(2,1)S(1)} %get-tuple-element.55), channel_id=1, source_target_pairs={{0,16},{4,20},{8,24},{12,28},{16,0},{20,4},{24,8},{28,12},{1,17},{... | collective-permute-start | bytes 221192 | tf_op jit(solution)/shard_map/ppermute | solution.py:297
  55.2 5.8 %collective-permute-start.22 = (bf16[2,48,384]{2,1,0:T(8,128)(2,1)S(1)}, bf16[2,48,384]{2,1,0:T(8,128)(2,1)S(1)}, u32[]{:S(2)}, u32[]{:S(2)}) collective-permute-start(bf16[2,48,384]{2,1,0:T(8,128)(2,1)S(1)} %get-tuple-element.56), channel_id=1, source_target_pairs={{0,24},{4,28},{8,16},{12,20},{16,8},{20,12},{24,0},{28,4},{1,25},{... | collective-permute-start | bytes 221192 | tf_op jit(solution)/shard_map/ppermute | solution.py:297
  56.6 5.0 %collective-permute-start.23 = (bf16[2,48,384]{2,1,0:T(8,128)(2,1)S(1)}, bf16[2,48,384]{2,1,0:T(8,128)(2,1)S(1)}, u32[]{:S(2)}, u32[]{:S(2)}) collective-permute-start(bf16[2,48,384]{2,1,0:T(8,128)(2,1)S(1)} %get-tuple-element.57), channel_id=1, source_target_pairs={{0,4},{4,0},{8,12},{12,8},{16,20},{20,16},{24,28},{28,24},{1,5},{5... | collective-permute-start | bytes 221192 | tf_op jit(solution)/shard_map/ppermute | solution.py:297
  56.6 5.0 %collective-permute-start.24 = (bf16[2,48,384]{2,1,0:T(8,128)(2,1)S(1)}, bf16[2,48,384]{2,1,0:T(8,128)(2,1)S(1)}, u32[]{:S(2)}, u32[]{:S(2)}) collective-permute-start(bf16[2,48,384]{2,1,0:T(8,128)(2,1)S(1)} %get-tuple-element.58), channel_id=1, source_target_pairs={{0,12},{4,8},{8,4},{12,0},{16,28},{20,24},{24,20},{28,16},{1,13},{... | collective-permute-start | bytes 221192 | tf_op jit(solution)/shard_map/ppermute | solution.py:297
  58.6 4.4 %collective-permute-start.25 = (bf16[2,48,384]{2,1,0:T(8,128)(2,1)S(1)}, bf16[2,48,384]{2,1,0:T(8,128)(2,1)S(1)}, u32[]{:S(2)}, u32[]{:S(2)}) collective-permute-start(bf16[2,48,384]{2,1,0:T(8,128)(2,1)S(1)} %get-tuple-element.59), channel_id=1, source_target_pairs={{0,20},{4,16},{8,28},{12,24},{16,4},{20,0},{24,12},{28,8},{1,21},{... | collective-permute-start | bytes 221192 | tf_op jit(solution)/shard_map/ppermute | solution.py:297
  61.0 4.7 %collective-permute-start.26 = (bf16[2,48,384]{2,1,0:T(8,128)(2,1)S(1)}, bf16[2,48,384]{2,1,0:T(8,128)(2,1)S(1)}, u32[]{:S(2)}, u32[]{:S(2)}) collective-permute-start(bf16[2,48,384]{2,1,0:T(8,128)(2,1)S(1)} %get-tuple-element.60), channel_id=1, source_target_pairs={{0,28},{4,24},{8,20},{12,16},{16,12},{20,8},{24,4},{28,0},{1,29},{... | collective-permute-start | bytes 221192 | tf_op jit(solution)/shard_map/ppermute | solution.py:297

commit v5 on v4

--- a/solution.py
+++ b/solution.py
@@ -41,7 +41,7 @@
         body((pl.ds(row, height), pl.ds(col, LANES)))
         return carry
 
-    lax.fori_loop(0, down * across, step, 0, unroll=across if down == 1 else 2)
+    lax.fori_loop(0, down * across, step, 0, unroll=across)
 
 
 def sum_of(terms):
@@ -476,7 +476,8 @@
 
 
 def sequence_far(parts):
-    return (*(j + core for j in (6, 4, 2) if j < parts for core in range(2)), *range(8, parts), 1)
+    chips = [j for j in (6, 4, 2) if j < parts] + list(range(8, parts, 2))
+    return (*(j + core for j in chips for core in range(2)), 1)
 
 
 def solution(mesh):

time: 67.6 us -> 67.5 us (level)
  the two profiles are of different devices: /device:TPU:16 before, /device:TPU:8 now
where the time goes in v5:
time: 67.5 us; the launch traced here: 67.4 us
  starting transfers between devices  30.5 us (45%)
  waiting for transfers between devices  27.3 us (40%)
  Pallas kernels  9.34 us (14%)
    ppermute x21, starting transfers between devices, swap(): lax.ppermute(pieces[j], 'energy', [(i, i ^ j) for i in range(parts)])  20.6 us
    ppermute x21, waiting for transfers between devices, swap(): lax.ppermute(pieces[j], 'energy', [(i, i ^ j) for i in range(parts)])  15.8 us
    ppermute x6, waiting for transfers between devices, meet(): lax.ppermute(value, 'space', [p for i in lows for p in ((i, i + 1), (i +...  11.4 us
    ppermute x6, starting transfers between devices, meet(): lax.ppermute(value, 'space', [p for i in lows for p in ((i, i + 1), (i +...  9.93 us
    pallas_call x8, Pallas kernels, call(): pl.pallas_call(kernel, out_shape=outs, in_specs=[smem()] * tables + [vmem...  5.27 us
    pallas_call x2, Pallas kernels, take(): pl.pallas_call(functools.partial(cut_kernel, order, partners), out_shape=...  2.33 us
    pallas_call x1, Pallas kernels, direct(): pl.pallas_call(functools.partial(sigma_kernel, order, scaling), name='sig...  1.74 us
  transfers between devices with their start and end apart: 27, of which 10 were waited for; matrix products, arithmetic and copies ran while one was open for 0% of the time, Pallas kernels for 8%

profile of v5, /device:TPU:8, one launch (start us, length us, event | category | flops | bytes accessed | tf_op | source)
XLA Modules:
  0.0 67.4 jit_solution(2866485546324420230)
XLA Ops:
  0.0 1.3 %shard_map.46 = (bf16[4,48,384]{2,1,0:T(8,128)(2,1)S(1)}, bf16[4,48,384]{2,1,0:T(8,128)(2,1)S(1)}, bf16[4,48,384]{2,1,0:T(8,128)(2,1)S(1)}, bf16[4,48,384]{2,1,0...) custom-call(bf16[4,1,1,384,384]{4,3,2,1,0:T(8,128)(2,1)} %green.3), custom_call_target="tpu_custom_call" | custom-call | tf_op jit(solution)/shard_map/pallas_call | solution.py:308
  1.3 0.1 collective-permute-start
  1.4 1.6 %collective-permute-start.1 = (bf16[4,48,384]{2,1,0:T(8,128)(2,1)S(1)}, bf16[4,48,384]{2,1,0:T(8,128)(2,1)S(1)}, u32[]{:S(2)}, u32[]{:S(2)}) collective-permute-start(bf16[4,48,384]{2,1,0:T(8,128)(2,1)S(1)} %get-tuple-element.35), channel_id=1, source_target_pairs={{0,8},{4,12},{8,0},{12,4},{16,24},{20,28},{24,16},{28,20},{1,9},{5... | collective-permute-start | bytes 442376 | tf_op jit(solution)/shard_map/ppermute | solution.py:297
  3.0 0.3 collective-permute-start.2
  3.3 1.5 %collective-permute-start.3 = (bf16[4,48,384]{2,1,0:T(8,128)(2,1)S(1)}, bf16[4,48,384]{2,1,0:T(8,128)(2,1)S(1)}, u32[]{:S(2)}, u32[]{:S(2)}) collective-permute-start(bf16[4,48,384]{2,1,0:T(8,128)(2,1)S(1)} %get-tuple-element.37), channel_id=1, source_target_pairs={{0,16},{4,20},{8,24},{12,28},{16,0},{20,4},{24,8},{28,12},{1,17},{... | collective-permute-start | bytes 442376 | tf_op jit(solution)/shard_map/ppermute | solution.py:297
  4.8 0.2 collective-permute-start.4
  5.0 1.0 %shard_map.47 = (bf16[4,48,384]{2,1,0:T(8,128)(2,1)S(1)}, bf16[4,48,384]{2,1,0:T(8,128)(2,1)S(1)}) custom-call(bf16[4,1,1,384,384]{4,3,2,1,0:T(8,128)(2,1)} %green.3), custom_call_target="tpu_custom_call" | custom-call | tf_op jit(solution)/shard_map/pallas_call | solution.py:308
  6.0 0.0 collective-permute-done.refs_2_
  6.0 2.5 %collective-permute-start.5 = (bf16[4,48,384]{2,1,0:T(8,128)(2,1)S(1)}, bf16[4,48,384]{2,1,0:T(8,128)(2,1)S(1)}, u32[]{:S(2)}, u32[]{:S(2)}) collective-permute-start(bf16[4,48,384]{2,1,0:T(8,128)(2,1)S(1)} %get-tuple-element.39), channel_id=1, source_target_pairs={{0,24},{4,28},{8,16},{12,20},{16,8},{20,12},{24,0},{28,4},{1,25},{... | collective-permute-start | bytes 442376 | tf_op jit(solution)/shard_map/ppermute | solution.py:297
  8.5 0.0 collective-permute-done.1.refs_3_
  8.5 0.8 %collective-permute-start.6 = (bf16[4,48,384]{2,1,0:T(8,128)(2,1)S(1)}, bf16[4,48,384]{2,1,0:T(8,128)(2,1)S(1)}, u32[]{:S(2)}, u32[]{:S(2)}) collective-permute-start(bf16[4,48,384]{2,1,0:T(8,128)(2,1)S(1)} %get-tuple-element.40), channel_id=1, source_target_pairs={{0,28},{4,24},{8,20},{12,16},{16,12},{20,8},{24,4},{28,0},{1,29},{... | collective-permute-start | bytes 442376 | tf_op jit(solution)/shard_map/ppermute | solution.py:297
  9.3 1.1 %collective-permute-done.2.refs_4_ = bf16[4,48,384]{2,1,0:T(8,128)(2,1)S(1)} collective-permute-done((bf16[4,48,384]{2,1,0:T(8,128)(2,1)S(1)}, bf16[4,48,384]{2,1,0:T(8,128)(2,1)S(1)}, u32[]{:S(2)}, u32[]{:S(2)}) %collective-permute-start.2) | collective-permute-done | bytes 147488 | tf_op jit(solution)/shard_map/ppermute | solution.py:297
  10.4 0.4 collective-permute-start.7
  10.8 0.0 collective-permute-done.3.refs_5_
  10.8 7.4 %collective-permute-done.4.refs_6_ = bf16[4,48,384]{2,1,0:T(8,128)(2,1)S(1)} collective-permute-done((bf16[4,48,384]{2,1,0:T(8,128)(2,1)S(1)}, bf16[4,48,384]{2,1,0:T(8,128)(2,1)S(1)}, u32[]{:S(2)}, u32[]{:S(2)}) %collective-permute-start.4) | collective-permute-done | bytes 147488 | tf_op jit(solution)/shard_map/ppermute | solution.py:297
  18.3 0.0 collective-permute-done.5.refs_7_
  18.3 0.0 collective-permute-done.6.refs_8_
  18.3 0.0 copy-start.1
  18.3 1.5 %shard_map.48 = (bf16[2,48,384]{2,1,0:T(8,128)(2,1)S(1)}, bf16[2,48,384]{2,1,0:T(8,128)(2,1)S(1)}, bf16[2,48,384]{2,1,0:T(8,128)(2,1)S(1)}, bf16[2,48,384]{2,1,0...) custom-call(s32[8]{0:T(128)S(1)} %copy-done.2, ...), custom_call_target="tpu_custom_call" | custom-call | bytes 2949152 | tf_op jit(solution)/shard_map/pallas_call | solution.py:269
  19.8 0.8 %collective-permute-start.9 = (bf16[2,48,384]{2,1,0:T(8,128)(2,1)S(1)}, bf16[2,48,384]{2,1,0:T(8,128)(2,1)S(1)}, u32[]{:S(2)}, u32[]{:S(2)}) collective-permute-start(bf16[2,48,384]{2,1,0:T(8,128)(2,1)S(1)} %get-tuple-element.46), channel_id=1, source_target_pairs={{0,4},{4,0},{8,12},{12,8},{16,20},{20,16},{24,28},{28,24},{1,5},{5... | collective-permute-start | bytes 221192 | tf_op jit(solution)/shard_map/ppermute | solution.py:297
  20.6 1.5 %collective-permute-start.10 = (bf16[2,48,384]{2,1,0:T(8,128)(2,1)S(1)}, bf16[2,48,384]{2,1,0:T(8,128)(2,1)S(1)}, u32[]{:S(2)}, u32[]{:S(2)}) collective-permute-start(bf16[2,48,384]{2,1,0:T(8,128)(2,1)S(1)} %get-tuple-element.47), channel_id=1, source_target_pairs={{0,8},{4,12},{8,0},{12,4},{16,24},{20,28},{24,16},{28,20},{1,9},{5... | collective-permute-start | bytes 221192 | tf_op jit(solution)/shard_map/ppermute | solution.py:297
  22.1 0.0 collective-permute-start.11
  22.1 1.5 %collective-permute-start.14 = (bf16[2,48,384]{2,1,0:T(8,128)(2,1)S(1)}, bf16[2,48,384]{2,1,0:T(8,128)(2,1)S(1)}, u32[]{:S(2)}, u32[]{:S(2)}) collective-permute-start(bf16[2,48,384]{2,1,0:T(8,128)(2,1)S(1)} %get-tuple-element.49), channel_id=1, source_target_pairs={{0,16},{4,20},{8,24},{12,28},{16,0},{20,4},{24,8},{28,12},{1,17},{... | collective-permute-start | bytes 221192 | tf_op jit(solution)/shard_map/ppermute | solution.py:297
  23.6 0.0 collective-permute-done.9.refs_1_
  23.6 0.5 collective-permute-start.15
  24.1 0.9 %collective-permute-done.10.refs_2_ = bf16[2,48,384]{2,1,0:T(8,128)(2,1)S(1)} collective-permute-done((bf16[2,48,384]{2,1,0:T(8,128)(2,1)S(1)}, bf16[2,48,384]{2,1,0:T(8,128)(2,1)S(1)}, u32[]{:S(2)}, u32[]{:S(2)}) %collective-permute-start.10) | collective-permute-done | bytes 73760 | tf_op jit(solution)/shard_map/ppermute | solution.py:297
  25.0 3.2 %collective-permute-start.16 = (bf16[2,48,384]{2,1,0:T(8,128)(2,1)S(1)}, bf16[2,48,384]{2,1,0:T(8,128)(2,1)S(1)}, u32[]{:S(2)}, u32[]{:S(2)}) collective-permute-start(bf16[2,48,384]{2,1,0:T(8,128)(2,1)S(1)} %get-tuple-element.51), channel_id=1, source_target_pairs={{0,24},{4,28},{8,16},{12,20},{16,8},{20,12},{24,0},{28,4},{1,25},{... | collective-permute-start | bytes 221192 | tf_op jit(solution)/shard_map/ppermute | solution.py:297
  28.2 0.0 collective-permute-done.11.refs_3_
  28.2 0.5 collective-permute-start.17
  28.7 0.0 collective-permute-done.14.refs_0_
  28.7 3.5 %collective-permute-start.8 = (bf16[384,384]{1,0:T(8,128)(2,1)S(1)}, bf16[384,384]{1,0:T(8,128)(2,1)S(1)}, u32[]{:S(2)}, u32[]{:S(2)}) collective-permute-start(bf16[384,384]{1,0:T(8,128)(2,1)S(1)} %bitcast.3), channel_id=1, source_target_pairs={{1,2},{2,1},{5,6},{6,5},{9,10},{10,9},{13,14},{14,13},{17,18},{18,... | collective-permute-start | bytes 884744 | tf_op jit(solution)/shard_map/ppermute | solution.py:304
  32.2 0.0 collective-permute-done.15.refs_1_
  32.2 0.1 collective-permute-start.12
  32.3 0.0 collective-permute-done.16.refs_2_
  32.3 2.4 %collective-permute-start.13 = (bf16[2,192,384]{2,1,0:T(8,128)(2,1)S(1)}, bf16[2,192,384]{2,1,0:T(8,128)(2,1)S(1)}, u32[]{:S(2)}, u32[]{:S(2)}) collective-permute-start(bf16[2,192,384]{2,1,0:T(8,128)(2,1)S(1)} %shard_map.50.refs_0_), channel_id=1, source_target_pairs={{1,2},{2,1},{5,6},{6,5},{9,10},{10,9},{13,14},{14,13},{17,18},{18,... | collective-permute-start | bytes 884744 | tf_op jit(solution)/shard_map/ppermute | solution.py:304
  34.7 0.0 collective-permute-done.17.refs_3_
  34.8 0.4 collective-permute-start.18
  35.1 0.0 collective-permute-done.7.up_even
  35.1 3.2 %collective-permute-start.19 = (bf16[2,192,384]{2,1,0:T(8,128)(2,1)S(1)}, bf16[2,192,384]{2,1,0:T(8,128)(2,1)S(1)}, u32[]{:S(2)}, u32[]{:S(2)}) collective-permute-start(bf16[2,192,384]{2,1,0:T(8,128)(2,1)S(1)} %shard_map.52.refs_1_), channel_id=1, source_target_pairs={{1,2},{2,1},{5,6},{6,5},{9,10},{10,9},{13,14},{14,13},{17,18},{18,... | collective-permute-start | bytes 884744 | tf_op jit(solution)/shard_map/ppermute | solution.py:304
  38.4 1.1 %shard_map.53.own = f32[2,384,384]{2,1,0:T(8,128)S(1)} custom-call(bf16[384,384]{1,0:T(8,128)(2,1)S(1)} %bitcast.5, bf16[2,192,384]{2,1,0:T(8,128)(2,1)S(1)} %shard_map.50.refs_0_, bf16[2,192,384]{2,1,0:T(8,128)(2,1)S(1)} %shard_map.52.refs_1_), custom_call_target="tpu_custom_call" | custom-call | flops 452984832 | bytes 2064384 | tf_op jit(solution)/shard_map/pallas_call | solution.py:269
  39.4 1.1 %collective-permute-done.8.up_odd = bf16[384,384]{1,0:T(8,128)(2,1)S(1)} collective-permute-done((bf16[384,384]{1,0:T(8,128)(2,1)S(1)}, bf16[384,384]{1,0:T(8,128)(2,1)S(1)}, u32[]{:S(2)}, u32[]{:S(2)}) %collective-permute-start.8) | collective-permute-done | bytes 294944 | tf_op jit(solution)/shard_map/ppermute | solution.py:304
  40.5 0.4 shard_map.49
  40.9 1.3 %collective-permute-done.12.even = bf16[2,192,384]{2,1,0:T(8,128)(2,1)S(1)} collective-permute-done((bf16[2,192,384]{2,1,0:T(8,128)(2,1)S(1)}, bf16[2,192,384]{2,1,0:T(8,128)(2,1)S(1)}, u32[]{:S(2)}, u32[]{:S(2)}) %collective-permute-start.12) | collective-permute-done | bytes 294944 | tf_op jit(solution)/shard_map/ppermute | solution.py:304
  42.2 4.6 %collective-permute-done.13.odd = bf16[2,192,384]{2,1,0:T(8,128)(2,1)S(1)} collective-permute-done((bf16[2,192,384]{2,1,0:T(8,128)(2,1)S(1)}, bf16[2,192,384]{2,1,0:T(8,128)(2,1)S(1)}, u32[]{:S(2)}, u32[]{:S(2)}) %collective-permute-start.13) | collective-permute-done | bytes 294944 | tf_op jit(solution)/shard_map/ppermute | solution.py:304
  46.8 0.5 shard_map.51.begun
  47.3 0.0 collective-permute-done.18.even
  47.3 4.5 %collective-permute-done.19.odd = bf16[2,192,384]{2,1,0:T(8,128)(2,1)S(1)} collective-permute-done((bf16[2,192,384]{2,1,0:T(8,128)(2,1)S(1)}, bf16[2,192,384]{2,1,0:T(8,128)(2,1)S(1)}, u32[]{:S(2)}, u32[]{:S(2)}) %collective-permute-start.19) | collective-permute-done | bytes 294944 | tf_op jit(solution)/shard_map/ppermute | solution.py:304
  51.8 1.2 %shard_map.54 = (bf16[2,48,384]{2,1,0:T(8,128)(2,1)S(1)}, bf16[2,48,384]{2,1,0:T(8,128)(2,1)S(1)}, bf16[2,48,384]{2,1,0:T(8,128)(2,1)S(1)}, bf16[2,48,384]{2,1,0...) custom-call(bf16[768,384]{1,0:T(8,128)(2,1)S(1)} %get-tuple-element., ...), custom_call_target="tpu_custom_call" | custom-call | flops 679477248 | bytes 5603328 | tf_op jit(solution)/shard_map/pallas_call | solution.py:269
  53.0 2.0 %collective-permute-start.20 = (bf16[2,48,384]{2,1,0:T(8,128)(2,1)S(1)}, bf16[2,48,384]{2,1,0:T(8,128)(2,1)S(1)}, u32[]{:S(2)}, u32[]{:S(2)}) collective-permute-start(bf16[2,48,384]{2,1,0:T(8,128)(2,1)S(1)} %get-tuple-element.54), channel_id=1, source_target_pairs={{0,8},{4,12},{8,0},{12,4},{16,24},{20,28},{24,16},{28,20},{1,9},{5... | collective-permute-start | bytes 221192 | tf_op jit(solution)/shard_map/ppermute | solution.py:297
  55.0 0.2 collective-permute-start.21
  55.2 1.4 %collective-permute-start.22 = (bf16[2,48,384]{2,1,0:T(8,128)(2,1)S(1)}, bf16[2,48,384]{2,1,0:T(8,128)(2,1)S(1)}, u32[]{:S(2)}, u32[]{:S(2)}) collective-permute-start(bf16[2,48,384]{2,1,0:T(8,128)(2,1)S(1)} %get-tuple-element.56), channel_id=1, source_target_pairs={{0,24},{4,28},{8,16},{12,20},{16,8},{20,12},{24,0},{28,4},{1,25},{... | collective-permute-start | bytes 221192 | tf_op jit(solution)/shard_map/ppermute | solution.py:297
  56.5 0.0 collective-permute-start.23
  56.6 2.1 %collective-permute-start.24 = (bf16[2,48,384]{2,1,0:T(8,128)(2,1)S(1)}, bf16[2,48,384]{2,1,0:T(8,128)(2,1)S(1)}, u32[]{:S(2)}, u32[]{:S(2)}) collective-permute-start(bf16[2,48,384]{2,1,0:T(8,128)(2,1)S(1)} %get-tuple-element.58), channel_id=1, source_target_pairs={{0,12},{4,8},{8,4},{12,0},{16,28},{20,24},{24,20},{28,16},{1,13},{... | collective-permute-start | bytes 221192 | tf_op jit(solution)/shard_map/ppermute | solution.py:297
  58.6 0.0 collective-permute-done.20.refs_1_
  58.6 0.0 collective-permute-start.25
  58.6 2.3 %collective-permute-done.21.refs_2_ = bf16[2,48,384]{2,1,0:T(8,128)(2,1)S(1)} collective-permute-done((bf16[2,48,384]{2,1,0:T(8,128)(2,1)S(1)}, bf16[2,48,384]{2,1,0:T(8,128)(2,1)S(1)}, u32[]{:S(2)}, u32[]{:S(2)}) %collective-permute-start.21) | collective-permute-done | bytes 73760 | tf_op jit(solution)/shard_map/ppermute | solution.py:297
  60.9 0.0 collective-permute-start.26
  61.0 0.0 collective-permute-done.22.refs_3_
  61.0 0.5 shard_map.55.part
  61.5 0.0 collective-permute-done.23.refs_0_
  61.5 0.0 collective-permute-done.24.refs_1_
  61.5 1.5 %collective-permute-done.25.refs_2_ = bf16[2,48,384]{2,1,0:T(8,128)(2,1)S(1)} collective-permute-done((bf16[2,48,384]{2,1,0:T(8,128)(2,1)S(1)}, bf16[2,48,384]{2,1,0:T(8,128)(2,1)S(1)}, u32[]{:S(2)}, u32[]{:S(2)}) %collective-permute-start.25) | collective-permute-done | bytes 73760 | tf_op jit(solution)/shard_map/ppermute | solution.py:297
  63.0 2.6 %collective-permute-done.26.refs_3_ = bf16[2,48,384]{2,1,0:T(8,128)(2,1)S(1)} collective-permute-done((bf16[2,48,384]{2,1,0:T(8,128)(2,1)S(1)}, bf16[2,48,384]{2,1,0:T(8,128)(2,1)S(1)}, u32[]{:S(2)}, u32[]{:S(2)}) %collective-permute-start.26) | collective-permute-done | bytes 73760 | tf_op jit(solution)/shard_map/ppermute | solution.py:297
  65.6 1.7 %sigma.1 = bf16[2,8,1,48,384]{4,3,2,1,0:T(8,128)(2,1)} custom-call(s32[8]{0:T(128)S(1)} %copy-done.2, f32[2,8,48,384]{3,2,1,0:T(8,128)S(1)} %get-tuple-element.41.lesser, f32[2,8,48,384]{3,2,1,0:T(8,128)S(1)} %shard_map.55.part, bf16[2,48,384]{2,1,0:T(8,128)(2,1)S(1)} %collective-permute-done.23.refs_0_, ...), custom_call_target="tpu_custom_call" | custom-call | tf_op jit(solution)/shard_map/sigma/pallas_call | solution.py:375
  (7 shorter events, 0.1 us)
Async XLA Ops:
  0.0 10.4 %copy-start = (bf16[1,384,384]{2,1,0:T(8,128)(2,1)S(1)}, bf16[1,384,384]{2,1,0:T(8,128)(2,1)}, u32[]{:S(2)}) copy-start(bf16[1,384,384]{2,1,0:T(8,128)(2,1)} %param.6) | copy-start | bytes 884740
  0.0 18.3 %copy-start.2 = (s32[8]{0:T(128)S(1)}, s32[8]{0:T(128)}, u32[]{:S(2)}) copy-start(s32[8]{0:T(128)} %slot_ref.1) | copy-start | bytes 100
  1.3 4.6 %collective-permute-start = (bf16[4,48,384]{2,1,0:T(8,128)(2,1)S(1)}, bf16[4,48,384]{2,1,0:T(8,128)(2,1)S(1)}, u32[]{:S(2)}, u32[]{:S(2)}) collective-permute-start(bf16[4,48,384]{2,1,0:T(8,128)(2,1)S(1)} %get-tuple-element.34), channel_id=1, source_target_pairs={{0,4},{4,0},{8,12},{12,8},{16,20},{20,16},{24,28},{28,24},{1,5},{5... | collective-permute-start | bytes 442376 | tf_op jit(solution)/shard_map/ppermute | solution.py:297
  1.4 7.1 %collective-permute-start.1 = (bf16[4,48,384]{2,1,0:T(8,128)(2,1)S(1)}, bf16[4,48,384]{2,1,0:T(8,128)(2,1)S(1)}, u32[]{:S(2)}, u32[]{:S(2)}) collective-permute-start(bf16[4,48,384]{2,1,0:T(8,128)(2,1)S(1)} %get-tuple-element.35), channel_id=1, source_target_pairs={{0,8},{4,12},{8,0},{12,4},{16,24},{20,28},{24,16},{28,20},{1,9},{5... | collective-permute-start | bytes 442376 | tf_op jit(solution)/shard_map/ppermute | solution.py:297
  3.0 7.4 %collective-permute-start.2 = (bf16[4,48,384]{2,1,0:T(8,128)(2,1)S(1)}, bf16[4,48,384]{2,1,0:T(8,128)(2,1)S(1)}, u32[]{:S(2)}, u32[]{:S(2)}) collective-permute-start(bf16[4,48,384]{2,1,0:T(8,128)(2,1)S(1)} %get-tuple-element.36), channel_id=1, source_target_pairs={{0,12},{4,8},{8,4},{12,0},{16,28},{20,24},{24,20},{28,16},{1,13},{... | collective-permute-start | bytes 442376 | tf_op jit(solution)/shard_map/ppermute | solution.py:297
  3.3 7.6 %collective-permute-start.3 = (bf16[4,48,384]{2,1,0:T(8,128)(2,1)S(1)}, bf16[4,48,384]{2,1,0:T(8,128)(2,1)S(1)}, u32[]{:S(2)}, u32[]{:S(2)}) collective-permute-start(bf16[4,48,384]{2,1,0:T(8,128)(2,1)S(1)} %get-tuple-element.37), channel_id=1, source_target_pairs={{0,16},{4,20},{8,24},{12,28},{16,0},{20,4},{24,8},{28,12},{1,17},{... | collective-permute-start | bytes 442376 | tf_op jit(solution)/shard_map/ppermute | solution.py:297
  4.8 13.5 %collective-permute-start.4 = (bf16[4,48,384]{2,1,0:T(8,128)(2,1)S(1)}, bf16[4,48,384]{2,1,0:T(8,128)(2,1)S(1)}, u32[]{:S(2)}, u32[]{:S(2)}) collective-permute-start(bf16[4,48,384]{2,1,0:T(8,128)(2,1)S(1)} %get-tuple-element.38), channel_id=1, source_target_pairs={{0,20},{4,16},{8,28},{12,24},{16,4},{20,0},{24,12},{28,8},{1,21},{... | collective-permute-start | bytes 442376 | tf_op jit(solution)/shard_map/ppermute | solution.py:297
  6.0 12.3 %collective-permute-start.5 = (bf16[4,48,384]{2,1,0:T(8,128)(2,1)S(1)}, bf16[4,48,384]{2,1,0:T(8,128)(2,1)S(1)}, u32[]{:S(2)}, u32[]{:S(2)}) collective-permute-start(bf16[4,48,384]{2,1,0:T(8,128)(2,1)S(1)} %get-tuple-element.39), channel_id=1, source_target_pairs={{0,24},{4,28},{8,16},{12,20},{16,8},{20,12},{24,0},{28,4},{1,25},{... | collective-permute-start | bytes 442376 | tf_op jit(solution)/shard_map/ppermute | solution.py:297
  8.5 9.7 %collective-permute-start.6 = (bf16[4,48,384]{2,1,0:T(8,128)(2,1)S(1)}, bf16[4,48,384]{2,1,0:T(8,128)(2,1)S(1)}, u32[]{:S(2)}, u32[]{:S(2)}) collective-permute-start(bf16[4,48,384]{2,1,0:T(8,128)(2,1)S(1)} %get-tuple-element.40), channel_id=1, source_target_pairs={{0,28},{4,24},{8,20},{12,16},{16,12},{20,8},{24,4},{28,0},{1,29},{... | collective-permute-start | bytes 442376 | tf_op jit(solution)/shard_map/ppermute | solution.py:297
  10.4 24.8 %collective-permute-start.7 = (bf16[384,384]{1,0:T(8,128)(2,1)S(1)}, bf16[384,384]{1,0:T(8,128)(2,1)S(1)}, u32[]{:S(2)}, u32[]{:S(2)}) collective-permute-start(bf16[384,384]{1,0:T(8,128)(2,1)S(1)} %bitcast.2), channel_id=1, source_target_pairs={{0,1},{1,0},{2,3},{3,2},{4,5},{5,4},{6,7},{7,6},{8,9},{9,8},{10,11... | collective-permute-start | bytes 884744 | tf_op jit(solution)/shard_map/ppermute | solution.py:304
  18.3 20.1 %copy-start.1 = (bf16[1,384,384]{2,1,0:T(8,128)(2,1)S(1)}, bf16[1,384,384]{2,1,0:T(8,128)(2,1)}, u32[]{:S(2)}) copy-start(bf16[1,384,384]{2,1,0:T(8,128)(2,1)} %param.5) | copy-start | bytes 884740
  19.8 3.8 %collective-permute-start.9 = (bf16[2,48,384]{2,1,0:T(8,128)(2,1)S(1)}, bf16[2,48,384]{2,1,0:T(8,128)(2,1)S(1)}, u32[]{:S(2)}, u32[]{:S(2)}) collective-permute-start(bf16[2,48,384]{2,1,0:T(8,128)(2,1)S(1)} %get-tuple-element.46), channel_id=1, source_target_pairs={{0,4},{4,0},{8,12},{12,8},{16,20},{20,16},{24,28},{28,24},{1,5},{5... | collective-permute-start | bytes 221192 | tf_op jit(solution)/shard_map/ppermute | solution.py:297
  20.6 4.4 %collective-permute-start.10 = (bf16[2,48,384]{2,1,0:T(8,128)(2,1)S(1)}, bf16[2,48,384]{2,1,0:T(8,128)(2,1)S(1)}, u32[]{:S(2)}, u32[]{:S(2)}) collective-permute-start(bf16[2,48,384]{2,1,0:T(8,128)(2,1)S(1)} %get-tuple-element.47), channel_id=1, source_target_pairs={{0,8},{4,12},{8,0},{12,4},{16,24},{20,28},{24,16},{28,20},{1,9},{5... | collective-permute-start | bytes 221192 | tf_op jit(solution)/shard_map/ppermute | solution.py:297
  22.1 6.1 %collective-permute-start.11 = (bf16[2,48,384]{2,1,0:T(8,128)(2,1)S(1)}, bf16[2,48,384]{2,1,0:T(8,128)(2,1)S(1)}, u32[]{:S(2)}, u32[]{:S(2)}) collective-permute-start(bf16[2,48,384]{2,1,0:T(8,128)(2,1)S(1)} %get-tuple-element.48), channel_id=1, source_target_pairs={{0,12},{4,8},{8,4},{12,0},{16,28},{20,24},{24,20},{28,16},{1,13},{... | collective-permute-start | bytes 221192 | tf_op jit(solution)/shard_map/ppermute | solution.py:297
  22.1 6.6 %collective-permute-start.14 = (bf16[2,48,384]{2,1,0:T(8,128)(2,1)S(1)}, bf16[2,48,384]{2,1,0:T(8,128)(2,1)S(1)}, u32[]{:S(2)}, u32[]{:S(2)}) collective-permute-start(bf16[2,48,384]{2,1,0:T(8,128)(2,1)S(1)} %get-tuple-element.49), channel_id=1, source_target_pairs={{0,16},{4,20},{8,24},{12,28},{16,0},{20,4},{24,8},{28,12},{1,17},{... | collective-permute-start | bytes 221192 | tf_op jit(solution)/shard_map/ppermute | solution.py:297
  23.6 8.6 %collective-permute-start.15 = (bf16[2,48,384]{2,1,0:T(8,128)(2,1)S(1)}, bf16[2,48,384]{2,1,0:T(8,128)(2,1)S(1)}, u32[]{:S(2)}, u32[]{:S(2)}) collective-permute-start(bf16[2,48,384]{2,1,0:T(8,128)(2,1)S(1)} %get-tuple-element.50), channel_id=1, source_target_pairs={{0,20},{4,16},{8,28},{12,24},{16,4},{20,0},{24,12},{28,8},{1,21},{... | collective-permute-start | bytes 221192 | tf_op jit(solution)/shard_map/ppermute | solution.py:297
  25.0 7.3 %collective-permute-start.16 = (bf16[2,48,384]{2,1,0:T(8,128)(2,1)S(1)}, bf16[2,48,384]{2,1,0:T(8,128)(2,1)S(1)}, u32[]{:S(2)}, u32[]{:S(2)}) collective-permute-start(bf16[2,48,384]{2,1,0:T(8,128)(2,1)S(1)} %get-tuple-element.51), channel_id=1, source_target_pairs={{0,24},{4,28},{8,16},{12,20},{16,8},{20,12},{24,0},{28,4},{1,25},{... | collective-permute-start | bytes 221192 | tf_op jit(solution)/shard_map/ppermute | solution.py:297
  28.2 6.5 %collective-permute-start.17 = (bf16[2,48,384]{2,1,0:T(8,128)(2,1)S(1)}, bf16[2,48,384]{2,1,0:T(8,128)(2,1)S(1)}, u32[]{:S(2)}, u32[]{:S(2)}) collective-permute-start(bf16[2,48,384]{2,1,0:T(8,128)(2,1)S(1)} %get-tuple-element.52), channel_id=1, source_target_pairs={{0,28},{4,24},{8,20},{12,16},{16,12},{20,8},{24,4},{28,0},{1,29},{... | collective-permute-start | bytes 221192 | tf_op jit(solution)/shard_map/ppermute | solution.py:297
  28.7 11.8 %collective-permute-start.8 = (bf16[384,384]{1,0:T(8,128)(2,1)S(1)}, bf16[384,384]{1,0:T(8,128)(2,1)S(1)}, u32[]{:S(2)}, u32[]{:S(2)}) collective-permute-start(bf16[384,384]{1,0:T(8,128)(2,1)S(1)} %bitcast.3), channel_id=1, source_target_pairs={{1,2},{2,1},{5,6},{6,5},{9,10},{10,9},{13,14},{14,13},{17,18},{18,... | collective-permute-start | bytes 884744 | tf_op jit(solution)/shard_map/ppermute | solution.py:304
  32.2 9.9 %collective-permute-start.12 = (bf16[2,192,384]{2,1,0:T(8,128)(2,1)S(1)}, bf16[2,192,384]{2,1,0:T(8,128)(2,1)S(1)}, u32[]{:S(2)}, u32[]{:S(2)}) collective-permute-start(bf16[2,192,384]{2,1,0:T(8,128)(2,1)S(1)} %shard_map.50.refs_0_), channel_id=1, source_target_pairs={{0,1},{1,0},{2,3},{3,2},{4,5},{5,4},{6,7},{7,6},{8,9},{9,8},{10,11... | collective-permute-start | bytes 884744 | tf_op jit(solution)/shard_map/ppermute | solution.py:304
  32.3 14.5 %collective-permute-start.13 = (bf16[2,192,384]{2,1,0:T(8,128)(2,1)S(1)}, bf16[2,192,384]{2,1,0:T(8,128)(2,1)S(1)}, u32[]{:S(2)}, u32[]{:S(2)}) collective-permute-start(bf16[2,192,384]{2,1,0:T(8,128)(2,1)S(1)} %shard_map.50.refs_0_), channel_id=1, source_target_pairs={{1,2},{2,1},{5,6},{6,5},{9,10},{10,9},{13,14},{14,13},{17,18},{18,... | collective-permute-start | bytes 884744 | tf_op jit(solution)/shard_map/ppermute | solution.py:304
  34.8 12.6 %collective-permute-start.18 = (bf16[2,192,384]{2,1,0:T(8,128)(2,1)S(1)}, bf16[2,192,384]{2,1,0:T(8,128)(2,1)S(1)}, u32[]{:S(2)}, u32[]{:S(2)}) collective-permute-start(bf16[2,192,384]{2,1,0:T(8,128)(2,1)S(1)} %shard_map.52.refs_1_), channel_id=1, source_target_pairs={{0,1},{1,0},{2,3},{3,2},{4,5},{5,4},{6,7},{7,6},{8,9},{9,8},{10,11... | collective-permute-start | bytes 884744 | tf_op jit(solution)/shard_map/ppermute | solution.py:304
  35.1 16.7 %collective-permute-start.19 = (bf16[2,192,384]{2,1,0:T(8,128)(2,1)S(1)}, bf16[2,192,384]{2,1,0:T(8,128)(2,1)S(1)}, u32[]{:S(2)}, u32[]{:S(2)}) collective-permute-start(bf16[2,192,384]{2,1,0:T(8,128)(2,1)S(1)} %shard_map.52.refs_1_), channel_id=1, source_target_pairs={{1,2},{2,1},{5,6},{6,5},{9,10},{10,9},{13,14},{14,13},{17,18},{18,... | collective-permute-start | bytes 884744 | tf_op jit(solution)/shard_map/ppermute | solution.py:304
  53.0 5.6 %collective-permute-start.20 = (bf16[2,48,384]{2,1,0:T(8,128)(2,1)S(1)}, bf16[2,48,384]{2,1,0:T(8,128)(2,1)S(1)}, u32[]{:S(2)}, u32[]{:S(2)}) collective-permute-start(bf16[2,48,384]{2,1,0:T(8,128)(2,1)S(1)} %get-tuple-element.54), channel_id=1, source_target_pairs={{0,8},{4,12},{8,0},{12,4},{16,24},{20,28},{24,16},{28,20},{1,9},{5... | collective-permute-start | bytes 221192 | tf_op jit(solution)/shard_map/ppermute | solution.py:297
  55.0 5.9 %collective-permute-start.21 = (bf16[2,48,384]{2,1,0:T(8,128)(2,1)S(1)}, bf16[2,48,384]{2,1,0:T(8,128)(2,1)S(1)}, u32[]{:S(2)}, u32[]{:S(2)}) collective-permute-start(bf16[2,48,384]{2,1,0:T(8,128)(2,1)S(1)} %get-tuple-element.55), channel_id=1, source_target_pairs={{0,16},{4,20},{8,24},{12,28},{16,0},{20,4},{24,8},{28,12},{1,17},{... | collective-permute-start | bytes 221192 | tf_op jit(solution)/shard_map/ppermute | solution.py:297
  55.2 5.8 %collective-permute-start.22 = (bf16[2,48,384]{2,1,0:T(8,128)(2,1)S(1)}, bf16[2,48,384]{2,1,0:T(8,128)(2,1)S(1)}, u32[]{:S(2)}, u32[]{:S(2)}) collective-permute-start(bf16[2,48,384]{2,1,0:T(8,128)(2,1)S(1)} %get-tuple-element.56), channel_id=1, source_target_pairs={{0,24},{4,28},{8,16},{12,20},{16,8},{20,12},{24,0},{28,4},{1,25},{... | collective-permute-start | bytes 221192 | tf_op jit(solution)/shard_map/ppermute | solution.py:297
  56.5 4.9 %collective-permute-start.23 = (bf16[2,48,384]{2,1,0:T(8,128)(2,1)S(1)}, bf16[2,48,384]{2,1,0:T(8,128)(2,1)S(1)}, u32[]{:S(2)}, u32[]{:S(2)}) collective-permute-start(bf16[2,48,384]{2,1,0:T(8,128)(2,1)S(1)} %get-tuple-element.57), channel_id=1, source_target_pairs={{0,4},{4,0},{8,12},{12,8},{16,20},{20,16},{24,28},{28,24},{1,5},{5... | collective-permute-start | bytes 221192 | tf_op jit(solution)/shard_map/ppermute | solution.py:297
  56.6 4.9 %collective-permute-start.24 = (bf16[2,48,384]{2,1,0:T(8,128)(2,1)S(1)}, bf16[2,48,384]{2,1,0:T(8,128)(2,1)S(1)}, u32[]{:S(2)}, u32[]{:S(2)}) collective-permute-start(bf16[2,48,384]{2,1,0:T(8,128)(2,1)S(1)} %get-tuple-element.58), channel_id=1, source_target_pairs={{0,12},{4,8},{8,4},{12,0},{16,28},{20,24},{24,20},{28,16},{1,13},{... | collective-permute-start | bytes 221192 | tf_op jit(solution)/shard_map/ppermute | solution.py:297
  58.6 4.4 %collective-permute-start.25 = (bf16[2,48,384]{2,1,0:T(8,128)(2,1)S(1)}, bf16[2,48,384]{2,1,0:T(8,128)(2,1)S(1)}, u32[]{:S(2)}, u32[]{:S(2)}) collective-permute-start(bf16[2,48,384]{2,1,0:T(8,128)(2,1)S(1)} %get-tuple-element.59), channel_id=1, source_target_pairs={{0,20},{4,16},{8,28},{12,24},{16,4},{20,0},{24,12},{28,8},{1,21},{... | collective-permute-start | bytes 221192 | tf_op jit(solution)/shard_map/ppermute | solution.py:297
  60.9 4.7 %collective-permute-start.26 = (bf16[2,48,384]{2,1,0:T(8,128)(2,1)S(1)}, bf16[2,48,384]{2,1,0:T(8,128)(2,1)S(1)}, u32[]{:S(2)}, u32[]{:S(2)}) collective-permute-start(bf16[2,48,384]{2,1,0:T(8,128)(2,1)S(1)} %get-tuple-element.60), channel_id=1, source_target_pairs={{0,28},{4,24},{8,20},{12,16},{16,12},{20,8},{24,4},{28,0},{1,29},{... | collective-permute-start | bytes 221192 | tf_op jit(solution)/shard_map/ppermute | solution.py:297
